TPU v7x, 256 devices: a whole 4x4x8 slice. The times are simulated.
256 devices in a mesh: grp: 16 (over z, core), ep: 16 (over y, x).
Axes of the slice: x: 4, y: 4, z: 8, core: 2. Of those that a mesh axis runs over, the one named last changes fastest.
Arguments:
- queries: bfloat16 [1024, 64, 576], P(('grp', 'ep')), may hold values from -75 to 75
- cache: bfloat16 [1024, 256, 576], P(('grp', 'ep')), may hold values from -6 to 6
- lengths: int32 [1024], P(('grp', 'ep')), may hold values from 2 to 256, as said below
- live_rows: int32 [256], P(('grp', 'ep')), may hold values from 1 to 4, as said below
- tokens: bfloat16 [4096, 3584], P(('grp', 'ep')), may hold values from -6 to 6
- ids: int32 [4096, 8], P(('grp', 'ep')), may hold values from 0 to 127, all different within a row; in each aligned block of 16 rows (0 to 15, 16 to 31, ...) at most 2 rows name the same one
- gates: float32 [4096, 8], P(('grp', 'ep')), may hold values from 0.1 to 1
- w_gate: bfloat16 [256, 3584, 512], P(('grp', 'ep')), may hold values from -0.09375 to 0.09375
- w_up: bfloat16 [256, 3584, 512], P(('grp', 'ep')), may hold values from -0.09375 to 0.09375
- w_down: bfloat16 [256, 512, 3584], P(('grp', 'ep')), may hold values from -0.1875 to 0.1875
Outputs:
- context: bfloat16 [1024, 64, 512], P(('grp', 'ep'))
- mixed: bfloat16 [4096, 3584], P(('grp', 'ep'))
Inputs may be any that keep to these rules, and one draw needn't show every extreme that they name: `ids`: each row names 8 different experts; among the rows of one device no expert is named more than 2 times. `lengths`: the first request slot of every device holds 256 positions. `live_rows`: a device's live request slots are its first ones; on a quarter of the grp indices every device holds 2 or fewer, elsewhere exactly 4.
All inputs are finite; a program needn't handle non-finite values.
Results may differ from a plain program's by a relative error of at most 0.012.
Values may be sent and summed in bfloat16 or wider, within the bound.
A program may use at most 128 MiB of HBM per device.

v0:
```python
from functools import partial

import jax
import jax.numpy as jnp
from jax import lax
from jax.sharding import PartitionSpec as P

TOPK = 8
LAT = 512


score_scale = 192.0 ** (-0.5)
neg_large = -1e30


def attend(queries, cache, lengths, live_count):
    scores = (
        jnp.einsum("rhc,rlc->rhl", queries, cache, preferred_element_type=jnp.float32) * score_scale
    )
    positions = lax.broadcasted_iota(jnp.int32, scores.shape, 2)
    inside = positions < lengths[:, None, None]
    masked = jnp.where(inside, scores, neg_large)
    highest = jnp.max(masked, axis=2, keepdims=True)
    powers = jnp.where(inside, jnp.exp(masked - highest), 0.0)
    totals = jnp.sum(powers, axis=2, keepdims=True)
    weights = (powers / totals).astype(jnp.bfloat16)
    context = jnp.einsum(
        "rhl,rlc->rhc", weights, cache[:, :, :LAT], preferred_element_type=jnp.float32
    ).astype(jnp.bfloat16)
    request_slot = lax.broadcasted_iota(jnp.int32, context.shape, 0)
    return jnp.where(request_slot < live_count, context, jnp.zeros_like(context))


def expert_partial(blocks, w_gate, w_up, w_down):
    layout = blocks.shape
    flat_rows = blocks.reshape(-1, layout[-1])
    gate_part = jnp.dot(flat_rows, w_gate[0], preferred_element_type=jnp.float32)
    up_part = jnp.dot(flat_rows, w_up[0], preferred_element_type=jnp.float32)
    hidden = (jax.nn.silu(gate_part) * up_part).astype(jnp.bfloat16)
    partials = jnp.dot(hidden, w_down[0], preferred_element_type=jnp.float32)
    return partials.reshape(layout[:-1] + (w_down.shape[2],))


def per_device(queries, cache, lengths, live_rows, tokens, ids, gates, w_gate, w_up, w_down):
    context = attend(queries, cache, lengths, live_rows[0])
    group_count = lax.axis_size("grp")
    peer_count = lax.axis_size("ep")
    pair_count = peer_count // 2
    expert_count = group_count * pair_count
    row_count = tokens.shape[0]
    feature = tokens.shape[1]
    capacity = 2 * row_count * TOPK // expert_count
    compute = partial(expert_partial, w_gate=w_gate, w_up=w_up, w_down=w_down)
    chosen_ids = ids.reshape(-1)
    onehot = (chosen_ids[:, None] == jnp.arange(expert_count, dtype=jnp.int32)[None, :]).astype(
        jnp.int32
    )
    earlier = jnp.cumsum(onehot, axis=0) - onehot
    slot_only = jnp.sum(earlier * onehot, axis=1)
    position = chosen_ids * capacity + slot_only
    source_row = jnp.arange(row_count * TOPK, dtype=jnp.int32) // TOPK
    outgoing = (
        jnp.zeros((expert_count * capacity, feature), jnp.bfloat16)
        .at[position]
        .set(tokens[source_row])
    )
    outgoing = outgoing.reshape(group_count, pair_count, capacity, feature)
    arriving = lax.all_to_all(outgoing, "grp", split_axis=0, concat_axis=0, tiled=True)
    doubled = jnp.repeat(arriving, 2, axis=1)
    partials = lax.all_to_all(
        compute(lax.all_to_all(doubled, "ep", split_axis=1, concat_axis=1, tiled=True)).astype(
            jnp.bfloat16
        ),
        "ep",
        split_axis=1,
        concat_axis=1,
        tiled=True,
    ).astype(jnp.float32)
    answered = (
        partials.reshape(group_count, pair_count, 2, capacity, feature)
        .sum(axis=2)
        .astype(jnp.bfloat16)
    )
    homebound = lax.all_to_all(answered, "grp", split_axis=0, concat_axis=0, tiled=True)
    picked = homebound.reshape(expert_count * capacity, feature)[position].reshape(
        row_count, TOPK, feature
    )
    summed = jnp.zeros((row_count, feature), jnp.float32)
    for which_pick in range(TOPK):
        summed = summed + gates[:, which_pick : which_pick + 1] * picked[:, which_pick, :].astype(
            jnp.float32
        )
    mixed = summed.astype(jnp.bfloat16)
    return (context, mixed)


def solution(mesh):
    in_specs = (
        P(("grp", "ep"), None, None),
        P(("grp", "ep"), None, None),
        P(("grp", "ep")),
        P(("grp", "ep")),
        P(("grp", "ep"), None),
        P(("grp", "ep"), None),
        P(("grp", "ep"), None),
        P(("grp", "ep"), None, None),
        P(("grp", "ep"), None, None),
        P(("grp", "ep"), None, None),
    )
    out_specs = (P(("grp", "ep"), None, None), P(("grp", "ep"), None))
    return jax.shard_map(
        per_device, mesh=mesh, in_specs=in_specs, out_specs=out_specs, check_vma=False
    )
```

profile of v0, /device:TPU:1, one launch (start us, length us, event | category | flops | bytes accessed | tf_op | source)
XLA Modules:
  0.0 272.4 jit_solution(7599573015922555550)
XLA Ops:
  0.6 0.8 copy.53
  1.4 0.7 broadcast_multiply_fusion
  2.3 0.2 reduce_window_sum.11
  2.5 0.2 select_reduce_fusion
  2.8 0.1 mul.118
  2.9 7.2 %scatter_custom_fusion = bf16[256,3584]{1,0:T(8,128)(2,1)} fusion(s32[128]{0:T(128)S(1)} %fusion.33, bf16[16,3584]{1,0:T(8,128)(2,1)} %param.14, s32[1024]{0:T(1024)S(1)} %pad_clamp_fusion.1, bf16[]{:T(256)} %constant.34.clone.1), kind=kCustom, calls=%fused_computation.21 | custom fusion | bytes 1835520 | tf_op jit(solution)/shard_map/scatter | solution.py:65
  10.1 3.9 %reshape.119 = bf16[16,8,2,3584]{3,2,1,0:T(2,128)(2,1)S(1)} reshape(bf16[256,3584]{1,0:T(8,128)(2,1)} %scatter_custom_fusion) | data formatting | bytes 3670016 | tf_op jit(solution)/shard_map/reshape | solution.py:67
  14.0 55.2 %all_to_all.20 = bf16[16,8,2,3584]{3,2,1,0:T(2,128)(2,1)S(1)} all-to-all(bf16[16,8,2,3584]{3,2,1,0:T(2,128)(2,1)S(1)} %reshape.119), channel_id=1, replica_groups=mesh['grp'=16,'ep'=16] {'grp'}, dimensions={0} | all-to-all | bytes 3670016 | tf_op jit(solution)/shard_map/all_to_all | solution.py:68
  69.2 1.3 copy.54
  70.5 4.6 %broadcast_in_dim.27 = bf16[16,8,2,2,3584]{4,3,0,2,1:T(2,128)(2,1)} broadcast(bf16[16,8,2,3584]{3,2,0,1:T(2,128)(2,1)S(1)} %copy.54), dimensions={0,1,3,4} | broadcast | bytes 5505024 | tf_op jit(solution)/shard_map/broadcast_in_dim | solution.py:69
  75.1 52.8 %all_to_all.21 = bf16[16,16,2,3584]{3,2,0,1:T(2,128)(2,1)S(1)} all-to-all(bf16[16,16,2,3584]{3,2,0,1:T(2,128)(2,1)} %bitcast.93), channel_id=1, replica_groups=mesh['grp'=16,'ep'=16] {'ep'}, dimensions={1} | all-to-all | bytes 7340032 | tf_op jit(solution)/shard_map/all_to_all | solution.py:71
  127.9 5.3 %copy.55 = bf16[16,16,2,3584]{3,2,1,0:T(2,128)(2,1)} copy(bf16[16,16,2,3584]{3,2,0,1:T(2,128)(2,1)S(1)} %all_to_all.21) | data formatting | bytes 7340032 | tf_op jit(solution)/shard_map/all_to_all | solution.py:71
  133.2 8.4 %reshape.121 = bf16[512,3584]{1,0:T(8,128)(2,1)} reshape(bf16[16,16,2,3584]{3,2,1,0:T(2,128)(2,1)} %copy.55) | data formatting | bytes 7340032 | tf_op jit(solution)/shard_map/reshape | solution.py:36
  141.6 5.3 %fusion.4 = f32[512,512]{1,0:T(8,128)S(1)} fusion(bf16[512,3584]{1,0:T(8,128)(2,1)} %reshape.121, bf16[1,3584,512]{2,1,0:T(8,128)(2,1)} %param.17), kind=kOutput, calls=%fused_computation.9 | convolution fusion | flops 1879048192 | bytes 8388608 | tf_op jit(solution)/shard_map/dot_general | solution.py:37
  147.0 2.1 fusion.9
  149.1 0.2 dot_general.21
  149.3 4.1 %convolution_convert_fusion = bf16[16,16,2,3584]{3,1,2,0:T(8,128)(2,1)S(1)} fusion(bf16[1,512,3584]{2,1,0:T(8,128)(2,1)} %param.19, bf16[16,16,2,512]{3,2,1,0:T(2,128)(2,1)S(1)} %dot_general.21), kind=kOutput, calls=%fused_computation.4 | convolution fusion | flops 1880883200 | bytes 7864320 | tf_op jit(solution)/shard_map/dot_general | solution.py:40
  153.5 3.8 %copy.57 = bf16[16,16,2,3584]{3,2,0,1:T(2,128)(2,1)S(1)} copy(bf16[16,16,2,3584]{3,1,2,0:T(8,128)(2,1)S(1)} %convolution_convert_fusion) | data formatting | bytes 7340032 | tf_op jit(solution)/shard_map/convert_element_type | solution.py:71
  157.2 46.8 %all_to_all.22 = bf16[16,16,2,3584]{3,2,0,1:T(2,128)(2,1)S(1)} all-to-all(bf16[16,16,2,3584]{3,2,0,1:T(2,128)(2,1)S(1)} %copy.57), channel_id=1, replica_groups=mesh['grp'=16,'ep'=16] {'ep'}, dimensions={1} | all-to-all | bytes 7340032 | tf_op jit(solution)/shard_map/all_to_all | solution.py:70
  204.1 6.0 %bitcast_reduce_fusion = bf16[16,8,2,3584]{3,2,0,1:T(2,128)(2,1)S(1)} fusion(bf16[16,16,2,3584]{3,2,0,1:T(2,128)(2,1)S(1)} %all_to_all.22), kind=kLoop, calls=%fused_computation.6 | loop fusion | flops 917504 | bytes 5505024 | tf_op jit(solution)/shard_map/reduce_sum | solution.py:81
  210.1 2.3 copy.69
  212.4 5.6 %all-to-all-start.3 = ((bf16[16,8,2,3584]{3,1,2,0:T(8,128)(2,1)}), bf16[16,8,2,3584]{3,1,2,0:T(8,128)(2,1)S(1)}, u32[]{:S(2)}, u32[]{:S(2)}) async-start(bf16[16,8,2,3584]{3,1,2,0:T(8,128)(2,1)} %copy.69), calls=%async_computation.3 | async-start | bytes 3670016 | tf_op jit(solution)/shard_map/all_to_all | solution.py:84
  218.8 0.3 fusion.13
  219.1 0.7 copy-done.3
  219.8 0.2 fusion.37
  220.1 2.3 fusion.16
  222.4 39.4 %all-to-all-done.3 = bf16[16,8,2,3584]{3,1,2,0:T(8,128)(2,1)S(1)} async-done(((bf16[16,8,2,3584]{3,1,2,0:T(8,128)(2,1)}), bf16[16,8,2,3584]{3,1,2,0:T(8,128)(2,1)S(1)}, u32[]{:S(2)}, u32[]{:S(2)}) %all-to-all-start.3) | async-done | bytes 1835040 | tf_op jit(solution)/shard_map/all_to_all | solution.py:84
  261.7 2.9 %copy.59 = bf16[16,8,2,3584]{3,2,1,0:T(2,128)(2,1)} copy(bf16[16,8,2,3584]{3,1,2,0:T(8,128)(2,1)S(1)} %all-to-all-done.3) | data formatting | bytes 3670016 | tf_op jit(solution)/shard_map/all_to_all | solution.py:84
  264.7 4.1 %reshape.124 = bf16[256,3584]{1,0:T(8,128)(2,1)S(1)} reshape(bf16[16,8,2,3584]{3,2,1,0:T(2,128)(2,1)} %copy.59) | data formatting | bytes 3670016 | tf_op jit(solution)/shard_map/reshape | solution.py:85
  268.7 1.1 gather_fusion
  269.8 1.6 fusion.36
  271.5 0.9 fusion.23
  (22 shorter events, 0.3 us)
Async XLA Ops:
  0.6 218.1 %copy-start = (bf16[4,64,576]{2,1,0:T(8,128)(2,1)S(1)}, bf16[4,64,576]{2,1,0:T(8,128)(2,1)}, u32[]{:S(2)}) copy-start(bf16[4,64,576]{2,1,0:T(8,128)(2,1)} %param.10) | copy-start | bytes 884740
  141.6 5.4 %copy-start.1 = (bf16[512,3584]{1,0:T(8,128)(2,1)S(1)}, bf16[512,3584]{1,0:T(8,128)(2,1)}, u32[]{:S(2)}) copy-start(bf16[512,3584]{1,0:T(8,128)(2,1)} %reshape.121) | copy-start | bytes 11010052
  141.6 5.4 %copy-start.6 = (bf16[1,3584,512]{2,1,0:T(8,128)(2,1)S(1)}, bf16[1,3584,512]{2,1,0:T(8,128)(2,1)}, u32[]{:S(2)}) copy-start(bf16[1,3584,512]{2,1,0:T(8,128)(2,1)} %param.18) | copy-start | bytes 11010052
  210.1 8.6 %copy-start.2 = (bf16[4,256,576]{1,2,0:T(8,128)(2,1)S(1)}, bf16[4,256,576]{1,2,0:T(8,128)(2,1)}, u32[]{:S(2)}) copy-start(bf16[4,256,576]{1,2,0:T(8,128)(2,1)} %param.11) | copy-start | bytes 3538948
  210.1 8.6 %copy-start.5 = (s32[4]{0:T(128)S(1)}, s32[4]{0:T(128)}, u32[]{:S(2)}) copy-start(s32[4]{0:T(128)} %param.12) | copy-start | bytes 52
  212.4 7.7 %copy-start.4 = (f32[16,8]{0,1:T(8,128)S(1)}, f32[16,8]{0,1:T(8,128)}, u32[]{:S(2)}) copy-start(f32[16,8]{0,1:T(8,128)} %param.16) | copy-start | bytes 1540
  212.4 49.4 %all-to-all-start.3 = ((bf16[16,8,2,3584]{3,1,2,0:T(8,128)(2,1)}), bf16[16,8,2,3584]{3,1,2,0:T(8,128)(2,1)S(1)}, u32[]{:S(2)}, u32[]{:S(2)}) async-start(bf16[16,8,2,3584]{3,1,2,0:T(8,128)(2,1)} %copy.69), calls=%async_computation.3 | async-start | bytes 3670016 | tf_op jit(solution)/shard_map/all_to_all | solution.py:84
  219.1 0.7 copy-start.3
where the time goes:
time: 273 us; the launch traced here: 272 us
  blocking collectives  155 us (57%)
  local copies, waits for them, and re-layouts  48.5 us (18%)
  waiting for transfers between devices  39.4 us (14%)
  matrix products  14.2 us (5%)
  other arithmetic  8.3 us (3%)
  starting transfers between devices  5.65 us (2%)
    all_to_all x1, blocking collectives, per_device(): lax.all_to_all(outgoing, 'grp', split_axis=0, concat_axis=0, tiled=True)  55.2 us
    all_to_all x1, blocking collectives, per_device(): lax.all_to_all(doubled, 'ep', split_axis=1, concat_axis=1, tiled=True)  52.8 us
    all_to_all x1, blocking collectives, per_device(): lax.all_to_all(compute(lax.all_to_all(doubled, 'ep', split_axis=1, concat...  46.8 us
    all_to_all x1, waiting for transfers between devices, per_device(): lax.all_to_all(answered, 'grp', split_axis=0, concat_axis=0, tiled=True)  39.4 us
    reshape x1, local copies, waits for them, and re-layouts, expert_partial(): flat_rows = blocks.reshape(-1, layout[-1])  8.4 us
    scatter x1, local copies, waits for them, and re-layouts, per_device(): outgoing = jnp.zeros((expert_count * capacity, feature), jnp.bfloat16).at...  7.25 us
    reduce_sum x1, other arithmetic, per_device(): answered = partials.reshape(group_count, pair_count, 2, capacity, feature...  6.02 us
    all_to_all x1, starting transfers between devices, per_device(): lax.all_to_all(answered, 'grp', split_axis=0, concat_axis=0, tiled=True)  5.65 us
  transfers between devices with their start and end apart: 1, of which 1 were waited for; matrix products, arithmetic and copies ran while one was open for 1% of the time, Pallas kernels for 0%

commit v1 on v0

v1 whole, which is shorter than its diff:
```python
import jax
import jax.numpy as jnp
from jax import lax
from jax.sharding import PartitionSpec as P

TOPK = 8
LAT = 512
CAP = 2


score_scale = 192.0 ** (-0.5)
neg_large = -1e30


def attend(queries, cache, lengths, live_count):
    scores = (
        jnp.einsum("rhc,rlc->rhl", queries, cache, preferred_element_type=jnp.float32) * score_scale
    )
    positions = lax.broadcasted_iota(jnp.int32, scores.shape, 2)
    inside = positions < lengths[:, None, None]
    masked = jnp.where(inside, scores, neg_large)
    highest = jnp.max(masked, axis=2, keepdims=True)
    powers = jnp.where(inside, jnp.exp(masked - highest), 0.0)
    totals = jnp.sum(powers, axis=2, keepdims=True)
    weights = (powers / totals).astype(jnp.bfloat16)
    context = jnp.einsum(
        "rhl,rlc->rhc", weights, cache[:, :, :LAT], preferred_element_type=jnp.float32
    ).astype(jnp.bfloat16)
    request_slot = lax.broadcasted_iota(jnp.int32, context.shape, 0)
    return jnp.where(request_slot < live_count, context, jnp.zeros_like(context))


def expert_partial(flat_rows, w_gate, w_up, w_down):
    gate_part = jnp.dot(flat_rows, w_gate[0], preferred_element_type=jnp.float32)
    up_part = jnp.dot(flat_rows, w_up[0], preferred_element_type=jnp.float32)
    hidden = (jax.nn.silu(gate_part) * up_part).astype(jnp.bfloat16)
    return jnp.dot(hidden, w_down[0], preferred_element_type=jnp.float32)


def per_device(queries, cache, lengths, live_rows, tokens, ids, gates, w_gate, w_up, w_down):
    context = attend(queries, cache, lengths, live_rows[0])
    group_count = lax.axis_size("grp")
    peer_count = lax.axis_size("ep")
    pair_count = peer_count // 2
    row_count = tokens.shape[0]
    feature = tokens.shape[1]
    expert_slots = group_count * CAP
    slot_count = pair_count * expert_slots
    column_rows = group_count * row_count

    all_tokens = lax.all_gather(tokens, "grp", axis=0, tiled=True)
    all_ids = lax.all_gather(ids, "grp", axis=0, tiled=True)
    all_gates = lax.all_gather(gates, "grp", axis=0, tiled=True)

    my_group = lax.axis_index("grp")
    local = all_ids - pair_count * my_group
    experts = jnp.arange(pair_count, dtype=jnp.int32)
    pick_hot = (local[:, :, None] == experts[None, None, :]).astype(jnp.int32)
    token_hot = jnp.sum(pick_hot, axis=1)
    gate_of = jnp.sum(all_gates[:, :, None] * pick_hot.astype(jnp.float32), axis=1)
    blocks = token_hot.reshape(group_count, row_count, pair_count)
    earlier = (jnp.cumsum(blocks, axis=1) - blocks).reshape(column_rows, pair_count)
    source = jnp.arange(column_rows, dtype=jnp.int32)[:, None] // row_count
    slot_id = experts[None, :] * expert_slots + source * CAP + earlier
    slot_id = jnp.where(token_hot > 0, slot_id, slot_count)
    slots = jnp.arange(slot_count, dtype=jnp.int32)
    match = slot_id[:, :, None] == slots[None, None, :]
    dispatch = jnp.any(match, axis=1).T.astype(jnp.bfloat16)
    combine = jnp.sum(jnp.where(match, gate_of[:, :, None], 0.0), axis=1)

    outgoing = jnp.dot(dispatch, all_tokens, preferred_element_type=jnp.float32).astype(
        jnp.bfloat16
    )
    doubled = jnp.repeat(outgoing.reshape(pair_count, expert_slots, feature), 2, axis=0)
    arriving = lax.all_to_all(doubled, "ep", split_axis=0, concat_axis=0, tiled=True)
    partials = expert_partial(
        arriving.reshape(peer_count * expert_slots, feature), w_gate, w_up, w_down
    ).astype(jnp.bfloat16)
    returned = lax.all_to_all(
        partials.reshape(peer_count, expert_slots, feature),
        "ep",
        split_axis=0,
        concat_axis=0,
        tiled=True,
    )
    expert_out = (
        returned.reshape(pair_count, 2, expert_slots, feature)
        .astype(jnp.float32)
        .sum(axis=1)
        .astype(jnp.bfloat16)
        .reshape(slot_count, feature)
    )
    column_mixed = jnp.dot(
        combine,
        expert_out.astype(jnp.float32),
        precision=lax.Precision.HIGHEST,
        preferred_element_type=jnp.float32,
    )
    mixed = lax.psum_scatter(column_mixed, "grp", scatter_dimension=0, tiled=True)
    return (context, mixed.astype(jnp.bfloat16))


def solution(mesh):
    in_specs = (
        P(("grp", "ep"), None, None),
        P(("grp", "ep"), None, None),
        P(("grp", "ep")),
        P(("grp", "ep")),
        P(("grp", "ep"), None),
        P(("grp", "ep"), None),
        P(("grp", "ep"), None),
        P(("grp", "ep"), None, None),
        P(("grp", "ep"), None, None),
        P(("grp", "ep"), None, None),
    )
    out_specs = (P(("grp", "ep"), None, None), P(("grp", "ep"), None))
    return jax.shard_map(
        per_device, mesh=mesh, in_specs=in_specs, out_specs=out_specs, check_vma=False
    )
```

time: 273 us -> 252 us (0.923)
  waiting for transfers between devices: 39.4 us -> 110 us
  blocking collectives: 155 us -> 89.9 us
  local copies, waits for them, and re-layouts: 48.5 us -> 3.1 us
  between operations: 1.51 us -> 14.9 us
  matrix products: 14.2 us -> 19.4 us
    all_to_all x3 -> x1, blocking collectives: 155 us -> 51.1 us  [per_device(): lax.all_to_all(doubled, 'ep', split_axis=0, concat_axis=0, tiled=True)]
    reduce_scatter x0 -> x1, waiting for transfers between devices: none -> 53.8 us  [per_device(): lax.psum_scatter(column_mixed, 'grp', scatter_dimension=0, tiled=True)]
    all_gather x0 -> x2, blocking collectives: none -> 38.8 us  [the longest x1 21.7 us: per_device(): all_ids = lax.all_gather(ids, 'grp', axis=0, tiled=True)]
    all_gather x0 -> x1, waiting for transfers between devices: none -> 21.8 us  [per_device(): all_tokens = lax.all_gather(tokens, 'grp', axis=0, tiled=True)]
    reshape x3 -> x2, local copies, waits for them, and re-layouts: 16.3 us -> 0.2 us  [per_device(): blocks = token_hot.reshape(group_count, row_count, pair_count)]
    all_to_all x3 -> x0, local copies, waits for them, and re-layouts: 9.5 us -> none  [the longest x1 5.33 us: per_device(): lax.all_to_all(doubled, 'ep', split_axis=1, concat_axis=1, tiled=True)]
    dot_general x2 -> x3, matrix products: 6.24 us -> 15.7 us  [the longest x1 10.1 us: expert_partial(): return jnp.dot(hidden, w_down[0], preferred_element_type=jnp.float32)]
    scatter x1 -> x0, local copies, waits for them, and re-layouts: 7.25 us -> none  [per_device(): outgoing = jnp.zeros((expert_count * capacity, feature), jnp.bfloat16).at...]
  transfers between devices with their start and end apart: 1 -> 3, of which waited for: 1 -> 3; matrix products, arithmetic and copies ran while one was open for 1% -> 2% of each run, Pallas kernels for 0% -> 0%
where the time goes in v1:
time: 252 us; the launch traced here: 250 us
  waiting for transfers between devices  110 us (44%)
  blocking collectives  89.9 us (36%)
  matrix products  19.4 us (8%)
  between operations  14.9 us (6%)
  other arithmetic  7.63 us (3%)
  starting transfers between devices  4.72 us (2%)
  local copies, waits for them, and re-layouts  3.1 us (1%)
    reduce_scatter x1, waiting for transfers between devices, per_device(): lax.psum_scatter(column_mixed, 'grp', scatter_dimension=0, tiled=True)  53.8 us
    all_to_all x1, blocking collectives, per_device(): lax.all_to_all(doubled, 'ep', split_axis=0, concat_axis=0, tiled=True)  51.1 us
    all_to_all x1, waiting for transfers between devices, per_device(): lax.all_to_all(partials.reshape(peer_count, expert_slots, feature), 'ep',...  33.7 us
    all_gather x1, waiting for transfers between devices, per_device(): all_tokens = lax.all_gather(tokens, 'grp', axis=0, tiled=True)  21.8 us
    all_gather x1, blocking collectives, per_device(): all_ids = lax.all_gather(ids, 'grp', axis=0, tiled=True)  21.7 us
    all_gather x1, blocking collectives, per_device(): all_gates = lax.all_gather(gates, 'grp', axis=0, tiled=True)  17 us
    dot_general x1, matrix products, expert_partial(): return jnp.dot(hidden, w_down[0], preferred_element_type=jnp.float32)  10.1 us
  transfers between devices with their start and end apart: 3, of which 3 were waited for; matrix products, arithmetic and copies ran while one was open for 2% of the time, Pallas kernels for 0%

profile of v1, /device:TPU:1, one launch (start us, length us, event | category | flops | bytes accessed | tf_op | source)
XLA Modules:
  0.0 249.6 jit_solution(4051258885842507781)
XLA Ops:
  7.2 0.7 all-gather.4.cloned.1.call-update
  7.9 21.7 %all-gather = s32[16,16,8]{1,2,0:T(8,128)S(1)} all-gather(s32[1,16,8]{1,2,0:T(8,128)} %bitcast.51), channel_id=1, replica_groups=mesh['grp'=16,'ep'=16] {'grp'}, dimensions={0}, use_global_device_ids=true | all-gather | bytes 8704 | tf_op jit(solution)/shard_map/all_gather | solution.py:52
  29.7 0.1 reshape.126
  29.8 0.1 reshape.114
  29.9 0.1 copy.31
  30.0 0.7 fusion.30
  30.7 0.1 copy.32
  30.8 0.1 reduce_window_sum.14
  30.9 0.1 add_select_fusion
  31.0 0.1 copy.33
  31.1 0.7 fusion.6
  31.9 21.8 %all-gather.4.cloned.1.call-done = bf16[256,3584]{1,0:T(8,128)(2,1)} async-done(((bf16[16,3584]{1,0:T(8,128)(2,1)}), bf16[256,3584]{1,0:T(8,128)(2,1)}) %all-gather.4.cloned.1.call-update) | async-done | bytes 1835024 | tf_op jit(solution)/shard_map/all_gather | solution.py:51
  53.6 2.2 convolution_convert_fusion.1
  55.8 0.4 broadcast_in_dim.46
  56.2 51.1 %all_to_all.10 = bf16[16,32,3584]{2,1,0:T(8,128)(2,1)S(1)} all-to-all(bf16[16,32,3584]{2,1,0:T(8,128)(2,1)S(1)} %bitcast.45), channel_id=1, replica_groups=mesh['grp'=16,'ep'=16] {'ep'}, dimensions={0} | all-to-all | bytes 7340032 | tf_op jit(solution)/shard_map/all_to_all | solution.py:75
  107.4 1.8 copy-done.1
  109.2 2.0 fusion.4
  111.3 10.1 %convolution_convert_fusion = bf16[512,3584]{1,0:T(8,128)(2,1)} fusion(bf16[1,512,3584]{2,1,0:T(8,128)(2,1)} %param.19, bf16[512,3584]{1,0:T(8,128)(2,1)} %bitcast.50, bf16[1,3584,512]{2,1,0:T(8,128)(2,1)} %param.18, f32[512,512]{1,0:T(8,128)S(1)} %fusion.4), kind=kOutput, calls=%fused_computation.1 | convolution fusion | flops 3761504256 | bytes 15728640 | tf_op jit(solution)/shard_map/dot_general | solution.py:37
  121.3 4.6 %all-to-all-start.1 = ((bf16[16,32,3584]{2,1,0:T(8,128)(2,1)}), bf16[16,32,3584]{2,1,0:T(8,128)(2,1)}, u32[]{:S(2)}, u32[]{:S(2)}) async-start(bf16[16,32,3584]{2,1,0:T(8,128)(2,1)} %bitcast.48), calls=%async_computation.1 | async-start | bytes 7340032 | tf_op jit(solution)/shard_map/all_to_all | solution.py:79
  126.0 0.0 reduce-scatter.2.cloned.1.call-start
  126.0 17.0 %all-gather.1 = f32[16,16,8]{1,2,0:T(8,128)S(1)} all-gather(f32[1,16,8]{1,2,0:T(8,128)S(1)} %bitcast.52), channel_id=1, replica_groups=mesh['grp'=16,'ep'=16] {'grp'}, dimensions={0}, use_global_device_ids=true | all-gather | bytes 8704 | tf_op jit(solution)/shard_map/all_gather | solution.py:53
  143.1 0.1 reshape.124
  143.2 0.1 copy.35
  143.3 1.5 select_reduce_fusion
  144.8 33.7 %all-to-all-done.1 = bf16[16,32,3584]{2,1,0:T(8,128)(2,1)} async-done(((bf16[16,32,3584]{2,1,0:T(8,128)(2,1)}), bf16[16,32,3584]{2,1,0:T(8,128)(2,1)}, u32[]{:S(2)}, u32[]{:S(2)}) %all-to-all-start.1) | async-done | bytes 3670048 | tf_op jit(solution)/shard_map/all_to_all | solution.py:79
  178.5 2.8 %bitcast_reduce_fusion = bf16[8,32,3584]{2,1,0:T(8,128)(2,1)S(1)} fusion(bf16[16,32,3584]{2,1,0:T(8,128)(2,1)} %all-to-all-done.1), kind=kLoop, calls=%fused_computation.3 | loop fusion | flops 917504 | bytes 5505024 | tf_op jit(solution)/shard_map/reduce_sum | solution.py:89
  181.3 3.5 %fusion.31 = f32[256,3584]{1,0:T(8,128)} fusion(f32[256,256]{1,0:T(8,128)S(1)} %select_reduce_fusion, bf16[256,3584]{1,0:T(8,128)(2,1)S(1)} %bitcast.47), kind=kOutput, calls=%fused_computation.45 | convolution fusion | flops 2818572288 | bytes 5767168 | tf_op jit(solution)/shard_map/dot_general | solution.py:93
  185.5 0.3 fusion.14
  185.9 0.2 fusion.29
  186.1 1.2 fusion.17
  187.4 53.8 %reduce-scatter.2.cloned.1.call-done = f32[16,3584]{1,0:T(8,128)} async-done(((f32[256,3584]{1,0:T(8,128)}), f32[16,3584]{1,0:T(8,128)}) %reduce-scatter.2.cloned.1.call-update) | async-done | bytes 229392 | tf_op jit(solution)/shard_map/reduce_scatter | solution.py:99
  241.1 1.6 convert_element_type.35
  (21 shorter events, 0.2 us)
Async XLA Ops:
  7.2 178.3 %copy-start = (bf16[4,64,576]{2,1,0:T(8,128)(2,1)S(1)}, bf16[4,64,576]{2,1,0:T(8,128)(2,1)}, u32[]{:S(2)}) copy-start(bf16[4,64,576]{2,1,0:T(8,128)(2,1)} %param.10) | copy-start | bytes 884740
  7.2 46.5 %all-gather.4.cloned.1.call-start = ((), (), s32[]{:S(2)}) async-start(), calls=%async_computation.3 | async-start | bytes 1949696 | tf_op jit(solution)/shard_map/all_gather | solution.py:51
  56.2 53.0 %copy-start.5 = (bf16[1,3584,512]{2,1,0:T(8,128)(2,1)S(1)}, bf16[1,3584,512]{2,1,0:T(8,128)(2,1)}, u32[]{:S(2)}) copy-start(bf16[1,3584,512]{2,1,0:T(8,128)(2,1)} %param.17) | copy-start | bytes 11010052
  107.4 1.8 copy-start.1
  121.3 4.7 %copy-start.3 = (f32[16,8]{0,1:T(8,128)S(1)}, f32[16,8]{0,1:T(8,128)}, u32[]{:S(2)}) copy-start(f32[16,8]{0,1:T(8,128)} %param.16) | copy-start | bytes 1540
  121.3 57.2 %all-to-all-start.1 = ((bf16[16,32,3584]{2,1,0:T(8,128)(2,1)}), bf16[16,32,3584]{2,1,0:T(8,128)(2,1)}, u32[]{:S(2)}, u32[]{:S(2)}) async-start(bf16[16,32,3584]{2,1,0:T(8,128)(2,1)} %bitcast.48), calls=%async_computation.1 | async-start | bytes 7340032 | tf_op jit(solution)/shard_map/all_to_all | solution.py:79
  126.0 115.2 %reduce-scatter.2.cloned.1.call-start = ((), (), s32[]{:S(2)}) async-start(), calls=%async_computation.4 | async-start | bytes 3899392 | tf_op jit(solution)/shard_map/reduce_scatter | solution.py:99
  181.3 4.2 %copy-start.2 = (bf16[4,256,576]{1,2,0:T(8,128)(2,1)S(1)}, bf16[4,256,576]{1,2,0:T(8,128)(2,1)}, u32[]{:S(2)}) copy-start(bf16[4,256,576]{1,2,0:T(8,128)(2,1)} %param.11) | copy-start | bytes 3538948
  181.3 4.2 %copy-start.4 = (s32[4]{0:T(128)S(1)}, s32[4]{0:T(128)}, u32[]{:S(2)}) copy-start(s32[4]{0:T(128)} %param.12) | copy-start | bytes 52
Sparse Core Ops, SparseCore 0:
  9.8 43.7 all-gather.3
  184.9 56.1 reduce-scatter.1

commit v2 on v1

--- a/solution.py
+++ b/solution.py
@@ -48,9 +48,18 @@
     slot_count = pair_count * expert_slots
     column_rows = group_count * row_count
 
-    all_tokens = lax.all_gather(tokens, "grp", axis=0, tiled=True)
-    all_ids = lax.all_gather(ids, "grp", axis=0, tiled=True)
-    all_gates = lax.all_gather(gates, "grp", axis=0, tiled=True)
+    gate_high = gates.astype(jnp.bfloat16)
+    gate_low = (gates - gate_high.astype(jnp.float32)).astype(jnp.bfloat16)
+    meta = jnp.concatenate([ids.astype(jnp.bfloat16), gate_high, gate_low], axis=1)
+    meta = jnp.pad(meta, ((0, 0), (0, 128 - meta.shape[1])))
+    packed = lax.all_gather(
+        jnp.concatenate([tokens, meta], axis=1), "grp", axis=0, tiled=True
+    )
+    all_tokens = packed[:, :feature]
+    all_ids = packed[:, feature : feature + TOPK].astype(jnp.int32)
+    all_gates = packed[:, feature + TOPK : feature + 2 * TOPK].astype(jnp.float32) + packed[
+        :, feature + 2 * TOPK : feature + 3 * TOPK
+    ].astype(jnp.float32)
 
     my_group = lax.axis_index("grp")
     local = all_ids - pair_count * my_group
@@ -96,8 +105,10 @@
         precision=lax.Precision.HIGHEST,
         preferred_element_type=jnp.float32,
     )
-    mixed = lax.psum_scatter(column_mixed, "grp", scatter_dimension=0, tiled=True)
-    return (context, mixed.astype(jnp.bfloat16))
+    mixed = lax.psum_scatter(
+        column_mixed.astype(jnp.bfloat16), "grp", scatter_dimension=0, tiled=True
+    )
+    return (context, mixed)
 
 
 def solution(mesh):

time: 252 us -> 251 us (level)
  blocking collectives: 89.9 us -> 51.1 us
  waiting for transfers between devices: 110 us -> 145 us
  local copies, waits for them, and re-layouts: 3.1 us -> 5.71 us
    all_gather x2 -> x0, blocking collectives: 38.8 us -> none  [the longest x1 21.7 us: per_device(): all_ids = lax.all_gather(ids, 'grp', axis=0, tiled=True)]
    all_gather x1, waiting for transfers between devices: 21.8 us -> 43.9 us  [per_device(): lax.all_gather(jnp.concatenate([tokens, meta], axis=1), 'grp', axis=0, ti...]
    all_to_all x1, waiting for transfers between devices: 33.7 us -> 50.7 us  [per_device(): lax.all_to_all(partials.reshape(peer_count, expert_slots, feature), 'ep',...]
    reduce_scatter x1, waiting for transfers between devices: 53.8 us -> 50.7 us  [per_device(): lax.psum_scatter(column_mixed.astype(jnp.bfloat16), 'grp', scatter_dimens...]
  transfers between devices with their start and end apart: 3 -> 3, of which waited for: 3 -> 3; matrix products, arithmetic and copies ran while one was open for 2% -> 1% of each run, Pallas kernels for 0% -> 0%
where the time goes in v2:
time: 251 us; the launch traced here: 248 us
  waiting for transfers between devices  145 us (58%)
  blocking collectives  51.1 us (20%)
  matrix products  18.8 us (7%)
  between operations  14.9 us (6%)
  other arithmetic  7.73 us (3%)
  local copies, waits for them, and re-layouts  5.71 us (2%)
  starting transfers between devices  4.59 us (2%)
    all_to_all x1, blocking collectives, per_device(): lax.all_to_all(doubled, 'ep', split_axis=0, concat_axis=0, tiled=True)  51.1 us
    all_to_all x1, waiting for transfers between devices, per_device(): lax.all_to_all(partials.reshape(peer_count, expert_slots, feature), 'ep',...  50.7 us
    reduce_scatter x1, waiting for transfers between devices, per_device(): lax.psum_scatter(column_mixed.astype(jnp.bfloat16), 'grp', scatter_dimens...  50.7 us
    all_gather x1, waiting for transfers between devices, per_device(): lax.all_gather(jnp.concatenate([tokens, meta], axis=1), 'grp', axis=0, ti...  43.9 us
    dot_general x1, matrix products, expert_partial(): return jnp.dot(hidden, w_down[0], preferred_element_type=jnp.float32)  10.1 us
  transfers between devices with their start and end apart: 3, of which 3 were waited for; matrix products, arithmetic and copies ran while one was open for 1% of the time, Pallas kernels for 0%

profile of v2, /device:TPU:1, one launch (start us, length us, event | category | flops | bytes accessed | tf_op | source)
XLA Modules:
  0.0 248.3 jit_solution(11067031756763123263)
XLA Ops:
  7.2 0.8 copy.35
  8.0 0.8 copy.34
  8.8 0.1 fusion.30
  8.9 1.6 pad_maximum_fusion
  10.5 43.9 %all-gather.2.cloned.1.call-done = bf16[256,3712]{1,0:T(8,128)(2,1)} async-done(((bf16[16,3712]{1,0:T(8,128)(2,1)}), bf16[256,3712]{1,0:T(8,128)(2,1)}) %all-gather.2.cloned.1.call-update) | async-done | bytes 1900560 | tf_op jit(solution)/shard_map/all_gather | solution.py:55
  54.4 1.1 fusion.35
  55.5 0.1 copy.45
  55.6 0.1 reshape.114
  55.7 0.1 copy.38
  55.8 0.7 fusion.37
  56.5 0.1 copy.39
  56.6 0.1 reduce_window_sum.14
  56.7 0.1 add_select_fusion
  56.8 0.1 copy.40
  56.9 0.7 fusion.6
  57.7 2.2 convolution_convert_fusion.2
  59.9 0.4 broadcast_in_dim.46
  60.3 51.1 %all_to_all.10 = bf16[16,32,3584]{2,1,0:T(8,128)(2,1)S(1)} all-to-all(bf16[16,32,3584]{2,1,0:T(8,128)(2,1)S(1)} %bitcast.38), channel_id=1, replica_groups=mesh['grp'=16,'ep'=16] {'ep'}, dimensions={0} | all-to-all | bytes 7340032 | tf_op jit(solution)/shard_map/all_to_all | solution.py:84
  111.4 1.8 copy-done.1
  113.2 2.1 fusion.4
  115.3 10.1 %convolution_convert_fusion = bf16[512,3584]{1,0:T(8,128)(2,1)} fusion(bf16[1,512,3584]{2,1,0:T(8,128)(2,1)} %param.19, bf16[512,3584]{1,0:T(8,128)(2,1)} %bitcast.43, bf16[1,3584,512]{2,1,0:T(8,128)(2,1)} %param.18, f32[512,512]{1,0:T(8,128)S(1)} %fusion.4), kind=kOutput, calls=%fused_computation.1 | convolution fusion | flops 3761504256 | bytes 15728640 | tf_op jit(solution)/shard_map/dot_general | solution.py:37
  125.3 4.5 %all-to-all-start.1 = ((bf16[16,32,3584]{2,1,0:T(8,128)(2,1)}), bf16[16,32,3584]{2,1,0:T(8,128)(2,1)}, u32[]{:S(2)}, u32[]{:S(2)}) async-start(bf16[16,32,3584]{2,1,0:T(8,128)(2,1)} %bitcast.41), calls=%async_computation.1 | async-start | bytes 7340032 | tf_op jit(solution)/shard_map/all_to_all | solution.py:88
  130.0 0.1 copy.47
  130.1 0.1 copy.43
  130.2 1.5 select_reduce_fusion
  131.7 50.7 %all-to-all-done.1 = bf16[16,32,3584]{2,1,0:T(8,128)(2,1)} async-done(((bf16[16,32,3584]{2,1,0:T(8,128)(2,1)}), bf16[16,32,3584]{2,1,0:T(8,128)(2,1)}, u32[]{:S(2)}, u32[]{:S(2)}) %all-to-all-start.1) | async-done | bytes 3670048 | tf_op jit(solution)/shard_map/all_to_all | solution.py:88
  182.4 2.8 %bitcast_reduce_fusion = bf16[8,32,3584]{2,1,0:T(8,128)(2,1)S(1)} fusion(bf16[16,32,3584]{2,1,0:T(8,128)(2,1)} %all-to-all-done.1), kind=kLoop, calls=%fused_computation.4 | loop fusion | flops 917504 | bytes 5505024 | tf_op jit(solution)/shard_map/reduce_sum | solution.py:98
  185.2 2.9 %convolution_convert_fusion.1 = bf16[256,3584]{1,0:T(8,128)(2,1)} fusion(f32[256,256]{1,0:T(8,128)S(1)} %select_reduce_fusion, bf16[256,3584]{1,0:T(8,128)(2,1)S(1)} %bitcast.40), kind=kOutput, calls=%fused_computation.2 | convolution fusion | flops 2819489792 | bytes 3932160 | tf_op jit(solution)/shard_map/dot_general | solution.py:102
  188.9 0.3 fusion.15
  189.2 0.2 fusion.36
  189.5 1.3 fusion.18
  190.7 50.7 %reduce-scatter.2.cloned.1.call-done = bf16[16,3584]{1,0:T(8,128)(2,1)} async-done(((bf16[256,3584]{1,0:T(8,128)(2,1)}), bf16[16,3584]{1,0:T(8,128)(2,1)}) %reduce-scatter.2.cloned.1.call-update) | async-done | bytes 114704 | tf_op jit(solution)/shard_map/reduce_scatter | solution.py:108
  (23 shorter events, 0.3 us)
Async XLA Ops:
  7.2 181.7 %copy-start = (bf16[4,64,576]{2,1,0:T(8,128)(2,1)S(1)}, bf16[4,64,576]{2,1,0:T(8,128)(2,1)}, u32[]{:S(2)}) copy-start(bf16[4,64,576]{2,1,0:T(8,128)(2,1)} %param.10) | copy-start | bytes 884740
  7.2 47.2 %all-gather.2.cloned.1.call-start = ((), (), s32[]{:S(2)}) async-start(), calls=%async_computation.3 | async-start | bytes 2019328 | tf_op jit(solution)/shard_map/all_gather | solution.py:55
  60.2 53.0 %copy-start.4 = (bf16[1,3584,512]{2,1,0:T(8,128)(2,1)S(1)}, bf16[1,3584,512]{2,1,0:T(8,128)(2,1)}, u32[]{:S(2)}) copy-start(bf16[1,3584,512]{2,1,0:T(8,128)(2,1)} %param.17) | copy-start | bytes 11010052
  111.4 1.8 copy-start.1
  125.3 57.1 %all-to-all-start.1 = ((bf16[16,32,3584]{2,1,0:T(8,128)(2,1)}), bf16[16,32,3584]{2,1,0:T(8,128)(2,1)}, u32[]{:S(2)}, u32[]{:S(2)}) async-start(bf16[16,32,3584]{2,1,0:T(8,128)(2,1)} %bitcast.41), calls=%async_computation.1 | async-start | bytes 7340032 | tf_op jit(solution)/shard_map/all_to_all | solution.py:88
  129.9 111.6 %reduce-scatter.2.cloned.1.call-start = ((), (), s32[]{:S(2)}) async-start(), calls=%async_computation.4 | async-start | bytes 1949696 | tf_op jit(solution)/shard_map/reduce_scatter | solution.py:108
  185.2 3.7 %copy-start.2 = (bf16[4,256,576]{1,2,0:T(8,128)(2,1)S(1)}, bf16[4,256,576]{1,2,0:T(8,128)(2,1)}, u32[]{:S(2)}) copy-start(bf16[4,256,576]{1,2,0:T(8,128)(2,1)} %param.11) | copy-start | bytes 3538948
  185.2 3.6 %copy-start.3 = (s32[4]{0:T(128)S(1)}, s32[4]{0:T(128)}, u32[]{:S(2)}) copy-start(s32[4]{0:T(128)} %param.12) | copy-start | bytes 52
Sparse Core Ops, SparseCore 0:
  10.6 43.8 all-gather.1
  188.3 53.0 reduce-scatter.1

commit v3 on v2

--- a/solution.py
+++ b/solution.py
@@ -1,8 +1,13 @@
+import functools
+
 import jax
 import jax.numpy as jnp
 from jax import lax
+from jax.experimental import pallas as pl
+from jax.experimental.pallas import tpu as pltpu
 from jax.sharding import PartitionSpec as P
 
+MESH = pl.DeviceIdType.MESH
 TOPK = 8
 LAT = 512
 CAP = 2
@@ -30,6 +35,89 @@
     return jnp.where(request_slot < live_count, context, jnp.zeros_like(context))
 
 
+def gather_kernel(chips, x_ref, out_ref, send_sem, recv_sem):
+    group = lax.axis_index("grp")
+    peer_col = lax.axis_index("ep")
+    z = group // 2
+    core = group % 2
+    right = lax.rem(z + 1, chips) * 2 + core
+    left = lax.rem(z + chips - 1, chips) * 2 + core
+    partner = z * 2 + (1 - core)
+
+    barrier = pltpu.get_barrier_semaphore()
+    for peer in (left, right, partner):
+        pl.semaphore_signal(barrier, inc=1, device_id=(peer, peer_col), device_id_type=MESH)
+    pl.semaphore_wait(barrier, 3)
+
+    started = []
+
+    def send(src, origin, peer):
+        copy = pltpu.make_async_remote_copy(
+            src_ref=src,
+            dst_ref=out_ref.at[origin],
+            send_sem=send_sem.at[len(started)],
+            recv_sem=recv_sem.at[origin],
+            device_id=(peer, peer_col),
+            device_id_type=MESH,
+        )
+        copy.start()
+        started.append(copy)
+
+    def arrive(origin, peer):
+        pltpu.make_async_remote_copy(
+            src_ref=out_ref.at[origin],
+            dst_ref=out_ref.at[origin],
+            send_sem=send_sem.at[0],
+            recv_sem=recv_sem.at[origin],
+            device_id=(peer, peer_col),
+            device_id_type=MESH,
+        ).wait_recv()
+
+    send(x_ref, group, right)
+    send(x_ref, group, left)
+    send(x_ref, group, partner)
+    out_ref[group] = x_ref[...]
+    forward_hops = chips // 2
+    backward_hops = (chips - 1) // 2
+    for step in range(1, forward_hops + 1):
+        origin = lax.rem(z + chips - step, chips) * 2 + core
+        arrive(origin, left)
+        if step < forward_hops:
+            send(out_ref.at[origin], origin, right)
+        send(out_ref.at[origin], origin, partner)
+        if step <= backward_hops:
+            origin = lax.rem(z + step, chips) * 2 + core
+            arrive(origin, right)
+            if step < backward_hops:
+                send(out_ref.at[origin], origin, left)
+            send(out_ref.at[origin], origin, partner)
+    for other in range(chips):
+        arrive(other * 2 + (1 - core), partner)
+    for copy in started:
+        copy.wait_send()
+
+
+def send_count(chips):
+    forward_hops = chips // 2
+    backward_hops = (chips - 1) // 2
+    return 3 + 2 * forward_hops - 1 + 2 * backward_hops - 1
+
+
+def ring_gather(block, group_count):
+    chips = group_count // 2
+    return pl.pallas_call(
+        functools.partial(gather_kernel, chips),
+        out_shape=jax.ShapeDtypeStruct((group_count,) + block.shape, block.dtype),
+        in_specs=[pl.BlockSpec(memory_space=pltpu.VMEM)],
+        out_specs=pl.BlockSpec(memory_space=pltpu.VMEM),
+        scratch_shapes=[
+            pltpu.SemaphoreType.DMA((send_count(chips),)),
+            pltpu.SemaphoreType.DMA((group_count,)),
+        ],
+        compiler_params=pltpu.CompilerParams(collective_id=0, has_side_effects=True),
+    )(block)
+
+
 def expert_partial(flat_rows, w_gate, w_up, w_down):
     gate_part = jnp.dot(flat_rows, w_gate[0], preferred_element_type=jnp.float32)
     up_part = jnp.dot(flat_rows, w_up[0], preferred_element_type=jnp.float32)
@@ -52,8 +140,8 @@
     gate_low = (gates - gate_high.astype(jnp.float32)).astype(jnp.bfloat16)
     meta = jnp.concatenate([ids.astype(jnp.bfloat16), gate_high, gate_low], axis=1)
     meta = jnp.pad(meta, ((0, 0), (0, 128 - meta.shape[1])))
-    packed = lax.all_gather(
-        jnp.concatenate([tokens, meta], axis=1), "grp", axis=0, tiled=True
+    packed = ring_gather(jnp.concatenate([tokens, meta], axis=1), group_count).reshape(
+        column_rows, feature + meta.shape[1]
     )
     all_tokens = packed[:, :feature]
     all_ids = packed[:, feature : feature + TOPK].astype(jnp.int32)

time: 251 us -> 236 us (0.940)
  waiting for transfers between devices: 145 us -> 104 us
  Pallas kernels: 0 us -> 26.1 us
    all_gather x1 -> x0, waiting for transfers between devices: 43.9 us -> none  [per_device(): lax.all_gather(jnp.concatenate([tokens, meta], axis=1), 'grp', axis=0, ti...]
    pallas_call x0 -> x1, Pallas kernels: none -> 26.1 us  [ring_gather(): pl.pallas_call(functools.partial(gather_kernel, chips), out_shape=jax.Sha...]
  transfers between devices with their start and end apart: 3 -> 2, of which waited for: 3 -> 2; matrix products, arithmetic and copies ran while one was open for 1% -> 2% of each run, Pallas kernels for 0% -> 0%
where the time goes in v3:
time: 236 us; the launch traced here: 234 us
  waiting for transfers between devices  104 us (44%)
  blocking collectives  51.7 us (22%)
  Pallas kernels  26.1 us (11%)
  matrix products  18.8 us (8%)
  between operations  14.9 us (6%)
  other arithmetic  9.15 us (4%)
  local copies, waits for them, and re-layouts  5.09 us (2%)
  starting transfers between devices  4.55 us (2%)
    reduce_scatter x1, waiting for transfers between devices, per_device(): lax.psum_scatter(column_mixed.astype(jnp.bfloat16), 'grp', scatter_dimens...  52.8 us
    all_to_all x1, blocking collectives, per_device(): lax.all_to_all(doubled, 'ep', split_axis=0, concat_axis=0, tiled=True)  51.7 us
    all_to_all x1, waiting for transfers between devices, per_device(): lax.all_to_all(partials.reshape(peer_count, expert_slots, feature), 'ep',...  50.9 us
    pallas_call x1, Pallas kernels, ring_gather(): pl.pallas_call(functools.partial(gather_kernel, chips), out_shape=jax.Sha...  26.1 us
    dot_general x1, matrix products, expert_partial(): return jnp.dot(hidden, w_down[0], preferred_element_type=jnp.float32)  10.1 us
  transfers between devices with their start and end apart: 2, of which 2 were waited for; matrix products, arithmetic and copies ran while one was open for 2% of the time, Pallas kernels for 0%

profile of v3, /device:TPU:1, one launch (start us, length us, event | category | flops | bytes accessed | tf_op | source)
XLA Modules:
  0.0 234.0 jit_solution(16964579826946847334)
XLA Ops:
  7.2 0.7 convert_element_type.54
  7.9 0.8 copy.35
  8.7 0.1 copy.37
  8.8 0.7 convert_element_type.53
  9.5 0.1 copy.36
  9.5 0.1 fusion.30
  9.6 1.6 pad_maximum_fusion.x_ref
  11.2 26.1 %shard_map.113 = bf16[16,16,3712]{2,1,0:T(8,128)(2,1)} custom-call(bf16[16,3712]{1,0:T(8,128)(2,1)} %pad_maximum_fusion.x_ref), custom_call_target="tpu_custom_call" | custom-call | tf_op jit(solution)/shard_map/pallas_call | solution.py:108
  37.3 1.1 fusion.35
  38.5 0.1 copy.39
  38.7 0.7 fusion.37
  39.4 0.1 copy.40
  39.5 0.1 reduce_window_sum.14
  39.6 0.1 copy.41
  39.8 0.7 fusion.6
  40.5 2.2 convolution_convert_fusion.2
  42.7 0.4 broadcast_in_dim.46
  43.1 51.7 %all_to_all.10 = bf16[16,32,3584]{2,1,0:T(8,128)(2,1)S(1)} all-to-all(bf16[16,32,3584]{2,1,0:T(8,128)(2,1)S(1)} %bitcast.39), channel_id=1, replica_groups=mesh['grp'=16,'ep'=16] {'ep'}, dimensions={0} | all-to-all | bytes 7340032 | tf_op jit(solution)/shard_map/all_to_all | solution.py:172
  94.8 1.8 copy-done.1
  96.7 2.0 fusion.4
  98.7 10.1 %convolution_convert_fusion = bf16[512,3584]{1,0:T(8,128)(2,1)} fusion(bf16[1,512,3584]{2,1,0:T(8,128)(2,1)} %param.19, bf16[512,3584]{1,0:T(8,128)(2,1)} %bitcast.46, bf16[1,3584,512]{2,1,0:T(8,128)(2,1)} %param.18, f32[512,512]{1,0:T(8,128)S(1)} %fusion.4), kind=kOutput, calls=%fused_computation.1 | convolution fusion | flops 3761504256 | bytes 15728640 | tf_op jit(solution)/shard_map/dot_general | solution.py:125
  108.8 4.5 %all-to-all-start.1 = ((bf16[16,32,3584]{2,1,0:T(8,128)(2,1)}), bf16[16,32,3584]{2,1,0:T(8,128)(2,1)}, u32[]{:S(2)}, u32[]{:S(2)}) async-start(bf16[16,32,3584]{2,1,0:T(8,128)(2,1)} %bitcast.44), calls=%async_computation.1 | async-start | bytes 7340032 | tf_op jit(solution)/shard_map/all_to_all | solution.py:176
  113.4 0.1 copy.48
  113.5 0.1 copy.44
  113.7 1.5 select_reduce_fusion
  115.1 50.9 %all-to-all-done.1 = bf16[16,32,3584]{2,1,0:T(8,128)(2,1)} async-done(((bf16[16,32,3584]{2,1,0:T(8,128)(2,1)}), bf16[16,32,3584]{2,1,0:T(8,128)(2,1)}, u32[]{:S(2)}, u32[]{:S(2)}) %all-to-all-start.1) | async-done | bytes 3670048 | tf_op jit(solution)/shard_map/all_to_all | solution.py:176
  166.1 2.8 %bitcast_reduce_fusion = bf16[8,32,3584]{2,1,0:T(8,128)(2,1)S(1)} fusion(bf16[16,32,3584]{2,1,0:T(8,128)(2,1)} %all-to-all-done.1), kind=kLoop, calls=%fused_computation.4 | loop fusion | flops 917504 | bytes 5505024 | tf_op jit(solution)/shard_map/reduce_sum | solution.py:186
  168.9 2.9 %convolution_convert_fusion.1 = bf16[256,3584]{1,0:T(8,128)(2,1)} fusion(f32[256,256]{1,0:T(8,128)S(1)} %select_reduce_fusion, bf16[256,3584]{1,0:T(8,128)(2,1)S(1)} %bitcast.43), kind=kOutput, calls=%fused_computation.2 | convolution fusion | flops 2819489792 | bytes 3932160 | tf_op jit(solution)/shard_map/dot_general | solution.py:190
  172.5 0.3 fusion.15
  172.9 0.2 fusion.36
  173.1 1.3 fusion.18
  174.4 52.8 %reduce-scatter.2.cloned.1.call-done = bf16[16,3584]{1,0:T(8,128)(2,1)} async-done(((bf16[256,3584]{1,0:T(8,128)(2,1)}), bf16[16,3584]{1,0:T(8,128)(2,1)}) %reduce-scatter.2.cloned.1.call-update) | async-done | bytes 114704 | tf_op jit(solution)/shard_map/reduce_scatter | solution.py:196
  (23 shorter events, 0.5 us)
Async XLA Ops:
  7.2 165.3 %copy-start = (bf16[4,64,576]{2,1,0:T(8,128)(2,1)S(1)}, bf16[4,64,576]{2,1,0:T(8,128)(2,1)}, u32[]{:S(2)}) copy-start(bf16[4,64,576]{2,1,0:T(8,128)(2,1)} %param.10) | copy-start | bytes 884740
  43.1 53.6 %copy-start.4 = (bf16[1,3584,512]{2,1,0:T(8,128)(2,1)S(1)}, bf16[1,3584,512]{2,1,0:T(8,128)(2,1)}, u32[]{:S(2)}) copy-start(bf16[1,3584,512]{2,1,0:T(8,128)(2,1)} %param.17) | copy-start | bytes 11010052
  94.8 1.8 copy-start.1
  108.8 57.3 %all-to-all-start.1 = ((bf16[16,32,3584]{2,1,0:T(8,128)(2,1)}), bf16[16,32,3584]{2,1,0:T(8,128)(2,1)}, u32[]{:S(2)}, u32[]{:S(2)}) async-start(bf16[16,32,3584]{2,1,0:T(8,128)(2,1)} %bitcast.44), calls=%async_computation.1 | async-start | bytes 7340032 | tf_op jit(solution)/shard_map/all_to_all | solution.py:176
  113.3 113.9 %reduce-scatter.2.cloned.1.call-start = ((), (), s32[]{:S(2)}) async-start(), calls=%async_computation.3 | async-start | bytes 1949696 | tf_op jit(solution)/shard_map/reduce_scatter | solution.py:196
  168.9 3.7 %copy-start.2 = (bf16[4,256,576]{1,2,0:T(8,128)(2,1)S(1)}, bf16[4,256,576]{1,2,0:T(8,128)(2,1)}, u32[]{:S(2)}) copy-start(bf16[4,256,576]{1,2,0:T(8,128)(2,1)} %param.11) | copy-start | bytes 3538948
  168.9 3.6 %copy-start.3 = (s32[4]{0:T(128)S(1)}, s32[4]{0:T(128)}, u32[]{:S(2)}) copy-start(s32[4]{0:T(128)} %param.12) | copy-start | bytes 52
Sparse Core Ops, SparseCore 0:
  172.0 55.1 reduce-scatter.1

commit v4 on v3

--- a/solution.py
+++ b/solution.py
@@ -118,6 +118,103 @@
     )(block)
 
 
+def scatter_kernel(
+    chips, parts_ref, out_ref, early, forward_in, backward_in, forward_out, backward_out,
+    send_sem, recv_sem,
+):
+    group = lax.axis_index("grp")
+    peer_col = lax.axis_index("ep")
+    z = group // 2
+    core = group % 2
+    right = lax.rem(z + 1, chips) * 2 + core
+    left = lax.rem(z + chips - 1, chips) * 2 + core
+    partner = z * 2 + (1 - core)
+    forward_hops = chips // 2
+    backward_hops = (chips - 1) // 2
+
+    barrier = pltpu.get_barrier_semaphore()
+    for peer in (left, right, partner):
+        pl.semaphore_signal(barrier, inc=1, device_id=(peer, peer_col), device_id_type=MESH)
+    pl.semaphore_wait(barrier, 3)
+
+    started = []
+
+    def copy_of(src, dst, peer, slot, number):
+        return pltpu.make_async_remote_copy(
+            src_ref=src,
+            dst_ref=dst,
+            send_sem=send_sem.at[number],
+            recv_sem=recv_sem.at[slot],
+            device_id=(peer, peer_col),
+            device_id_type=MESH,
+        )
+
+    def send(src, dst, peer, slot):
+        copy = copy_of(src, dst, peer, slot, len(started))
+        copy.start()
+        started.append(copy)
+
+    def arrive(dst, peer, slot):
+        copy_of(dst, dst, peer, slot, 0).wait_recv()
+
+    for other in range(chips):
+        send(parts_ref.at[other * 2 + (1 - core)], early.at[other], partner, other)
+    for other in range(chips):
+        arrive(early.at[other], partner, other)
+
+    def chip_part(chip):
+        return parts_ref[chip * 2 + core].astype(jnp.float32) + early[chip].astype(jnp.float32)
+
+    for step in range(forward_hops):
+        chip = lax.rem(z + forward_hops - step, chips)
+        value = chip_part(chip)
+        if step > 0:
+            arrive(forward_in.at[step - 1], left, chips + step - 1)
+            value = value + forward_in[step - 1].astype(jnp.float32)
+        forward_out[step] = value.astype(forward_out.dtype)
+        send(forward_out.at[step], forward_in.at[step], right, chips + step)
+        if step < backward_hops:
+            chip = lax.rem(z + chips - backward_hops + step, chips)
+            value = chip_part(chip)
+            if step > 0:
+                arrive(backward_in.at[step - 1], right, chips + forward_hops + step - 1)
+                value = value + backward_in[step - 1].astype(jnp.float32)
+            backward_out[step] = value.astype(backward_out.dtype)
+            send(backward_out.at[step], backward_in.at[step], left, chips + forward_hops + step)
+    arrive(forward_in.at[forward_hops - 1], left, chips + forward_hops - 1)
+    total = chip_part(z) + forward_in[forward_hops - 1].astype(jnp.float32)
+    if backward_hops > 0:
+        arrive(backward_in.at[backward_hops - 1], right, chips + forward_hops + backward_hops - 1)
+        total = total + backward_in[backward_hops - 1].astype(jnp.float32)
+    out_ref[...] = total.astype(out_ref.dtype)
+    for copy in started:
+        copy.wait_send()
+
+
+def ring_scatter(parts, group_count):
+    chips = group_count // 2
+    forward_hops = chips // 2
+    backward_hops = (chips - 1) // 2
+    block = parts.shape[1:]
+    slots = chips + forward_hops + backward_hops
+    return pl.pallas_call(
+        functools.partial(scatter_kernel, chips),
+        out_shape=jax.ShapeDtypeStruct(block, parts.dtype),
+        in_specs=[pl.BlockSpec(memory_space=pltpu.VMEM)],
+        out_specs=pl.BlockSpec(memory_space=pltpu.VMEM),
+        scratch_shapes=[
+            pltpu.VMEM((chips,) + block, parts.dtype),
+            pltpu.VMEM((forward_hops,) + block, parts.dtype),
+            pltpu.VMEM((max(backward_hops, 1),) + block, parts.dtype),
+            pltpu.VMEM((forward_hops,) + block, parts.dtype),
+            pltpu.VMEM((max(backward_hops, 1),) + block, parts.dtype),
+            pltpu.SemaphoreType.DMA((slots,)),
+            pltpu.SemaphoreType.DMA((slots,)),
+        ],
+        compiler_params=pltpu.CompilerParams(collective_id=1, has_side_effects=True),
+    )(parts)
+
+
 def expert_partial(flat_rows, w_gate, w_up, w_down):
     gate_part = jnp.dot(flat_rows, w_gate[0], preferred_element_type=jnp.float32)
     up_part = jnp.dot(flat_rows, w_up[0], preferred_element_type=jnp.float32)
@@ -193,8 +290,8 @@
         precision=lax.Precision.HIGHEST,
         preferred_element_type=jnp.float32,
     )
-    mixed = lax.psum_scatter(
-        column_mixed.astype(jnp.bfloat16), "grp", scatter_dimension=0, tiled=True
+    mixed = ring_scatter(
+        column_mixed.astype(jnp.bfloat16).reshape(group_count, row_count, feature), group_count
     )
     return (context, mixed)
 

time: 236 us -> 192 us (0.81)
  waiting for transfers between devices: 104 us -> 48.4 us
  Pallas kernels: 26.1 us -> 50.3 us
  between operations: 14.9 us -> 1.49 us
    reduce_scatter x1 -> x0, waiting for transfers between devices: 52.8 us -> none  [per_device(): lax.psum_scatter(column_mixed.astype(jnp.bfloat16), 'grp', scatter_dimens...]
    pallas_call x0 -> x1, Pallas kernels: none -> 24.2 us  [ring_scatter(): pl.pallas_call(functools.partial(scatter_kernel, chips), out_shape=jax.Sh...]
    all_to_all x1, waiting for transfers between devices: 50.9 us -> 48.4 us  [per_device(): lax.all_to_all(partials.reshape(peer_count, expert_slots, feature), 'ep',...]
  transfers between devices with their start and end apart: 2 -> 1, of which waited for: 2 -> 1; matrix products, arithmetic and copies ran while one was open for 2% -> 2% of each run, Pallas kernels for 0% -> 0%
where the time goes in v4:
time: 192 us; the launch traced here: 191 us
  blocking collectives  51.7 us (27%)
  Pallas kernels  50.3 us (26%)
  waiting for transfers between devices  48.4 us (25%)
  matrix products  18.8 us (10%)
  other arithmetic  9.16 us (5%)
  local copies, waits for them, and re-layouts  6.64 us (3%)
  starting transfers between devices  4.64 us (2%)
    all_to_all x1, blocking collectives, per_device(): lax.all_to_all(doubled, 'ep', split_axis=0, concat_axis=0, tiled=True)  51.7 us
    all_to_all x1, waiting for transfers between devices, per_device(): lax.all_to_all(partials.reshape(peer_count, expert_slots, feature), 'ep',...  48.4 us
    pallas_call x1, Pallas kernels, ring_gather(): pl.pallas_call(functools.partial(gather_kernel, chips), out_shape=jax.Sha...  26.1 us
    pallas_call x1, Pallas kernels, ring_scatter(): pl.pallas_call(functools.partial(scatter_kernel, chips), out_shape=jax.Sh...  24.2 us
    dot_general x1, matrix products, expert_partial(): return jnp.dot(hidden, w_down[0], preferred_element_type=jnp.float32)  10.1 us
    all_to_all x1, starting transfers between devices, per_device(): lax.all_to_all(partials.reshape(peer_count, expert_slots, feature), 'ep',...  4.64 us
    unnamed x15, local copies, waits for them, and re-layouts  4.37 us
  transfers between devices with their start and end apart: 1, of which 1 were waited for; matrix products, arithmetic and copies ran while one was open for 2% of the time, Pallas kernels for 0%

profile of v4, /device:TPU:1, one launch (start us, length us, event | category | flops | bytes accessed | tf_op | source)
XLA Modules:
  0.0 191.2 jit_solution(4653328200085357164)
XLA Ops:
  0.6 0.7 convert_element_type.54
  1.4 0.8 copy.35
  2.1 0.1 copy.37
  2.2 0.7 convert_element_type.53
  2.9 0.1 copy.36
  3.0 0.1 fusion.30
  3.1 1.6 pad_maximum_fusion.x_ref
  4.7 26.1 %shard_map.113 = bf16[16,16,3712]{2,1,0:T(8,128)(2,1)} custom-call(bf16[16,3712]{1,0:T(8,128)(2,1)} %pad_maximum_fusion.x_ref), custom_call_target="tpu_custom_call" | custom-call | tf_op jit(solution)/shard_map/pallas_call | solution.py:108
  30.7 1.1 fusion.35
  32.0 0.1 copy.39
  32.1 0.7 fusion.37
  32.8 0.1 copy.40
  32.9 0.1 reduce_window_sum.14
  33.1 0.1 copy.41
  33.2 0.7 fusion.6
  34.0 2.2 %convolution_convert_fusion.2 = bf16[256,3584]{1,0:T(8,128)(2,1)S(1)} fusion(pred[256,256]{1,0:T(8,128)(4,1)S(1)} %fusion.6, bf16[256,3712]{1,0:T(8,128)(2,1)} %bitcast.42), kind=kOutput, calls=%fused_computation.3 | convolution fusion | flops 470679552 | bytes 3735552 | tf_op jit(solution)/shard_map/dot_general | solution.py:265
  36.2 0.4 broadcast_in_dim.46
  36.6 51.7 %all_to_all.10 = bf16[16,32,3584]{2,1,0:T(8,128)(2,1)S(1)} all-to-all(bf16[16,32,3584]{2,1,0:T(8,128)(2,1)S(1)} %bitcast.40), channel_id=1, replica_groups=mesh['grp'=16,'ep'=16] {'ep'}, dimensions={0} | all-to-all | bytes 7340032 | tf_op jit(solution)/shard_map/all_to_all | solution.py:269
  88.3 1.8 copy-done.1
  90.1 2.0 %fusion.4 = f32[512,512]{1,0:T(8,128)S(1)} fusion(bf16[512,3584]{1,0:T(8,128)(2,1)S(1)} %bitcast.47, bf16[1,3584,512]{2,1,0:T(8,128)(2,1)S(1)} %copy-done.4), kind=kOutput, calls=%fused_computation.8 | convolution fusion | flops 1879048192 | bytes 8388608 | tf_op jit(solution)/shard_map/dot_general | solution.py:219
  92.2 10.1 %convolution_convert_fusion = bf16[512,3584]{1,0:T(8,128)(2,1)} fusion(bf16[1,512,3584]{2,1,0:T(8,128)(2,1)} %param.19, bf16[512,3584]{1,0:T(8,128)(2,1)} %bitcast.48, bf16[1,3584,512]{2,1,0:T(8,128)(2,1)} %param.18, f32[512,512]{1,0:T(8,128)S(1)} %fusion.4), kind=kOutput, calls=%fused_computation.1 | convolution fusion | flops 3761504256 | bytes 15728640 | tf_op jit(solution)/shard_map/dot_general | solution.py:222
  102.2 4.6 %all-to-all-start.1 = ((bf16[16,32,3584]{2,1,0:T(8,128)(2,1)}), bf16[16,32,3584]{2,1,0:T(8,128)(2,1)}, u32[]{:S(2)}, u32[]{:S(2)}) async-start(bf16[16,32,3584]{2,1,0:T(8,128)(2,1)} %bitcast.46), calls=%async_computation.1 | async-start | bytes 7340032 | tf_op jit(solution)/shard_map/all_to_all | solution.py:273
  107.1 0.1 copy.44
  107.9 0.3 fusion.15
  108.3 0.2 fusion.36
  108.5 1.5 select_reduce_fusion
  110.0 1.2 fusion.18
  111.2 48.4 %all-to-all-done.1 = bf16[16,32,3584]{2,1,0:T(8,128)(2,1)} async-done(((bf16[16,32,3584]{2,1,0:T(8,128)(2,1)}), bf16[16,32,3584]{2,1,0:T(8,128)(2,1)}, u32[]{:S(2)}, u32[]{:S(2)}) %all-to-all-start.1) | async-done | bytes 3670048 | tf_op jit(solution)/shard_map/all_to_all | solution.py:273
  159.7 2.8 %bitcast_reduce_fusion = bf16[8,32,3584]{2,1,0:T(8,128)(2,1)S(1)} fusion(bf16[16,32,3584]{2,1,0:T(8,128)(2,1)} %all-to-all-done.1), kind=kLoop, calls=%fused_computation.4 | loop fusion | flops 917504 | bytes 5505024 | tf_op jit(solution)/shard_map/reduce_sum | solution.py:283
  162.5 2.9 %convolution_convert_fusion.1 = bf16[256,3584]{1,0:T(8,128)(2,1)} fusion(f32[256,256]{1,0:T(8,128)S(1)} %select_reduce_fusion, bf16[256,3584]{1,0:T(8,128)(2,1)S(1)} %bitcast.45), kind=kOutput, calls=%fused_computation.2 | convolution fusion | flops 2819489792 | bytes 3932160 | tf_op jit(solution)/shard_map/dot_general | solution.py:287
  165.4 24.2 %shard_map.114 = bf16[16,3584]{1,0:T(8,128)(2,1)} custom-call(bf16[16,16,3584]{2,1,0:T(8,128)(2,1)} %bitcast.44), custom_call_target="tpu_custom_call" | custom-call | tf_op jit(solution)/shard_map/pallas_call | solution.py:200
  189.6 1.6 copy.51
  (22 shorter events, 0.5 us)
Async XLA Ops:
  0.6 107.3 %copy-start = (bf16[4,64,576]{2,1,0:T(8,128)(2,1)S(1)}, bf16[4,64,576]{2,1,0:T(8,128)(2,1)}, u32[]{:S(2)}) copy-start(bf16[4,64,576]{2,1,0:T(8,128)(2,1)} %param.10) | copy-start | bytes 884740
  36.6 53.6 %copy-start.4 = (bf16[1,3584,512]{2,1,0:T(8,128)(2,1)S(1)}, bf16[1,3584,512]{2,1,0:T(8,128)(2,1)}, u32[]{:S(2)}) copy-start(bf16[1,3584,512]{2,1,0:T(8,128)(2,1)} %param.17) | copy-start | bytes 11010052
  88.3 1.8 copy-start.1
  102.2 5.7 %copy-start.2 = (bf16[4,256,576]{1,2,0:T(8,128)(2,1)S(1)}, bf16[4,256,576]{1,2,0:T(8,128)(2,1)}, u32[]{:S(2)}) copy-start(bf16[4,256,576]{1,2,0:T(8,128)(2,1)} %param.11) | copy-start | bytes 3538948
  102.2 5.7 %copy-start.3 = (s32[4]{0:T(128)S(1)}, s32[4]{0:T(128)}, u32[]{:S(2)}) copy-start(s32[4]{0:T(128)} %param.12) | copy-start | bytes 52
  102.2 57.4 %all-to-all-start.1 = ((bf16[16,32,3584]{2,1,0:T(8,128)(2,1)}), bf16[16,32,3584]{2,1,0:T(8,128)(2,1)}, u32[]{:S(2)}, u32[]{:S(2)}) async-start(bf16[16,32,3584]{2,1,0:T(8,128)(2,1)} %bitcast.46), calls=%async_computation.1 | async-start | bytes 7340032 | tf_op jit(solution)/shard_map/all_to_all | solution.py:273

commit v5 on v4

--- a/solution.py
+++ b/solution.py
@@ -215,6 +215,68 @@
     )(parts)
 
 
+def exchange_kernel(peer_count, from_pair, src_ref, out_ref, send_sem, recv_sem):
+    group = lax.axis_index("grp")
+    me = lax.axis_index("ep")
+
+    def source_of(dest):
+        return dest // 2 if from_pair else dest
+
+    barrier = pltpu.get_barrier_semaphore()
+    for shift in range(1, peer_count):
+        pl.semaphore_signal(
+            barrier,
+            inc=1,
+            device_id=(group, lax.rem(me + shift, peer_count)),
+            device_id_type=MESH,
+        )
+    pl.semaphore_wait(barrier, peer_count - 1)
+
+    started = []
+    for shift in range(1, peer_count):
+        dest = lax.rem(me + shift, peer_count)
+        copy = pltpu.make_async_remote_copy(
+            src_ref=src_ref.at[source_of(dest)],
+            dst_ref=out_ref.at[me],
+            send_sem=send_sem.at[shift - 1],
+            recv_sem=recv_sem.at[me],
+            device_id=(group, dest),
+            device_id_type=MESH,
+        )
+        copy.start()
+        started.append(copy)
+    out_ref[me] = src_ref[source_of(me)]
+    for shift in range(1, peer_count):
+        origin = lax.rem(me + peer_count - shift, peer_count)
+        pltpu.make_async_remote_copy(
+            src_ref=out_ref.at[origin],
+            dst_ref=out_ref.at[origin],
+            send_sem=send_sem.at[0],
+            recv_sem=recv_sem.at[origin],
+            device_id=(group, origin),
+            device_id_type=MESH,
+        ).wait_recv()
+    for copy in started:
+        copy.wait_send()
+
+
+def exchange(blocks, peer_count, from_pair, collective_id):
+    block = blocks.shape[1:]
+    return pl.pallas_call(
+        functools.partial(exchange_kernel, peer_count, from_pair),
+        out_shape=jax.ShapeDtypeStruct((peer_count,) + block, blocks.dtype),
+        in_specs=[pl.BlockSpec(memory_space=pltpu.VMEM)],
+        out_specs=pl.BlockSpec(memory_space=pltpu.VMEM),
+        scratch_shapes=[
+            pltpu.SemaphoreType.DMA((peer_count - 1,)),
+            pltpu.SemaphoreType.DMA((peer_count,)),
+        ],
+        compiler_params=pltpu.CompilerParams(
+            collective_id=collective_id, has_side_effects=True
+        ),
+    )(blocks)
+
+
 def expert_partial(flat_rows, w_gate, w_up, w_down):
     gate_part = jnp.dot(flat_rows, w_gate[0], preferred_element_type=jnp.float32)
     up_part = jnp.dot(flat_rows, w_up[0], preferred_element_type=jnp.float32)
@@ -265,17 +327,14 @@
     outgoing = jnp.dot(dispatch, all_tokens, preferred_element_type=jnp.float32).astype(
         jnp.bfloat16
     )
-    doubled = jnp.repeat(outgoing.reshape(pair_count, expert_slots, feature), 2, axis=0)
-    arriving = lax.all_to_all(doubled, "ep", split_axis=0, concat_axis=0, tiled=True)
+    arriving = exchange(
+        outgoing.reshape(pair_count, expert_slots, feature), peer_count, True, 2
+    )
     partials = expert_partial(
         arriving.reshape(peer_count * expert_slots, feature), w_gate, w_up, w_down
     ).astype(jnp.bfloat16)
-    returned = lax.all_to_all(
-        partials.reshape(peer_count, expert_slots, feature),
-        "ep",
-        split_axis=0,
-        concat_axis=0,
-        tiled=True,
+    returned = exchange(
+        partials.reshape(peer_count, expert_slots, feature), peer_count, False, 3
     )
     expert_out = (
         returned.reshape(pair_count, 2, expert_slots, feature)

time: 192 us -> 219 us (1.14)
  Pallas kernels: 50.3 us -> 178 us
  blocking collectives: 51.7 us -> 0 us
  waiting for transfers between devices: 48.4 us -> 0 us
  starting transfers between devices: 4.64 us -> 0 us
  matrix products: 18.8 us -> 23.2 us
    pallas_call x0 -> x2, Pallas kernels: none -> 128 us  [exchange(): pl.pallas_call(functools.partial(exchange_kernel, peer_count, from_pair),...]
    all_to_all x1 -> x0, blocking collectives: 51.7 us -> none  [per_device(): lax.all_to_all(doubled, 'ep', split_axis=0, concat_axis=0, tiled=True)]
    all_to_all x1 -> x0, waiting for transfers between devices: 48.4 us -> none  [per_device(): lax.all_to_all(partials.reshape(peer_count, expert_slots, feature), 'ep',...]
    all_to_all x1 -> x0, starting transfers between devices: 4.64 us -> none  [per_device(): lax.all_to_all(partials.reshape(peer_count, expert_slots, feature), 'ep',...]
    dot_general x1, matrix products: 2.05 us -> 5.21 us  [expert_partial(): jnp.dot(flat_rows, w_gate[0], preferred_element_type=jnp.float32)]
  transfers between devices with their start and end apart: 1 -> 0, of which waited for: 1 -> 0; matrix products, arithmetic and copies ran while one was open for 2% -> 0% of each run, Pallas kernels for 0% -> 0%
where the time goes in v5:
time: 219 us; the launch traced here: 218 us
  Pallas kernels  178 us (81%)
  matrix products  23.2 us (11%)
  other arithmetic  9.99 us (5%)
  local copies, waits for them, and re-layouts  5.74 us (3%)
    pallas_call x2, Pallas kernels, exchange(): pl.pallas_call(functools.partial(exchange_kernel, peer_count, from_pair),...  128 us
    pallas_call x1, Pallas kernels, ring_gather(): pl.pallas_call(functools.partial(gather_kernel, chips), out_shape=jax.Sha...  26.1 us
    pallas_call x1, Pallas kernels, ring_scatter(): pl.pallas_call(functools.partial(scatter_kernel, chips), out_shape=jax.Sh...  23.9 us
    dot_general x1, matrix products, expert_partial(): return jnp.dot(hidden, w_down[0], preferred_element_type=jnp.float32)  10.1 us
    dot_general x1, matrix products, expert_partial(): jnp.dot(flat_rows, w_gate[0], preferred_element_type=jnp.float32)  5.21 us

profile of v5, /device:TPU:1, one launch (start us, length us, event | category | flops | bytes accessed | tf_op | source)
XLA Modules:
  0.0 218.2 jit_solution(9869080970140190696)
XLA Ops:
  0.6 0.7 convert_element_type.54
  1.4 0.1 copy.37
  1.5 0.8 copy.35
  2.2 0.7 convert_element_type.53
  2.9 0.1 copy.36
  3.0 0.1 fusion.30
  3.1 1.6 pad_maximum_fusion.x_ref
  4.6 26.1 %shard_map.113 = bf16[16,16,3712]{2,1,0:T(8,128)(2,1)} custom-call(bf16[16,3712]{1,0:T(8,128)(2,1)} %pad_maximum_fusion.x_ref), custom_call_target="tpu_custom_call" | custom-call | tf_op jit(solution)/shard_map/pallas_call | solution.py:108
  30.7 1.7 fusion.35
  32.5 0.1 reshape.118
  32.6 0.1 copy.39
  32.8 0.7 fusion.37
  33.4 0.1 copy.40
  33.6 0.1 reduce_window_sum.14
  33.7 0.1 copy.41
  33.9 0.7 fusion.6
  34.6 3.5 %convolution_convert_fusion.2 = bf16[256,3584]{1,0:T(8,128)(2,1)} fusion(pred[256,256]{1,0:T(8,128)(4,1)S(1)} %fusion.6, bf16[256,3712]{1,0:T(8,128)(2,1)} %bitcast.40), kind=kOutput, calls=%fused_computation.3 | convolution fusion | flops 470679552 | bytes 3735552 | tf_op jit(solution)/shard_map/dot_general | solution.py:327
  38.1 67.4 %shard_map.114 = bf16[16,32,3584]{2,1,0:T(8,128)(2,1)} custom-call(bf16[8,32,3584]{2,1,0:T(8,128)(2,1)} %bitcast.41), custom_call_target="tpu_custom_call" | custom-call | tf_op jit(solution)/shard_map/pallas_call | solution.py:265
  105.4 5.2 %fusion.4 = f32[512,512]{1,0:T(8,128)S(1)} fusion(bf16[512,3584]{1,0:T(8,128)(2,1)} %bitcast.45, bf16[1,3584,512]{2,1,0:T(8,128)(2,1)} %param.17), kind=kOutput, calls=%fused_computation.8 | convolution fusion | flops 1879048192 | bytes 8388608 | tf_op jit(solution)/shard_map/dot_general | solution.py:281
  110.7 10.1 %convolution_convert_fusion = bf16[512,3584]{1,0:T(8,128)(2,1)} fusion(bf16[1,512,3584]{2,1,0:T(8,128)(2,1)} %param.19, bf16[512,3584]{1,0:T(8,128)(2,1)} %bitcast.46, bf16[1,3584,512]{2,1,0:T(8,128)(2,1)} %param.18, f32[512,512]{1,0:T(8,128)S(1)} %fusion.4), kind=kOutput, calls=%fused_computation.1 | convolution fusion | flops 3761504256 | bytes 15728640 | tf_op jit(solution)/shard_map/dot_general | solution.py:284
  120.7 60.5 %shard_map.115 = bf16[16,32,3584]{2,1,0:T(8,128)(2,1)} custom-call(bf16[16,32,3584]{2,1,0:T(8,128)(2,1)} %bitcast.44), custom_call_target="tpu_custom_call" | custom-call | tf_op jit(solution)/shard_map/pallas_call | solution.py:265
  181.2 2.8 %bitcast_reduce_fusion = bf16[8,32,3584]{2,1,0:T(8,128)(2,1)S(1)} fusion(bf16[16,32,3584]{2,1,0:T(8,128)(2,1)} %shard_map.115), kind=kLoop, calls=%fused_computation.4 | loop fusion | flops 917504 | bytes 5505024 | tf_op jit(solution)/shard_map/reduce_sum | solution.py:342
  184.0 1.0 copy.47
  185.0 0.1 copy.48
  185.2 0.8 copy.44
  186.0 2.3 %select_reduce_fusion = f32[256,256]{1,0:T(8,128)S(1)} fusion(f32[256,8]{1,0:T(8,128)} %copy.44, s32[256,8]{1,0:T(8,128)S(1)} %copy.41), kind=kLoop, calls=%fused_computation.10 | loop fusion | flops 1507328 | bytes 278528 | tf_op jit(solution)/shard_map/reduce_sum | solution.py:325
  188.3 2.9 %convolution_convert_fusion.1 = bf16[256,3584]{1,0:T(8,128)(2,1)} fusion(f32[256,256]{1,0:T(8,128)S(1)} %select_reduce_fusion, bf16[256,3584]{1,0:T(8,128)(2,1)S(1)} %bitcast.43), kind=kOutput, calls=%fused_computation.2 | convolution fusion | flops 2819489792 | bytes 3932160 | tf_op jit(solution)/shard_map/dot_general | solution.py:346
  191.1 23.9 %shard_map.116 = bf16[16,3584]{1,0:T(8,128)(2,1)} custom-call(bf16[16,16,3584]{2,1,0:T(8,128)(2,1)} %bitcast.42), custom_call_target="tpu_custom_call" | custom-call | tf_op jit(solution)/shard_map/pallas_call | solution.py:200
  215.1 0.3 fusion.15
  215.4 0.2 fusion.36
  216.3 1.2 fusion.18
  217.6 0.6 copy.51
  (18 shorter events, 0.3 us)
Async XLA Ops:
  0.6 214.4 %copy-start = (bf16[4,64,576]{2,1,0:T(8,128)(2,1)S(1)}, bf16[4,64,576]{2,1,0:T(8,128)(2,1)}, u32[]{:S(2)}) copy-start(bf16[4,64,576]{2,1,0:T(8,128)(2,1)} %param.10) | copy-start | bytes 884740
  184.0 31.0 %copy-start.1 = (bf16[4,256,576]{1,2,0:T(8,128)(2,1)S(1)}, bf16[4,256,576]{1,2,0:T(8,128)(2,1)}, u32[]{:S(2)}) copy-start(bf16[4,256,576]{1,2,0:T(8,128)(2,1)} %param.11) | copy-start | bytes 3538948
  185.1 29.9 %copy-start.3 = (s32[4]{0:T(128)S(1)}, s32[4]{0:T(128)}, u32[]{:S(2)}) copy-start(s32[4]{0:T(128)} %param.12) | copy-start | bytes 52
  215.1 2.5 %copy-start.2 = (bf16[16,3584]{1,0:T(8,128)(2,1)S(1)}, bf16[16,3584]{1,0:T(8,128)(2,1)}, u32[]{:S(2)}) copy-start(bf16[16,3584]{1,0:T(8,128)(2,1)} %shard_map.116) | copy-start | bytes 344068

commit v6 on v4

--- a/solution.py
+++ b/solution.py
@@ -265,25 +265,28 @@
     outgoing = jnp.dot(dispatch, all_tokens, preferred_element_type=jnp.float32).astype(
         jnp.bfloat16
     )
-    doubled = jnp.repeat(outgoing.reshape(pair_count, expert_slots, feature), 2, axis=0)
-    arriving = lax.all_to_all(doubled, "ep", split_axis=0, concat_axis=0, tiled=True)
-    partials = expert_partial(
-        arriving.reshape(peer_count * expert_slots, feature), w_gate, w_up, w_down
-    ).astype(jnp.bfloat16)
-    returned = lax.all_to_all(
-        partials.reshape(peer_count, expert_slots, feature),
-        "ep",
-        split_axis=0,
-        concat_axis=0,
-        tiled=True,
-    )
-    expert_out = (
-        returned.reshape(pair_count, 2, expert_slots, feature)
-        .astype(jnp.float32)
-        .sum(axis=1)
-        .astype(jnp.bfloat16)
-        .reshape(slot_count, feature)
-    )
+    staged = outgoing.reshape(pair_count, 2, expert_slots // 2, feature)
+    answers = []
+    for part in range(2):
+        doubled = jnp.repeat(staged[:, part], 2, axis=0)
+        arriving = lax.all_to_all(doubled, "ep", split_axis=0, concat_axis=0, tiled=True)
+        partials = expert_partial(
+            arriving.reshape(peer_count * expert_slots // 2, feature), w_gate, w_up, w_down
+        ).astype(jnp.bfloat16)
+        returned = lax.all_to_all(
+            partials.reshape(peer_count, expert_slots // 2, feature),
+            "ep",
+            split_axis=0,
+            concat_axis=0,
+            tiled=True,
+        )
+        answers.append(
+            returned.reshape(pair_count, 2, expert_slots // 2, feature)
+            .astype(jnp.float32)
+            .sum(axis=1)
+            .astype(jnp.bfloat16)
+        )
+    expert_out = jnp.stack(answers, axis=1).reshape(slot_count, feature)
     column_mixed = jnp.dot(
         combine,
         expert_out.astype(jnp.float32),

time: 192 us -> 194 us (1.010)
  blocking collectives: 51.7 us -> 31.8 us
  matrix products: 18.8 us -> 29.9 us
  starting transfers between devices: 4.64 us -> 15.4 us
  waiting for transfers between devices: 48.4 us -> 41.9 us
  local copies, waits for them, and re-layouts: 6.64 us -> 11 us
  Pallas kernels: 50.3 us -> 52.6 us
    all_to_all x1, blocking collectives: 51.7 us -> 31.8 us  [per_device(): lax.all_to_all(doubled, 'ep', split_axis=0, concat_axis=0, tiled=True)]
    all_to_all x1 -> x3, starting transfers between devices: 4.64 us -> 15.4 us  [the longest x2 11.7 us: per_device(): lax.all_to_all(partials.reshape(peer_count, expert_slots // 2, feature),...]
    all_to_all x1 -> x3, waiting for transfers between devices: 48.4 us -> 41.9 us  [the longest x2 27.7 us: per_device(): lax.all_to_all(partials.reshape(peer_count, expert_slots // 2, feature),...]
    dot_general x1 -> x2, matrix products: 2.05 us -> 7.39 us  [expert_partial(): jnp.dot(flat_rows, w_gate[0], preferred_element_type=jnp.float32)]
    dot_general x1 -> x2, matrix products: 10.1 us -> 14.2 us  [expert_partial(): return jnp.dot(hidden, w_down[0], preferred_element_type=jnp.float32)]
    pallas_call x1, Pallas kernels: 24.2 us -> 26.5 us  [ring_scatter(): pl.pallas_call(functools.partial(scatter_kernel, chips), out_shape=jax.Sh...]
    unnamed x15 -> x19, local copies, waits for them, and re-layouts: 4.37 us -> 6.08 us
  transfers between devices with their start and end apart: 1 -> 3, of which waited for: 1 -> 3; matrix products, arithmetic and copies ran while one was open for 2% -> 15% of each run, Pallas kernels for 0% -> 0%
where the time goes in v6:
time: 194 us; the launch traced here: 193 us
  Pallas kernels  52.6 us (27%)
  waiting for transfers between devices  41.9 us (22%)
  blocking collectives  31.8 us (16%)
  matrix products  29.9 us (15%)
  starting transfers between devices  15.4 us (8%)
  local copies, waits for them, and re-layouts  11 us (6%)
  other arithmetic  9.29 us (5%)
    all_to_all x1, blocking collectives, per_device(): lax.all_to_all(doubled, 'ep', split_axis=0, concat_axis=0, tiled=True)  31.8 us
    all_to_all x2, waiting for transfers between devices, per_device(): lax.all_to_all(partials.reshape(peer_count, expert_slots // 2, feature),...  27.7 us
    pallas_call x1, Pallas kernels, ring_scatter(): pl.pallas_call(functools.partial(scatter_kernel, chips), out_shape=jax.Sh...  26.5 us
    pallas_call x1, Pallas kernels, ring_gather(): pl.pallas_call(functools.partial(gather_kernel, chips), out_shape=jax.Sha...  26.1 us
    all_to_all x1, waiting for transfers between devices, per_device(): lax.all_to_all(doubled, 'ep', split_axis=0, concat_axis=0, tiled=True)  14.2 us
    dot_general x2, matrix products, expert_partial(): return jnp.dot(hidden, w_down[0], preferred_element_type=jnp.float32)  14.2 us
    all_to_all x2, starting transfers between devices, per_device(): lax.all_to_all(partials.reshape(peer_count, expert_slots // 2, feature),...  11.7 us
    dot_general x2, matrix products, expert_partial(): jnp.dot(flat_rows, w_gate[0], preferred_element_type=jnp.float32)  7.39 us
  transfers between devices with their start and end apart: 3, of which 3 were waited for; matrix products, arithmetic and copies ran while one was open for 15% of the time, Pallas kernels for 0%

profile of v6, /device:TPU:1, one launch (start us, length us, event | category | flops | bytes accessed | tf_op | source)
XLA Modules:
  0.0 193.5 jit_solution(16941908586816689181)
XLA Ops:
  0.6 0.7 convert_element_type.62
  1.4 0.8 copy.35
  2.2 0.7 convert_element_type.61
  3.1 1.6 pad_maximum_fusion.1.x_ref
  4.7 26.1 %shard_map.113 = bf16[16,16,3712]{2,1,0:T(8,128)(2,1)} custom-call(bf16[16,3712]{1,0:T(8,128)(2,1)} %pad_maximum_fusion.1.x_ref), custom_call_target="tpu_custom_call" | custom-call | tf_op jit(solution)/shard_map/pallas_call | solution.py:108
  30.7 1.7 fusion.60
  33.9 0.7 fusion.11
  34.6 2.2 %convolution_convert_fusion.3 = bf16[256,3584]{1,0:T(8,128)(2,1)S(1)} fusion(pred[256,256]{1,0:T(8,128)(4,1)S(1)} %fusion.11, bf16[256,3712]{1,0:T(8,128)(2,1)} %bitcast.66), kind=kOutput, calls=%fused_computation.4 | convolution fusion | flops 470679552 | bytes 3735552 | tf_op jit(solution)/shard_map/dot_general | solution.py:265
  37.1 31.8 %all_to_all.20 = bf16[16,16,3584]{2,1,0:T(8,128)(2,1)} all-to-all(bf16[16,16,3584]{2,1,0:T(8,128)(2,1)S(1)} %bitcast.69), channel_id=1, replica_groups=mesh['grp'=16,'ep'=16] {'ep'}, dimensions={0} | all-to-all | bytes 3670016 | tf_op jit(solution)/shard_map/all_to_all | solution.py:272
  68.9 1.4 broadcast_in_dim.50
  70.4 3.7 %all-to-all-start.2 = ((bf16[16,16,3584]{2,1,0:T(8,128)(2,1)}), bf16[16,16,3584]{2,1,0:T(8,128)(2,1)S(1)}, u32[]{:S(2)}, u32[]{:S(2)}) async-start(bf16[16,16,3584]{2,1,0:T(8,128)(2,1)} %bitcast.13), calls=%async_computation.2 | async-start | bytes 3670016 | tf_op jit(solution)/shard_map/all_to_all | solution.py:272
  74.1 3.7 %fusion.9 = f32[256,512]{1,0:T(8,128)S(1)} fusion(bf16[256,3584]{1,0:T(8,128)(2,1)} %bitcast.77, bf16[1,3584,512]{2,1,0:T(8,128)(2,1)} %param.17), kind=kOutput, calls=%fused_computation.13 | convolution fusion | flops 939524096 | bytes 6029312 | tf_op jit(solution)/shard_map/dot_general | solution.py:219
  77.8 7.1 %convolution_convert_fusion.2 = bf16[256,3584]{1,0:T(8,128)(2,1)} fusion(bf16[1,512,3584]{2,1,0:T(8,128)(2,1)} %param.19, bf16[256,3584]{1,0:T(8,128)(2,1)} %bitcast.78, bf16[1,3584,512]{2,1,0:T(8,128)(2,1)} %param.18, f32[256,512]{1,0:T(8,128)S(1)} %fusion.9), kind=kOutput, calls=%fused_computation.3 | convolution fusion | flops 1880752128 | bytes 11534336 | tf_op jit(solution)/shard_map/dot_general | solution.py:222
  84.9 14.2 %all-to-all-done.2 = bf16[16,16,3584]{2,1,0:T(8,128)(2,1)S(1)} async-done(((bf16[16,16,3584]{2,1,0:T(8,128)(2,1)}), bf16[16,16,3584]{2,1,0:T(8,128)(2,1)S(1)}, u32[]{:S(2)}, u32[]{:S(2)}) %all-to-all-start.2) | async-done | bytes 1835040 | tf_op jit(solution)/shard_map/all_to_all | solution.py:272
  99.1 1.3 copy-done.1
  100.3 5.5 %all-to-all-start.1 = ((bf16[16,16,3584]{2,1,0:T(8,128)(2,1)}), bf16[16,16,3584]{2,1,0:T(8,128)(2,1)S(1)}, u32[]{:S(2)}, u32[]{:S(2)}) async-start(bf16[16,16,3584]{2,1,0:T(8,128)(2,1)} %bitcast.76), calls=%async_computation.1 | async-start | bytes 3670016 | tf_op jit(solution)/shard_map/all_to_all | solution.py:276
  105.8 3.7 %fusion.7 = f32[256,512]{1,0:T(8,128)S(1)} fusion(bf16[256,3584]{1,0:T(8,128)(2,1)} %bitcast.74, bf16[1,3584,512]{2,1,0:T(8,128)(2,1)} %param.17), kind=kOutput, calls=%fused_computation.11 | convolution fusion | flops 939524096 | bytes 6029312 | tf_op jit(solution)/shard_map/dot_general | solution.py:219
  109.5 7.1 %convolution_convert_fusion.1 = bf16[256,3584]{1,0:T(8,128)(2,1)} fusion(bf16[1,512,3584]{2,1,0:T(8,128)(2,1)} %param.19, bf16[256,3584]{1,0:T(8,128)(2,1)} %bitcast.75, bf16[1,3584,512]{2,1,0:T(8,128)(2,1)} %param.18, f32[256,512]{1,0:T(8,128)S(1)} %fusion.7), kind=kOutput, calls=%fused_computation.2 | convolution fusion | flops 1880752128 | bytes 11534336 | tf_op jit(solution)/shard_map/dot_general | solution.py:222
  116.6 13.7 %all-to-all-done.1 = bf16[16,16,3584]{2,1,0:T(8,128)(2,1)S(1)} async-done(((bf16[16,16,3584]{2,1,0:T(8,128)(2,1)}), bf16[16,16,3584]{2,1,0:T(8,128)(2,1)S(1)}, u32[]{:S(2)}, u32[]{:S(2)}) %all-to-all-start.1) | async-done | bytes 1835040 | tf_op jit(solution)/shard_map/all_to_all | solution.py:276
  130.4 6.2 %all-to-all-start.3 = ((bf16[16,16,3584]{2,1,0:T(8,128)(2,1)}), bf16[16,16,3584]{2,1,0:T(8,128)(2,1)}, u32[]{:S(2)}, u32[]{:S(2)}) async-start(bf16[16,16,3584]{2,1,0:T(8,128)(2,1)} %bitcast.73), calls=%async_computation.3 | async-start | bytes 3670016 | tf_op jit(solution)/shard_map/all_to_all | solution.py:276
  136.6 0.9 copy.47
  137.6 0.8 copy.44
  139.1 1.0 fusion.26
  140.2 0.7 copy-done.5
  141.1 2.2 %select_reduce_fusion = f32[256,256]{1,0:T(8,128)} fusion(f32[256,8]{1,0:T(8,128)S(1)} %copy-done.4, s32[256,8]{1,0:T(8,128)S(1)} %copy.41), kind=kLoop, calls=%fused_computation.15 | loop fusion | flops 1507328 | bytes 278528 | tf_op jit(solution)/shard_map/reduce_sum | solution.py:263
  143.3 2.3 %fusion.29 = bf16[4,64,512]{2,1,0:T(8,128)(2,1)} fusion(bf16[4,256,576]{1,2,0:T(8,128)(2,1)S(1)} %copy-done.2, pred[4]{0:T(512)(128)(4,1)S(1)} %iota_compare_fusion.4, f32[4,64]{1,0:T(4,128)S(1)} %fusion.61, f32[4,64,256]{2,1,0:T(8,128)} %copy-done.5, s32[4]{0:T(128)S(1)} %copy-done.6), kind=kOutput, calls=%fused_computation.32 | convolution fusion | flops 67699200 | bytes 1838080 | tf_op jit(solution)/shard_map/rhl,rlc->rhc/dot_general | solution.py:31
  145.9 14.0 %all-to-all-done.3 = bf16[16,16,3584]{2,1,0:T(8,128)(2,1)} async-done(((bf16[16,16,3584]{2,1,0:T(8,128)(2,1)}), bf16[16,16,3584]{2,1,0:T(8,128)(2,1)}, u32[]{:S(2)}, u32[]{:S(2)}) %all-to-all-start.3) | async-done | bytes 1835040 | tf_op jit(solution)/shard_map/all_to_all | solution.py:276
  159.9 1.8 bitcast_reduce_fusion
  161.8 0.8 copy-done.3
  162.6 2.9 %convolution_convert_fusion = bf16[256,3584]{1,0:T(8,128)(2,1)} fusion(f32[256,256]{1,0:T(8,128)S(1)} %copy-done.3, bf16[256,3584]{1,0:T(8,128)(2,1)S(1)} %bitcast.68), kind=kOutput, calls=%fused_computation.1 | convolution fusion | flops 2819489792 | bytes 3932160 | tf_op jit(solution)/shard_map/dot_general | solution.py:290
  165.4 26.5 %shard_map.114 = bf16[16,3584]{1,0:T(8,128)(2,1)} custom-call(bf16[16,16,3584]{2,1,0:T(8,128)(2,1)} %bitcast.70), custom_call_target="tpu_custom_call" | custom-call | tf_op jit(solution)/shard_map/pallas_call | solution.py:200
  191.9 1.6 copy.51
  (36 shorter events, 2.8 us)
Async XLA Ops:
  0.6 138.5 %copy-start = (bf16[4,64,576]{2,1,0:T(8,128)(2,1)S(1)}, bf16[4,64,576]{2,1,0:T(8,128)(2,1)}, u32[]{:S(2)}) copy-start(bf16[4,64,576]{2,1,0:T(8,128)(2,1)} %param.10) | copy-start | bytes 884740
  70.4 28.7 %all-to-all-start.2 = ((bf16[16,16,3584]{2,1,0:T(8,128)(2,1)}), bf16[16,16,3584]{2,1,0:T(8,128)(2,1)S(1)}, u32[]{:S(2)}, u32[]{:S(2)}) async-start(bf16[16,16,3584]{2,1,0:T(8,128)(2,1)} %bitcast.13), calls=%async_computation.2 | async-start | bytes 3670016 | tf_op jit(solution)/shard_map/all_to_all | solution.py:272
  99.1 1.3 copy-start.1
  100.3 30.1 %all-to-all-start.1 = ((bf16[16,16,3584]{2,1,0:T(8,128)(2,1)}), bf16[16,16,3584]{2,1,0:T(8,128)(2,1)S(1)}, u32[]{:S(2)}, u32[]{:S(2)}) async-start(bf16[16,16,3584]{2,1,0:T(8,128)(2,1)} %bitcast.76), calls=%async_computation.1 | async-start | bytes 3670016 | tf_op jit(solution)/shard_map/all_to_all | solution.py:276
  130.4 8.8 %copy-start.2 = (bf16[4,256,576]{1,2,0:T(8,128)(2,1)S(1)}, bf16[4,256,576]{1,2,0:T(8,128)(2,1)}, u32[]{:S(2)}) copy-start(bf16[4,256,576]{1,2,0:T(8,128)(2,1)} %param.11) | copy-start | bytes 3538948
  130.4 29.5 %all-to-all-start.3 = ((bf16[16,16,3584]{2,1,0:T(8,128)(2,1)}), bf16[16,16,3584]{2,1,0:T(8,128)(2,1)}, u32[]{:S(2)}, u32[]{:S(2)}) async-start(bf16[16,16,3584]{2,1,0:T(8,128)(2,1)} %bitcast.73), calls=%async_computation.3 | async-start | bytes 3670016 | tf_op jit(solution)/shard_map/all_to_all | solution.py:276
  137.6 3.3 %copy-start.6 = (s32[4]{0:T(128)S(1)}, s32[4]{0:T(128)}, u32[]{:S(2)}) copy-start(s32[4]{0:T(128)} %param.12) | copy-start | bytes 52
  138.4 2.7 %copy-start.4 = (f32[256,8]{1,0:T(8,128)S(1)}, f32[256,8]{1,0:T(8,128)}, u32[]{:S(2)}) copy-start(f32[256,8]{1,0:T(8,128)} %copy.44) | copy-start | bytes 24580
  140.2 0.7 copy-start.5
  161.6 1.0 copy-start.3

commit v7 on v4

--- a/solution.py
+++ b/solution.py
@@ -277,18 +277,15 @@
         concat_axis=0,
         tiled=True,
     )
-    expert_out = (
-        returned.reshape(pair_count, 2, expert_slots, feature)
-        .astype(jnp.float32)
-        .sum(axis=1)
-        .astype(jnp.bfloat16)
-        .reshape(slot_count, feature)
-    )
-    column_mixed = jnp.dot(
-        combine,
-        expert_out.astype(jnp.float32),
-        precision=lax.Precision.HIGHEST,
-        preferred_element_type=jnp.float32,
+    by_half = jnp.broadcast_to(
+        combine.reshape(column_rows, pair_count, 1, expert_slots),
+        (column_rows, pair_count, 2, expert_slots),
+    ).reshape(column_rows, peer_count * expert_slots)
+    weight_high = by_half.astype(jnp.bfloat16)
+    weight_low = (by_half - weight_high.astype(jnp.float32)).astype(jnp.bfloat16)
+    halves = returned.reshape(peer_count * expert_slots, feature)
+    column_mixed = jnp.dot(weight_high, halves, preferred_element_type=jnp.float32) + jnp.dot(
+        weight_low, halves, preferred_element_type=jnp.float32
     )
     mixed = ring_scatter(
         column_mixed.astype(jnp.bfloat16).reshape(group_count, row_count, feature), group_count

time: 192 us -> 194 us (1.010)
  matrix products: 18.8 us -> 23.7 us
  other arithmetic: 9.16 us -> 6.39 us
    dot_general x1 -> x2, matrix products: 2.93 us -> 7.73 us  [the longest x1 4.53 us: per_device(): jnp.dot(weight_low, halves, preferred_element_type=jnp.float32)]
    reduce_sum x1 -> x0, other arithmetic: 2.8 us -> none  [per_device(): expert_out = returned.reshape(pair_count, 2, expert_slots, feature).astyp...]
where the time goes in v7:
time: 194 us; the launch traced here: 193 us
  blocking collectives  51.7 us (27%)
  Pallas kernels  50.3 us (26%)
  waiting for transfers between devices  48.2 us (25%)
  matrix products  23.7 us (12%)
  local copies, waits for them, and re-layouts  6.76 us (3%)
  other arithmetic  6.39 us (3%)
  starting transfers between devices  4.63 us (2%)
    all_to_all x1, blocking collectives, per_device(): lax.all_to_all(doubled, 'ep', split_axis=0, concat_axis=0, tiled=True)  51.7 us
    all_to_all x1, waiting for transfers between devices, per_device(): lax.all_to_all(partials.reshape(peer_count, expert_slots, feature), 'ep',...  48.2 us
    pallas_call x1, Pallas kernels, ring_gather(): pl.pallas_call(functools.partial(gather_kernel, chips), out_shape=jax.Sha...  26.1 us
    pallas_call x1, Pallas kernels, ring_scatter(): pl.pallas_call(functools.partial(scatter_kernel, chips), out_shape=jax.Sh...  24.2 us
    dot_general x1, matrix products, expert_partial(): return jnp.dot(hidden, w_down[0], preferred_element_type=jnp.float32)  10.1 us
    all_to_all x1, starting transfers between devices, per_device(): lax.all_to_all(partials.reshape(peer_count, expert_slots, feature), 'ep',...  4.63 us
    dot_general x1, matrix products, per_device(): jnp.dot(weight_low, halves, preferred_element_type=jnp.float32)  4.53 us
    unnamed x15, local copies, waits for them, and re-layouts  4.33 us
  transfers between devices with their start and end apart: 1, of which 1 were waited for; matrix products, arithmetic and copies ran while one was open for 2% of the time, Pallas kernels for 0%

profile of v7, /device:TPU:1, one launch (start us, length us, event | category | flops | bytes accessed | tf_op | source)
XLA Modules:
  0.0 193.2 jit_solution(7931532827818264643)
XLA Ops:
  0.6 0.7 convert_element_type.72
  1.4 0.8 copy.36
  2.1 0.1 copy.38
  2.2 0.7 convert_element_type.71
  2.9 0.1 copy.37
  3.1 1.6 pad_maximum_fusion.x_ref
  4.7 26.1 %shard_map.113 = bf16[16,16,3712]{2,1,0:T(8,128)(2,1)} custom-call(bf16[16,3712]{1,0:T(8,128)(2,1)} %pad_maximum_fusion.x_ref), custom_call_target="tpu_custom_call" | custom-call | tf_op jit(solution)/shard_map/pallas_call | solution.py:108
  30.7 1.1 fusion.36
  32.0 0.1 copy.40
  32.1 0.7 fusion.38
  32.8 0.1 copy.41
  32.9 0.1 reduce_window_sum.14
  33.1 0.1 copy.42
  33.2 0.7 fusion.7
  34.0 2.2 %convolution_convert_fusion.1 = bf16[256,3584]{1,0:T(8,128)(2,1)S(1)} fusion(pred[256,256]{1,0:T(8,128)(4,1)S(1)} %fusion.7, bf16[256,3712]{1,0:T(8,128)(2,1)} %bitcast.45), kind=kOutput, calls=%fused_computation.4 | convolution fusion | flops 470679552 | bytes 3735552 | tf_op jit(solution)/shard_map/dot_general | solution.py:265
  36.2 0.4 broadcast_in_dim.57
  36.6 51.7 %all_to_all.10 = bf16[16,32,3584]{2,1,0:T(8,128)(2,1)S(1)} all-to-all(bf16[16,32,3584]{2,1,0:T(8,128)(2,1)S(1)} %bitcast.43), channel_id=1, replica_groups=mesh['grp'=16,'ep'=16] {'ep'}, dimensions={0} | all-to-all | bytes 7340032 | tf_op jit(solution)/shard_map/all_to_all | solution.py:269
  88.3 1.8 copy-done.1
  90.1 2.0 %fusion.5 = f32[512,512]{1,0:T(8,128)S(1)} fusion(bf16[512,3584]{1,0:T(8,128)(2,1)S(1)} %bitcast.49, bf16[1,3584,512]{2,1,0:T(8,128)(2,1)S(1)} %copy-done.4), kind=kOutput, calls=%fused_computation.8 | convolution fusion | flops 1879048192 | bytes 8388608 | tf_op jit(solution)/shard_map/dot_general | solution.py:219
  92.1 10.1 %convolution_convert_fusion = bf16[512,3584]{1,0:T(8,128)(2,1)} fusion(bf16[1,512,3584]{2,1,0:T(8,128)(2,1)} %param.19, bf16[512,3584]{1,0:T(8,128)(2,1)} %bitcast.50, bf16[1,3584,512]{2,1,0:T(8,128)(2,1)} %param.18, f32[512,512]{1,0:T(8,128)S(1)} %fusion.5), kind=kOutput, calls=%fused_computation.1 | convolution fusion | flops 3761504256 | bytes 15728640 | tf_op jit(solution)/shard_map/dot_general | solution.py:222
  102.2 4.6 %all-to-all-start.1 = ((bf16[16,32,3584]{2,1,0:T(8,128)(2,1)}), bf16[16,32,3584]{2,1,0:T(8,128)(2,1)}, u32[]{:S(2)}, u32[]{:S(2)}) async-start(bf16[16,32,3584]{2,1,0:T(8,128)(2,1)} %bitcast.48), calls=%async_computation.1 | async-start | bytes 7340032 | tf_op jit(solution)/shard_map/all_to_all | solution.py:273
  107.1 0.1 copy.45
  107.2 1.5 select_reduce_fusion
  108.7 0.1 copy.46
  109.5 0.4 fusion.16
  109.9 0.2 fusion.37
  110.2 1.2 fusion.19
  111.4 48.2 %all-to-all-done.1 = bf16[16,32,3584]{2,1,0:T(8,128)(2,1)} async-done(((bf16[16,32,3584]{2,1,0:T(8,128)(2,1)}), bf16[16,32,3584]{2,1,0:T(8,128)(2,1)}, u32[]{:S(2)}, u32[]{:S(2)}) %all-to-all-start.1) | async-done | bytes 3670048 | tf_op jit(solution)/shard_map/all_to_all | solution.py:273
  159.7 3.2 %fusion.39 = f32[256,3584]{1,0:T(8,128)S(1)} fusion(bf16[256,512]{0,1:T(8,128)(2,1)S(1)} %bitcast.51, bf16[512,3584]{1,0:T(8,128)(2,1)} %bitcast.11), kind=kOutput, calls=%fused_computation.58 | convolution fusion | flops 939524096 | bytes 7602176 | tf_op jit(solution)/shard_map/dot_general | solution.py:287
  162.9 4.5 %fusion.1 = bf16[256,3584]{1,0:T(8,128)(2,1)} fusion(f32[256,3584]{1,0:T(8,128)S(1)} %fusion.39, bf16[256,512]{0,1:T(8,128)(2,1)S(1)} %bitcast.52, bf16[512,3584]{1,0:T(8,128)(2,1)} %bitcast.11), kind=kOutput, calls=%fused_computation.3 | convolution fusion | flops 941359104 | bytes 9437184 | tf_op jit(solution)/shard_map/dot_general | solution.py:287
  167.4 24.2 %shard_map.114 = bf16[16,3584]{1,0:T(8,128)(2,1)} custom-call(bf16[16,16,3584]{2,1,0:T(8,128)(2,1)} %bitcast.46), custom_call_target="tpu_custom_call" | custom-call | tf_op jit(solution)/shard_map/pallas_call | solution.py:200
  191.6 1.6 copy.53
  (26 shorter events, 0.6 us)
Async XLA Ops:
  0.6 108.9 %copy-start = (bf16[4,64,576]{2,1,0:T(8,128)(2,1)S(1)}, bf16[4,64,576]{2,1,0:T(8,128)(2,1)}, u32[]{:S(2)}) copy-start(bf16[4,64,576]{2,1,0:T(8,128)(2,1)} %param.10) | copy-start | bytes 884740
  36.6 53.5 %copy-start.4 = (bf16[1,3584,512]{2,1,0:T(8,128)(2,1)S(1)}, bf16[1,3584,512]{2,1,0:T(8,128)(2,1)}, u32[]{:S(2)}) copy-start(bf16[1,3584,512]{2,1,0:T(8,128)(2,1)} %param.17) | copy-start | bytes 11010052
  88.3 1.8 copy-start.1
  102.2 7.3 %copy-start.2 = (bf16[4,256,576]{1,2,0:T(8,128)(2,1)S(1)}, bf16[4,256,576]{1,2,0:T(8,128)(2,1)}, u32[]{:S(2)}) copy-start(bf16[4,256,576]{1,2,0:T(8,128)(2,1)} %param.11) | copy-start | bytes 3538948
  102.2 7.3 %copy-start.3 = (s32[4]{0:T(128)S(1)}, s32[4]{0:T(128)}, u32[]{:S(2)}) copy-start(s32[4]{0:T(128)} %param.12) | copy-start | bytes 52
  102.2 57.4 %all-to-all-start.1 = ((bf16[16,32,3584]{2,1,0:T(8,128)(2,1)}), bf16[16,32,3584]{2,1,0:T(8,128)(2,1)}, u32[]{:S(2)}, u32[]{:S(2)}) async-start(bf16[16,32,3584]{2,1,0:T(8,128)(2,1)} %bitcast.48), calls=%async_computation.1 | async-start | bytes 7340032 | tf_op jit(solution)/shard_map/all_to_all | solution.py:273

commit v8 on v4

--- a/solution.py
+++ b/solution.py
@@ -35,7 +35,7 @@
     return jnp.where(request_slot < live_count, context, jnp.zeros_like(context))
 
 
-def gather_kernel(chips, x_ref, out_ref, send_sem, recv_sem):
+def gather_kernel(chips, widths, x_ref, out_ref, send_sem, recv_sem):
     group = lax.axis_index("grp")
     peer_col = lax.axis_index("ep")
     z = group // 2
@@ -43,6 +43,7 @@
     right = lax.rem(z + 1, chips) * 2 + core
     left = lax.rem(z + chips - 1, chips) * 2 + core
     partner = z * 2 + (1 - core)
+    starts = [sum(widths[:piece]) for piece in range(len(widths))]
 
     barrier = pltpu.get_barrier_semaphore()
     for peer in (left, right, partner):
@@ -51,48 +52,58 @@
 
     started = []
 
-    def send(src, origin, peer):
+    def window(ref, origin, piece):
+        columns = pl.ds(starts[piece], widths[piece])
+        if origin is None:
+            return ref.at[:, columns]
+        return ref.at[origin, :, columns]
+
+    def send(origin, piece, peer, from_input):
         copy = pltpu.make_async_remote_copy(
-            src_ref=src,
-            dst_ref=out_ref.at[origin],
+            src_ref=window(x_ref, None, piece) if from_input else window(out_ref, origin, piece),
+            dst_ref=window(out_ref, origin, piece),
             send_sem=send_sem.at[len(started)],
-            recv_sem=recv_sem.at[origin],
+            recv_sem=recv_sem.at[origin, piece],
             device_id=(peer, peer_col),
             device_id_type=MESH,
         )
         copy.start()
         started.append(copy)
 
-    def arrive(origin, peer):
+    def arrive(origin, piece, peer):
         pltpu.make_async_remote_copy(
-            src_ref=out_ref.at[origin],
-            dst_ref=out_ref.at[origin],
+            src_ref=window(out_ref, origin, piece),
+            dst_ref=window(out_ref, origin, piece),
             send_sem=send_sem.at[0],
-            recv_sem=recv_sem.at[origin],
+            recv_sem=recv_sem.at[origin, piece],
             device_id=(peer, peer_col),
             device_id_type=MESH,
         ).wait_recv()
 
-    send(x_ref, group, right)
-    send(x_ref, group, left)
-    send(x_ref, group, partner)
+    for piece in range(len(widths)):
+        send(group, piece, right, True)
+        send(group, piece, left, True)
+        send(group, piece, partner, True)
     out_ref[group] = x_ref[...]
     forward_hops = chips // 2
     backward_hops = (chips - 1) // 2
     for step in range(1, forward_hops + 1):
         origin = lax.rem(z + chips - step, chips) * 2 + core
-        arrive(origin, left)
-        if step < forward_hops:
-            send(out_ref.at[origin], origin, right)
-        send(out_ref.at[origin], origin, partner)
+        for piece in range(len(widths)):
+            arrive(origin, piece, left)
+            if step < forward_hops:
+                send(origin, piece, right, False)
+            send(origin, piece, partner, False)
         if step <= backward_hops:
             origin = lax.rem(z + step, chips) * 2 + core
-            arrive(origin, right)
-            if step < backward_hops:
-                send(out_ref.at[origin], origin, left)
-            send(out_ref.at[origin], origin, partner)
+            for piece in range(len(widths)):
+                arrive(origin, piece, right)
+                if step < backward_hops:
+                    send(origin, piece, left, False)
+                send(origin, piece, partner, False)
     for other in range(chips):
-        arrive(other * 2 + (1 - core), partner)
+        for piece in range(len(widths)):
+            arrive(other * 2 + (1 - core), piece, partner)
     for copy in started:
         copy.wait_send()
 
@@ -105,14 +116,16 @@
 
 def ring_gather(block, group_count):
     chips = group_count // 2
+    lanes = block.shape[1] // 128
+    widths = (lanes // 2 * 128, (lanes - lanes // 2) * 128)
     return pl.pallas_call(
-        functools.partial(gather_kernel, chips),
+        functools.partial(gather_kernel, chips, widths),
         out_shape=jax.ShapeDtypeStruct((group_count,) + block.shape, block.dtype),
         in_specs=[pl.BlockSpec(memory_space=pltpu.VMEM)],
         out_specs=pl.BlockSpec(memory_space=pltpu.VMEM),
         scratch_shapes=[
-            pltpu.SemaphoreType.DMA((send_count(chips),)),
-            pltpu.SemaphoreType.DMA((group_count,)),
+            pltpu.SemaphoreType.DMA((send_count(chips) * len(widths),)),
+            pltpu.SemaphoreType.DMA((group_count, len(widths))),
         ],
         compiler_params=pltpu.CompilerParams(collective_id=0, has_side_effects=True),
     )(block)

time: 192 us -> 191 us (level)
  no operation moved by 1% of the time
where the time goes in v8:
time: 191 us; the launch traced here: 190 us
  blocking collectives  51.8 us (27%)
  Pallas kernels  49.1 us (26%)
  waiting for transfers between devices  48.6 us (25%)
  matrix products  18.8 us (10%)
  other arithmetic  9.16 us (5%)
  local copies, waits for them, and re-layouts  6.64 us (3%)
  starting transfers between devices  4.64 us (2%)
    all_to_all x1, blocking collectives, per_device(): lax.all_to_all(doubled, 'ep', split_axis=0, concat_axis=0, tiled=True)  51.8 us
    all_to_all x1, waiting for transfers between devices, per_device(): lax.all_to_all(partials.reshape(peer_count, expert_slots, feature), 'ep',...  48.6 us
    pallas_call x1, Pallas kernels, ring_gather(): pl.pallas_call(functools.partial(gather_kernel, chips, widths), out_shape...  25 us
    pallas_call x1, Pallas kernels, ring_scatter(): pl.pallas_call(functools.partial(scatter_kernel, chips), out_shape=jax.Sh...  24.1 us
    dot_general x1, matrix products, expert_partial(): return jnp.dot(hidden, w_down[0], preferred_element_type=jnp.float32)  10.1 us
    all_to_all x1, starting transfers between devices, per_device(): lax.all_to_all(partials.reshape(peer_count, expert_slots, feature), 'ep',...  4.64 us
    unnamed x15, local copies, waits for them, and re-layouts  4.37 us
  transfers between devices with their start and end apart: 1, of which 1 were waited for; matrix products, arithmetic and copies ran while one was open for 2% of the time, Pallas kernels for 0%

profile of v8, /device:TPU:1, one launch (start us, length us, event | category | flops | bytes accessed | tf_op | source)
XLA Modules:
  0.0 190.2 jit_solution(5448299381888237959)
XLA Ops:
  0.6 0.7 convert_element_type.54
  1.4 0.8 copy.35
  2.1 0.1 copy.37
  2.2 0.7 convert_element_type.53
  2.9 0.1 copy.36
  3.0 0.1 fusion.30
  3.1 1.6 pad_maximum_fusion.x_ref
  4.7 25.0 %shard_map.113 = bf16[16,16,3712]{2,1,0:T(8,128)(2,1)} custom-call(bf16[16,3712]{1,0:T(8,128)(2,1)} %pad_maximum_fusion.x_ref), custom_call_target="tpu_custom_call" | custom-call | tf_op jit(solution)/shard_map/pallas_call | solution.py:121
  29.7 1.1 fusion.35
  31.0 0.1 copy.39
  31.1 0.7 fusion.37
  31.8 0.1 copy.40
  31.9 0.1 reduce_window_sum.14
  32.1 0.1 copy.41
  32.2 0.7 fusion.6
  32.9 2.2 %convolution_convert_fusion.2 = bf16[256,3584]{1,0:T(8,128)(2,1)S(1)} fusion(pred[256,256]{1,0:T(8,128)(4,1)S(1)} %fusion.6, bf16[256,3712]{1,0:T(8,128)(2,1)} %bitcast.42), kind=kOutput, calls=%fused_computation.3 | convolution fusion | flops 470679552 | bytes 3735552 | tf_op jit(solution)/shard_map/dot_general | solution.py:278
  35.1 0.4 broadcast_in_dim.46
  35.5 51.8 %all_to_all.10 = bf16[16,32,3584]{2,1,0:T(8,128)(2,1)S(1)} all-to-all(bf16[16,32,3584]{2,1,0:T(8,128)(2,1)S(1)} %bitcast.40), channel_id=1, replica_groups=mesh['grp'=16,'ep'=16] {'ep'}, dimensions={0} | all-to-all | bytes 7340032 | tf_op jit(solution)/shard_map/all_to_all | solution.py:282
  87.3 1.8 copy-done.1
  89.2 2.0 %fusion.4 = f32[512,512]{1,0:T(8,128)S(1)} fusion(bf16[512,3584]{1,0:T(8,128)(2,1)S(1)} %bitcast.47, bf16[1,3584,512]{2,1,0:T(8,128)(2,1)S(1)} %copy-done.4), kind=kOutput, calls=%fused_computation.8 | convolution fusion | flops 1879048192 | bytes 8388608 | tf_op jit(solution)/shard_map/dot_general | solution.py:232
  91.2 10.1 %convolution_convert_fusion = bf16[512,3584]{1,0:T(8,128)(2,1)} fusion(bf16[1,512,3584]{2,1,0:T(8,128)(2,1)} %param.19, bf16[512,3584]{1,0:T(8,128)(2,1)} %bitcast.48, bf16[1,3584,512]{2,1,0:T(8,128)(2,1)} %param.18, f32[512,512]{1,0:T(8,128)S(1)} %fusion.4), kind=kOutput, calls=%fused_computation.1 | convolution fusion | flops 3761504256 | bytes 15728640 | tf_op jit(solution)/shard_map/dot_general | solution.py:235
  101.3 4.6 %all-to-all-start.1 = ((bf16[16,32,3584]{2,1,0:T(8,128)(2,1)}), bf16[16,32,3584]{2,1,0:T(8,128)(2,1)}, u32[]{:S(2)}, u32[]{:S(2)}) async-start(bf16[16,32,3584]{2,1,0:T(8,128)(2,1)} %bitcast.46), calls=%async_computation.1 | async-start | bytes 7340032 | tf_op jit(solution)/shard_map/all_to_all | solution.py:286
  106.1 0.1 copy.44
  107.0 0.4 fusion.15
  107.3 0.2 fusion.36
  107.6 1.5 select_reduce_fusion
  109.1 1.2 fusion.18
  110.3 48.6 %all-to-all-done.1 = bf16[16,32,3584]{2,1,0:T(8,128)(2,1)} async-done(((bf16[16,32,3584]{2,1,0:T(8,128)(2,1)}), bf16[16,32,3584]{2,1,0:T(8,128)(2,1)}, u32[]{:S(2)}, u32[]{:S(2)}) %all-to-all-start.1) | async-done | bytes 3670048 | tf_op jit(solution)/shard_map/all_to_all | solution.py:286
  158.9 2.8 %bitcast_reduce_fusion = bf16[8,32,3584]{2,1,0:T(8,128)(2,1)S(1)} fusion(bf16[16,32,3584]{2,1,0:T(8,128)(2,1)} %all-to-all-done.1), kind=kLoop, calls=%fused_computation.4 | loop fusion | flops 917504 | bytes 5505024 | tf_op jit(solution)/shard_map/reduce_sum | solution.py:296
  161.7 2.9 %convolution_convert_fusion.1 = bf16[256,3584]{1,0:T(8,128)(2,1)} fusion(f32[256,256]{1,0:T(8,128)S(1)} %select_reduce_fusion, bf16[256,3584]{1,0:T(8,128)(2,1)S(1)} %bitcast.45), kind=kOutput, calls=%fused_computation.2 | convolution fusion | flops 2819489792 | bytes 3932160 | tf_op jit(solution)/shard_map/dot_general | solution.py:300
  164.6 24.1 %shard_map.114 = bf16[16,3584]{1,0:T(8,128)(2,1)} custom-call(bf16[16,16,3584]{2,1,0:T(8,128)(2,1)} %bitcast.44), custom_call_target="tpu_custom_call" | custom-call | tf_op jit(solution)/shard_map/pallas_call | solution.py:213
  188.7 1.6 copy.51
  (22 shorter events, 0.5 us)
Async XLA Ops:
  0.6 106.3 %copy-start = (bf16[4,64,576]{2,1,0:T(8,128)(2,1)S(1)}, bf16[4,64,576]{2,1,0:T(8,128)(2,1)}, u32[]{:S(2)}) copy-start(bf16[4,64,576]{2,1,0:T(8,128)(2,1)} %param.10) | copy-start | bytes 884740
  35.5 53.7 %copy-start.4 = (bf16[1,3584,512]{2,1,0:T(8,128)(2,1)S(1)}, bf16[1,3584,512]{2,1,0:T(8,128)(2,1)}, u32[]{:S(2)}) copy-start(bf16[1,3584,512]{2,1,0:T(8,128)(2,1)} %param.17) | copy-start | bytes 11010052
  87.3 1.8 copy-start.1
  101.3 5.7 %copy-start.2 = (bf16[4,256,576]{1,2,0:T(8,128)(2,1)S(1)}, bf16[4,256,576]{1,2,0:T(8,128)(2,1)}, u32[]{:S(2)}) copy-start(bf16[4,256,576]{1,2,0:T(8,128)(2,1)} %param.11) | copy-start | bytes 3538948
  101.3 5.7 %copy-start.3 = (s32[4]{0:T(128)S(1)}, s32[4]{0:T(128)}, u32[]{:S(2)}) copy-start(s32[4]{0:T(128)} %param.12) | copy-start | bytes 52
  101.3 57.6 %all-to-all-start.1 = ((bf16[16,32,3584]{2,1,0:T(8,128)(2,1)}), bf16[16,32,3584]{2,1,0:T(8,128)(2,1)}, u32[]{:S(2)}, u32[]{:S(2)}) async-start(bf16[16,32,3584]{2,1,0:T(8,128)(2,1)} %bitcast.46), calls=%async_computation.1 | async-start | bytes 7340032 | tf_op jit(solution)/shard_map/all_to_all | solution.py:286

commit v9 on v8

--- a/solution.py
+++ b/solution.py
@@ -231,7 +231,7 @@
 def expert_partial(flat_rows, w_gate, w_up, w_down):
     gate_part = jnp.dot(flat_rows, w_gate[0], preferred_element_type=jnp.float32)
     up_part = jnp.dot(flat_rows, w_up[0], preferred_element_type=jnp.float32)
-    hidden = (jax.nn.silu(gate_part) * up_part).astype(jnp.bfloat16)
+    hidden = lax.optimization_barrier((jax.nn.silu(gate_part) * up_part).astype(jnp.bfloat16))
     return jnp.dot(hidden, w_down[0], preferred_element_type=jnp.float32)
 
 

time: 191 us -> 185 us (0.969)
  matrix products: 18.8 us -> 14.8 us
    dot_general x1, matrix products: 10.1 us -> 3.91 us  [expert_partial(): return jnp.dot(hidden, w_down[0], preferred_element_type=jnp.float32)]
    dot_general x0 -> x1, matrix products: none -> 2.14 us  [expert_partial(): up_part = jnp.dot(flat_rows, w_up[0], preferred_element_type=jnp.float32)]
    unnamed x15 -> x17, local copies, waits for them, and re-layouts: 4.37 us -> 2.54 us
where the time goes in v9:
time: 185 us; the launch traced here: 184 us
  blocking collectives  51.8 us (28%)
  Pallas kernels  49.1 us (27%)
  waiting for transfers between devices  48.6 us (26%)
  matrix products  14.8 us (8%)
  other arithmetic  9.15 us (5%)
  local copies, waits for them, and re-layouts  4.81 us (3%)
  starting transfers between devices  4.63 us (3%)
    all_to_all x1, blocking collectives, per_device(): lax.all_to_all(doubled, 'ep', split_axis=0, concat_axis=0, tiled=True)  51.8 us
    all_to_all x1, waiting for transfers between devices, per_device(): lax.all_to_all(partials.reshape(peer_count, expert_slots, feature), 'ep',...  48.6 us
    pallas_call x1, Pallas kernels, ring_gather(): pl.pallas_call(functools.partial(gather_kernel, chips, widths), out_shape...  25 us
    pallas_call x1, Pallas kernels, ring_scatter(): pl.pallas_call(functools.partial(scatter_kernel, chips), out_shape=jax.Sh...  24.1 us
    all_to_all x1, starting transfers between devices, per_device(): lax.all_to_all(partials.reshape(peer_count, expert_slots, feature), 'ep',...  4.63 us
    dot_general x1, matrix products, expert_partial(): return jnp.dot(hidden, w_down[0], preferred_element_type=jnp.float32)  3.91 us
  transfers between devices with their start and end apart: 1, of which 1 were waited for; matrix products, arithmetic and copies ran while one was open for 2% of the time, Pallas kernels for 0%

profile of v9, /device:TPU:1, one launch (start us, length us, event | category | flops | bytes accessed | tf_op | source)
XLA Modules:
  0.0 184.5 jit_solution(8530470964048756886)
XLA Ops:
  0.6 0.7 convert_element_type.54
  1.4 0.8 copy.35
  2.1 0.1 copy.37
  2.2 0.7 convert_element_type.53
  2.9 0.1 copy.36
  3.0 0.1 fusion.27
  3.1 1.6 pad_maximum_fusion.x_ref
  4.7 25.0 %shard_map.113 = bf16[16,16,3712]{2,1,0:T(8,128)(2,1)} custom-call(bf16[16,3712]{1,0:T(8,128)(2,1)} %pad_maximum_fusion.x_ref), custom_call_target="tpu_custom_call" | custom-call | tf_op jit(solution)/shard_map/pallas_call | solution.py:121
  29.7 1.1 fusion.31
  31.0 0.1 copy.39
  31.1 0.7 fusion.33
  31.8 0.1 copy.40
  31.9 0.1 reduce_window_sum.14
  32.1 0.1 copy.41
  32.2 0.7 fusion.6
  32.9 2.2 %convolution_convert_fusion.2 = bf16[256,3584]{1,0:T(8,128)(2,1)S(1)} fusion(pred[256,256]{1,0:T(8,128)(4,1)S(1)} %fusion.6, bf16[256,3712]{1,0:T(8,128)(2,1)} %bitcast.41), kind=kOutput, calls=%fused_computation.3 | convolution fusion | flops 470679552 | bytes 3735552 | tf_op jit(solution)/shard_map/dot_general | solution.py:278
  35.1 0.4 broadcast_in_dim.46
  35.5 51.8 %all_to_all.10 = bf16[16,32,3584]{2,1,0:T(8,128)(2,1)S(1)} all-to-all(bf16[16,32,3584]{2,1,0:T(8,128)(2,1)S(1)} %bitcast.39), channel_id=1, replica_groups=mesh['grp'=16,'ep'=16] {'ep'}, dimensions={0} | all-to-all | bytes 7340032 | tf_op jit(solution)/shard_map/all_to_all | solution.py:282
  87.4 2.0 %fusion.4 = f32[512,512]{1,0:T(8,128)S(1)} fusion(bf16[512,3584]{1,0:T(8,128)(2,1)S(1)} %bitcast.46, bf16[1,3584,512]{2,1,0:T(8,128)(2,1)S(1)} %copy-done.3), kind=kOutput, calls=%fused_computation.8 | convolution fusion | flops 1879048192 | bytes 8388608 | tf_op jit(solution)/shard_map/dot_general | solution.py:232
  89.4 2.1 %fusion.11 = bf16[512,512]{1,0:T(8,128)(2,1)S(1)} fusion(bf16[512,3584]{1,0:T(8,128)(2,1)S(1)} %bitcast.47, bf16[1,3584,512]{2,1,0:T(8,128)(2,1)S(1)} %copy-done.4, f32[512,512]{1,0:T(8,128)S(1)} %fusion.4), kind=kOutput, calls=%fused_computation.15 | convolution fusion | flops 1880621056 | bytes 8912896 | tf_op jit(solution)/shard_map/dot_general | solution.py:233
  91.6 3.9 %convolution_convert_fusion = bf16[512,3584]{1,0:T(8,128)(2,1)} fusion(bf16[512,512]{1,0:T(8,128)(2,1)S(1)} %fusion.11, bf16[1,512,3584]{2,1,0:T(8,128)(2,1)S(1)} %copy-done.5), kind=kOutput, calls=%fused_computation.1 | convolution fusion | flops 1880883200 | bytes 7864320 | tf_op jit(solution)/shard_map/dot_general | solution.py:235
  95.5 4.6 %all-to-all-start.1 = ((bf16[16,32,3584]{2,1,0:T(8,128)(2,1)}), bf16[16,32,3584]{2,1,0:T(8,128)(2,1)}, u32[]{:S(2)}, u32[]{:S(2)}) async-start(bf16[16,32,3584]{2,1,0:T(8,128)(2,1)} %bitcast.45), calls=%async_computation.1 | async-start | bytes 7340032 | tf_op jit(solution)/shard_map/all_to_all | solution.py:286
  100.3 0.1 copy.44
  101.2 0.3 fusion.15
  101.5 0.2 fusion.32
  101.8 1.5 select_reduce_fusion
  103.2 1.2 fusion.18
  104.5 48.6 %all-to-all-done.1 = bf16[16,32,3584]{2,1,0:T(8,128)(2,1)} async-done(((bf16[16,32,3584]{2,1,0:T(8,128)(2,1)}), bf16[16,32,3584]{2,1,0:T(8,128)(2,1)}, u32[]{:S(2)}, u32[]{:S(2)}) %all-to-all-start.1) | async-done | bytes 3670048 | tf_op jit(solution)/shard_map/all_to_all | solution.py:286
  153.1 2.8 %bitcast_reduce_fusion = bf16[8,32,3584]{2,1,0:T(8,128)(2,1)S(1)} fusion(bf16[16,32,3584]{2,1,0:T(8,128)(2,1)} %all-to-all-done.1), kind=kLoop, calls=%fused_computation.4 | loop fusion | flops 917504 | bytes 5505024 | tf_op jit(solution)/shard_map/reduce_sum | solution.py:296
  155.9 2.9 %convolution_convert_fusion.1 = bf16[256,3584]{1,0:T(8,128)(2,1)} fusion(f32[256,256]{1,0:T(8,128)S(1)} %select_reduce_fusion, bf16[256,3584]{1,0:T(8,128)(2,1)S(1)} %bitcast.44), kind=kOutput, calls=%fused_computation.2 | convolution fusion | flops 2819489792 | bytes 3932160 | tf_op jit(solution)/shard_map/dot_general | solution.py:300
  158.8 24.1 %shard_map.114 = bf16[16,3584]{1,0:T(8,128)(2,1)} custom-call(bf16[16,16,3584]{2,1,0:T(8,128)(2,1)} %bitcast.43), custom_call_target="tpu_custom_call" | custom-call | tf_op jit(solution)/shard_map/pallas_call | solution.py:213
  182.9 1.6 copy.51
  (25 shorter events, 0.5 us)
Async XLA Ops:
  0.6 100.5 %copy-start = (bf16[4,64,576]{2,1,0:T(8,128)(2,1)S(1)}, bf16[4,64,576]{2,1,0:T(8,128)(2,1)}, u32[]{:S(2)}) copy-start(bf16[4,64,576]{2,1,0:T(8,128)(2,1)} %param.10) | copy-start | bytes 884740
  35.5 51.8 %copy-start.3 = (bf16[1,3584,512]{2,1,0:T(8,128)(2,1)S(1)}, bf16[1,3584,512]{2,1,0:T(8,128)(2,1)}, u32[]{:S(2)}) copy-start(bf16[1,3584,512]{2,1,0:T(8,128)(2,1)} %param.17) | copy-start | bytes 11010052
  87.3 2.1 %copy-start.4 = (bf16[1,3584,512]{2,1,0:T(8,128)(2,1)S(1)}, bf16[1,3584,512]{2,1,0:T(8,128)(2,1)}, u32[]{:S(2)}) copy-start(bf16[1,3584,512]{2,1,0:T(8,128)(2,1)} %param.18) | copy-start | bytes 11010052
  89.4 2.2 %copy-start.5 = (bf16[1,512,3584]{2,1,0:T(8,128)(2,1)S(1)}, bf16[1,512,3584]{2,1,0:T(8,128)(2,1)}, u32[]{:S(2)}) copy-start(bf16[1,512,3584]{2,1,0:T(8,128)(2,1)} %param.19) | copy-start | bytes 11010052
  95.5 5.6 %copy-start.1 = (bf16[4,256,576]{1,2,0:T(8,128)(2,1)S(1)}, bf16[4,256,576]{1,2,0:T(8,128)(2,1)}, u32[]{:S(2)}) copy-start(bf16[4,256,576]{1,2,0:T(8,128)(2,1)} %param.11) | copy-start | bytes 3538948
  95.5 5.7 %copy-start.2 = (s32[4]{0:T(128)S(1)}, s32[4]{0:T(128)}, u32[]{:S(2)}) copy-start(s32[4]{0:T(128)} %param.12) | copy-start | bytes 52
  95.5 57.6 %all-to-all-start.1 = ((bf16[16,32,3584]{2,1,0:T(8,128)(2,1)}), bf16[16,32,3584]{2,1,0:T(8,128)(2,1)}, u32[]{:S(2)}, u32[]{:S(2)}) async-start(bf16[16,32,3584]{2,1,0:T(8,128)(2,1)} %bitcast.45), calls=%async_computation.1 | async-start | bytes 7340032 | tf_op jit(solution)/shard_map/all_to_all | solution.py:286

commit v10 on v9

--- a/solution.py
+++ b/solution.py
@@ -132,7 +132,7 @@
 
 
 def scatter_kernel(
-    chips, parts_ref, out_ref, early, forward_in, backward_in, forward_out, backward_out,
+    chips, widths, parts_ref, out_ref, early, forward_in, backward_in, forward_out, backward_out,
     send_sem, recv_sem,
 ):
     group = lax.axis_index("grp")
@@ -144,6 +144,11 @@
     partner = z * 2 + (1 - core)
     forward_hops = chips // 2
     backward_hops = (chips - 1) // 2
+    starts = [sum(widths[:piece]) for piece in range(len(widths))]
+    pieces = range(len(widths))
+
+    def cols(piece):
+        return pl.ds(starts[piece], widths[piece])
 
     barrier = pltpu.get_barrier_semaphore()
     for peer in (left, right, partner):
@@ -152,54 +157,68 @@
 
     started = []
 
-    def copy_of(src, dst, peer, slot, number):
+    def copy_of(src, dst, peer, slot, piece, number):
         return pltpu.make_async_remote_copy(
             src_ref=src,
             dst_ref=dst,
             send_sem=send_sem.at[number],
-            recv_sem=recv_sem.at[slot],
+            recv_sem=recv_sem.at[slot, piece],
             device_id=(peer, peer_col),
             device_id_type=MESH,
         )
 
-    def send(src, dst, peer, slot):
-        copy = copy_of(src, dst, peer, slot, len(started))
+    def send(src, dst, peer, slot, piece):
+        copy = copy_of(src, dst, peer, slot, piece, len(started))
         copy.start()
         started.append(copy)
 
-    def arrive(dst, peer, slot):
-        copy_of(dst, dst, peer, slot, 0).wait_recv()
+    def arrive(dst, peer, slot, piece):
+        copy_of(dst, dst, peer, slot, piece, 0).wait_recv()
 
     for other in range(chips):
-        send(parts_ref.at[other * 2 + (1 - core)], early.at[other], partner, other)
+        for piece in pieces:
+            send(
+                parts_ref.at[other * 2 + (1 - core), :, cols(piece)],
+                early.at[other, :, cols(piece)],
+                partner,
+                other,
+                piece,
+            )
     for other in range(chips):
-        arrive(early.at[other], partner, other)
-
-    def chip_part(chip):
-        return parts_ref[chip * 2 + core].astype(jnp.float32) + early[chip].astype(jnp.float32)
+        for piece in pieces:
+            arrive(early.at[other, :, cols(piece)], partner, other, piece)
+
+    def chip_part(chip, piece):
+        return parts_ref[chip * 2 + core, :, cols(piece)].astype(jnp.float32) + early[
+            chip, :, cols(piece)
+        ].astype(jnp.float32)
+
+    def hop(step, chip, inbox, outbox, source, dest, first_slot, piece):
+        value = chip_part(chip, piece)
+        if step > 0:
+            arrive(inbox.at[step - 1, :, cols(piece)], source, first_slot + step - 1, piece)
+            value = value + inbox[step - 1, :, cols(piece)].astype(jnp.float32)
+        outbox[step, :, cols(piece)] = value.astype(outbox.dtype)
+        send(outbox.at[step, :, cols(piece)], inbox.at[step, :, cols(piece)], dest, first_slot + step, piece)
 
     for step in range(forward_hops):
         chip = lax.rem(z + forward_hops - step, chips)
-        value = chip_part(chip)
-        if step > 0:
-            arrive(forward_in.at[step - 1], left, chips + step - 1)
-            value = value + forward_in[step - 1].astype(jnp.float32)
-        forward_out[step] = value.astype(forward_out.dtype)
-        send(forward_out.at[step], forward_in.at[step], right, chips + step)
+        for piece in pieces:
+            hop(step, chip, forward_in, forward_out, left, right, chips, piece)
         if step < backward_hops:
             chip = lax.rem(z + chips - backward_hops + step, chips)
-            value = chip_part(chip)
-            if step > 0:
-                arrive(backward_in.at[step - 1], right, chips + forward_hops + step - 1)
-                value = value + backward_in[step - 1].astype(jnp.float32)
-            backward_out[step] = value.astype(backward_out.dtype)
-            send(backward_out.at[step], backward_in.at[step], left, chips + forward_hops + step)
-    arrive(forward_in.at[forward_hops - 1], left, chips + forward_hops - 1)
-    total = chip_part(z) + forward_in[forward_hops - 1].astype(jnp.float32)
-    if backward_hops > 0:
-        arrive(backward_in.at[backward_hops - 1], right, chips + forward_hops + backward_hops - 1)
-        total = total + backward_in[backward_hops - 1].astype(jnp.float32)
-    out_ref[...] = total.astype(out_ref.dtype)
+            for piece in pieces:
+                hop(step, chip, backward_in, backward_out, right, left, chips + forward_hops, piece)
+    for piece in pieces:
+        arrive(forward_in.at[forward_hops - 1, :, cols(piece)], left, chips + forward_hops - 1, piece)
+        total = chip_part(z, piece) + forward_in[forward_hops - 1, :, cols(piece)].astype(
+            jnp.float32
+        )
+        if backward_hops > 0:
+            last = chips + forward_hops + backward_hops - 1
+            arrive(backward_in.at[backward_hops - 1, :, cols(piece)], right, last, piece)
+            total = total + backward_in[backward_hops - 1, :, cols(piece)].astype(jnp.float32)
+        out_ref[:, cols(piece)] = total.astype(out_ref.dtype)
     for copy in started:
         copy.wait_send()
 
@@ -209,9 +228,12 @@
     forward_hops = chips // 2
     backward_hops = (chips - 1) // 2
     block = parts.shape[1:]
+    lanes = block[1] // 128
+    widths = (lanes // 2 * 128, (lanes - lanes // 2) * 128)
     slots = chips + forward_hops + backward_hops
+    sends = (chips + forward_hops + backward_hops) * len(widths)
     return pl.pallas_call(
-        functools.partial(scatter_kernel, chips),
+        functools.partial(scatter_kernel, chips, widths),
         out_shape=jax.ShapeDtypeStruct(block, parts.dtype),
         in_specs=[pl.BlockSpec(memory_space=pltpu.VMEM)],
         out_specs=pl.BlockSpec(memory_space=pltpu.VMEM),
@@ -221,8 +243,8 @@
             pltpu.VMEM((max(backward_hops, 1),) + block, parts.dtype),
             pltpu.VMEM((forward_hops,) + block, parts.dtype),
             pltpu.VMEM((max(backward_hops, 1),) + block, parts.dtype),
-            pltpu.SemaphoreType.DMA((slots,)),
-            pltpu.SemaphoreType.DMA((slots,)),
+            pltpu.SemaphoreType.DMA((sends,)),
+            pltpu.SemaphoreType.DMA((slots, len(widths))),
         ],
         compiler_params=pltpu.CompilerParams(collective_id=1, has_side_effects=True),
     )(parts)
@@ -297,11 +319,10 @@
         .astype(jnp.bfloat16)
         .reshape(slot_count, feature)
     )
-    column_mixed = jnp.dot(
-        combine,
-        expert_out.astype(jnp.float32),
-        precision=lax.Precision.HIGHEST,
-        preferred_element_type=jnp.float32,
+    weight_high = combine.astype(jnp.bfloat16)
+    weight_low = (combine - weight_high.astype(jnp.float32)).astype(jnp.bfloat16)
+    column_mixed = jnp.dot(weight_high, expert_out, preferred_element_type=jnp.float32) + jnp.dot(
+        weight_low, expert_out, preferred_element_type=jnp.float32
     )
     mixed = ring_scatter(
         column_mixed.astype(jnp.bfloat16).reshape(group_count, row_count, feature), group_count

time: 185 us -> 184 us (level)
  no operation moved by 1% of the time
where the time goes in v10:
time: 184 us
  blocking collectives  51.8 us (28%)
  Pallas kernels  48.8 us (27%)
  waiting for transfers between devices  48.6 us (26%)
  matrix products  14.5 us (8%)
  other arithmetic  9.15 us (5%)
  local copies, waits for them, and re-layouts  4.81 us (3%)
  starting transfers between devices  4.63 us (3%)
    all_to_all x1, blocking collectives, per_device(): lax.all_to_all(doubled, 'ep', split_axis=0, concat_axis=0, tiled=True)  51.8 us
    all_to_all x1, waiting for transfers between devices, per_device(): lax.all_to_all(partials.reshape(peer_count, expert_slots, feature), 'ep',...  48.6 us
    pallas_call x1, Pallas kernels, ring_gather(): pl.pallas_call(functools.partial(gather_kernel, chips, widths), out_shape...  25 us
    pallas_call x1, Pallas kernels, ring_scatter(): pl.pallas_call(functools.partial(scatter_kernel, chips, widths), out_shap...  23.7 us
    all_to_all x1, starting transfers between devices, per_device(): lax.all_to_all(partials.reshape(peer_count, expert_slots, feature), 'ep',...  4.63 us
    dot_general x1, matrix products, expert_partial(): return jnp.dot(hidden, w_down[0], preferred_element_type=jnp.float32)  3.91 us
  transfers between devices with their start and end apart: 1, of which 1 were waited for; matrix products, arithmetic and copies ran while one was open for 2% of the time, Pallas kernels for 0%

profile of v10, /device:TPU:1, one launch (start us, length us, event | category | flops | bytes accessed | tf_op | source)
XLA Modules:
  0.0 183.8 jit_solution(7724701223729648509)
XLA Ops:
  0.6 0.7 convert_element_type.62
  1.4 0.8 copy.35
  2.1 0.1 copy.37
  2.2 0.7 convert_element_type.61
  2.9 0.1 copy.36
  3.1 1.6 pad_maximum_fusion.x_ref
  4.7 25.0 %shard_map.113 = bf16[16,16,3712]{2,1,0:T(8,128)(2,1)} custom-call(bf16[16,3712]{1,0:T(8,128)(2,1)} %pad_maximum_fusion.x_ref), custom_call_target="tpu_custom_call" | custom-call | tf_op jit(solution)/shard_map/pallas_call | solution.py:121
  29.7 1.1 fusion.35
  31.0 0.1 copy.39
  31.1 0.7 fusion.37
  31.8 0.1 copy.40
  31.9 0.1 reduce_window_sum.14
  32.1 0.1 copy.41
  32.2 0.7 fusion.7
  32.9 2.2 %convolution_convert_fusion.1 = bf16[256,3584]{1,0:T(8,128)(2,1)S(1)} fusion(pred[256,256]{1,0:T(8,128)(4,1)S(1)} %fusion.7, bf16[256,3712]{1,0:T(8,128)(2,1)} %bitcast.43), kind=kOutput, calls=%fused_computation.4 | convolution fusion | flops 470679552 | bytes 3735552 | tf_op jit(solution)/shard_map/dot_general | solution.py:300
  35.1 0.4 broadcast_in_dim.46
  35.5 51.8 %all_to_all.10 = bf16[16,32,3584]{2,1,0:T(8,128)(2,1)S(1)} all-to-all(bf16[16,32,3584]{2,1,0:T(8,128)(2,1)S(1)} %bitcast.41), channel_id=1, replica_groups=mesh['grp'=16,'ep'=16] {'ep'}, dimensions={0} | all-to-all | bytes 7340032 | tf_op jit(solution)/shard_map/all_to_all | solution.py:304
  87.4 2.0 %fusion.5 = f32[512,512]{1,0:T(8,128)S(1)} fusion(bf16[512,3584]{1,0:T(8,128)(2,1)S(1)} %bitcast.47, bf16[1,3584,512]{2,1,0:T(8,128)(2,1)S(1)} %copy-done.3), kind=kOutput, calls=%fused_computation.9 | convolution fusion | flops 1879048192 | bytes 8388608 | tf_op jit(solution)/shard_map/dot_general | solution.py:254
  89.4 2.1 %fusion.12 = bf16[512,512]{1,0:T(8,128)(2,1)S(1)} fusion(bf16[512,3584]{1,0:T(8,128)(2,1)S(1)} %bitcast.48, bf16[1,3584,512]{2,1,0:T(8,128)(2,1)S(1)} %copy-done.4, f32[512,512]{1,0:T(8,128)S(1)} %fusion.5), kind=kOutput, calls=%fused_computation.16 | convolution fusion | flops 1880621056 | bytes 8912896 | tf_op jit(solution)/shard_map/dot_general | solution.py:255
  91.6 3.9 %convolution_convert_fusion = bf16[512,3584]{1,0:T(8,128)(2,1)} fusion(bf16[512,512]{1,0:T(8,128)(2,1)S(1)} %fusion.12, bf16[1,512,3584]{2,1,0:T(8,128)(2,1)S(1)} %copy-done.5), kind=kOutput, calls=%fused_computation.1 | convolution fusion | flops 1880883200 | bytes 7864320 | tf_op jit(solution)/shard_map/dot_general | solution.py:257
  95.5 4.6 %all-to-all-start.1 = ((bf16[16,32,3584]{2,1,0:T(8,128)(2,1)}), bf16[16,32,3584]{2,1,0:T(8,128)(2,1)}, u32[]{:S(2)}, u32[]{:S(2)}) async-start(bf16[16,32,3584]{2,1,0:T(8,128)(2,1)} %bitcast.46), calls=%async_computation.1 | async-start | bytes 7340032 | tf_op jit(solution)/shard_map/all_to_all | solution.py:308
  100.3 0.1 copy.44
  101.2 0.3 fusion.16
  101.5 0.2 fusion.36
  101.8 1.5 select_reduce_fusion
  103.2 1.2 fusion.19
  104.5 48.6 %all-to-all-done.1 = bf16[16,32,3584]{2,1,0:T(8,128)(2,1)} async-done(((bf16[16,32,3584]{2,1,0:T(8,128)(2,1)}), bf16[16,32,3584]{2,1,0:T(8,128)(2,1)}, u32[]{:S(2)}, u32[]{:S(2)}) %all-to-all-start.1) | async-done | bytes 3670048 | tf_op jit(solution)/shard_map/all_to_all | solution.py:308
  153.1 2.8 %bitcast_reduce_fusion = bf16[8,32,3584]{2,1,0:T(8,128)(2,1)S(1)} fusion(bf16[16,32,3584]{2,1,0:T(8,128)(2,1)} %all-to-all-done.1), kind=kLoop, calls=%fused_computation.5 | loop fusion | flops 917504 | bytes 5505024 | tf_op jit(solution)/shard_map/reduce_sum | solution.py:318
  155.9 0.7 fusion.25
  156.5 1.9 %fusion.1 = bf16[256,3584]{1,0:T(8,128)(2,1)} fusion(f32[256,3584]{1,0:T(8,128)S(1)} %fusion.25, bf16[256,3584]{1,0:T(8,128)(2,1)S(1)} %bitcast.40, f32[256,256]{1,0:T(8,128)S(1)} %select_reduce_fusion), kind=kOutput, calls=%fused_computation.3 | convolution fusion | flops 471859200 | bytes 7602176 | tf_op jit(solution)/shard_map/dot_general | solution.py:324
  158.5 23.7 %shard_map.114 = bf16[16,3584]{1,0:T(8,128)(2,1)} custom-call(bf16[16,16,3584]{2,1,0:T(8,128)(2,1)} %bitcast.45), custom_call_target="tpu_custom_call" | custom-call | tf_op jit(solution)/shard_map/pallas_call | solution.py:235
  182.2 1.6 copy.51
  (26 shorter events, 0.6 us)
Async XLA Ops:
  0.6 100.5 %copy-start = (bf16[4,64,576]{2,1,0:T(8,128)(2,1)S(1)}, bf16[4,64,576]{2,1,0:T(8,128)(2,1)}, u32[]{:S(2)}) copy-start(bf16[4,64,576]{2,1,0:T(8,128)(2,1)} %param.10) | copy-start | bytes 884740
  35.5 51.8 %copy-start.3 = (bf16[1,3584,512]{2,1,0:T(8,128)(2,1)S(1)}, bf16[1,3584,512]{2,1,0:T(8,128)(2,1)}, u32[]{:S(2)}) copy-start(bf16[1,3584,512]{2,1,0:T(8,128)(2,1)} %param.17) | copy-start | bytes 11010052
  87.3 2.1 %copy-start.4 = (bf16[1,3584,512]{2,1,0:T(8,128)(2,1)S(1)}, bf16[1,3584,512]{2,1,0:T(8,128)(2,1)}, u32[]{:S(2)}) copy-start(bf16[1,3584,512]{2,1,0:T(8,128)(2,1)} %param.18) | copy-start | bytes 11010052
  89.4 2.2 %copy-start.5 = (bf16[1,512,3584]{2,1,0:T(8,128)(2,1)S(1)}, bf16[1,512,3584]{2,1,0:T(8,128)(2,1)}, u32[]{:S(2)}) copy-start(bf16[1,512,3584]{2,1,0:T(8,128)(2,1)} %param.19) | copy-start | bytes 11010052
  95.5 5.6 %copy-start.1 = (bf16[4,256,576]{1,2,0:T(8,128)(2,1)S(1)}, bf16[4,256,576]{1,2,0:T(8,128)(2,1)}, u32[]{:S(2)}) copy-start(bf16[4,256,576]{1,2,0:T(8,128)(2,1)} %param.11) | copy-start | bytes 3538948
  95.5 5.7 %copy-start.2 = (s32[4]{0:T(128)S(1)}, s32[4]{0:T(128)}, u32[]{:S(2)}) copy-start(s32[4]{0:T(128)} %param.12) | copy-start | bytes 52
  95.5 57.6 %all-to-all-start.1 = ((bf16[16,32,3584]{2,1,0:T(8,128)(2,1)}), bf16[16,32,3584]{2,1,0:T(8,128)(2,1)}, u32[]{:S(2)}, u32[]{:S(2)}) async-start(bf16[16,32,3584]{2,1,0:T(8,128)(2,1)} %bitcast.46), calls=%async_computation.1 | async-start | bytes 7340032 | tf_op jit(solution)/shard_map/all_to_all | solution.py:308

commit v11 on v10

--- a/solution.py
+++ b/solution.py
@@ -8,6 +8,7 @@
 from jax.sharding import PartitionSpec as P
 
 MESH = pl.DeviceIdType.MESH
+CHUNKS = 4
 TOPK = 8
 LAT = 512
 CAP = 2
@@ -117,7 +118,9 @@
 def ring_gather(block, group_count):
     chips = group_count // 2
     lanes = block.shape[1] // 128
-    widths = (lanes // 2 * 128, (lanes - lanes // 2) * 128)
+    widths = tuple(
+        (lanes * (piece + 1) // CHUNKS - lanes * piece // CHUNKS) * 128 for piece in range(CHUNKS)
+    )
     return pl.pallas_call(
         functools.partial(gather_kernel, chips, widths),
         out_shape=jax.ShapeDtypeStruct((group_count,) + block.shape, block.dtype),
@@ -229,7 +232,9 @@
     backward_hops = (chips - 1) // 2
     block = parts.shape[1:]
     lanes = block[1] // 128
-    widths = (lanes // 2 * 128, (lanes - lanes // 2) * 128)
+    widths = tuple(
+        (lanes * (piece + 1) // CHUNKS - lanes * piece // CHUNKS) * 128 for piece in range(CHUNKS)
+    )
     slots = chips + forward_hops + backward_hops
     sends = (chips + forward_hops + backward_hops) * len(widths)
     return pl.pallas_call(

time: 184 us -> 184 us (level)
  no operation moved by 1% of the time
where the time goes in v11:
time: 184 us
  blocking collectives  51.8 us (28%)
  waiting for transfers between devices  48.7 us (26%)
  Pallas kernels  48.6 us (26%)
  matrix products  14.5 us (8%)
  other arithmetic  9.15 us (5%)
  local copies, waits for them, and re-layouts  4.81 us (3%)
  starting transfers between devices  4.63 us (3%)
    all_to_all x1, blocking collectives, per_device(): lax.all_to_all(doubled, 'ep', split_axis=0, concat_axis=0, tiled=True)  51.8 us
    all_to_all x1, waiting for transfers between devices, per_device(): lax.all_to_all(partials.reshape(peer_count, expert_slots, feature), 'ep',...  48.7 us
    pallas_call x1, Pallas kernels, ring_gather(): pl.pallas_call(functools.partial(gather_kernel, chips, widths), out_shape...  26 us
    pallas_call x1, Pallas kernels, ring_scatter(): pl.pallas_call(functools.partial(scatter_kernel, chips, widths), out_shap...  22.7 us
    all_to_all x1, starting transfers between devices, per_device(): lax.all_to_all(partials.reshape(peer_count, expert_slots, feature), 'ep',...  4.63 us
    dot_general x1, matrix products, expert_partial(): return jnp.dot(hidden, w_down[0], preferred_element_type=jnp.float32)  3.91 us
  transfers between devices with their start and end apart: 1, of which 1 were waited for; matrix products, arithmetic and copies ran while one was open for 2% of the time, Pallas kernels for 0%

profile of v11, /device:TPU:1, one launch (start us, length us, event | category | flops | bytes accessed | tf_op | source)
XLA Modules:
  0.0 183.7 jit_solution(16977371137638478662)
XLA Ops:
  0.6 0.7 convert_element_type.62
  1.4 0.8 copy.35
  2.1 0.1 copy.37
  2.2 0.7 convert_element_type.61
  2.9 0.1 copy.36
  3.1 1.6 pad_maximum_fusion.x_ref
  4.7 26.0 %shard_map.113 = bf16[16,16,3712]{2,1,0:T(8,128)(2,1)} custom-call(bf16[16,3712]{1,0:T(8,128)(2,1)} %pad_maximum_fusion.x_ref), custom_call_target="tpu_custom_call" | custom-call | tf_op jit(solution)/shard_map/pallas_call | solution.py:124
  30.6 1.1 fusion.35
  31.9 0.1 copy.39
  32.0 0.7 fusion.37
  32.7 0.1 copy.40
  32.8 0.1 reduce_window_sum.14
  33.0 0.1 copy.41
  33.1 0.7 fusion.7
  33.8 2.2 %convolution_convert_fusion.1 = bf16[256,3584]{1,0:T(8,128)(2,1)S(1)} fusion(pred[256,256]{1,0:T(8,128)(4,1)S(1)} %fusion.7, bf16[256,3712]{1,0:T(8,128)(2,1)} %bitcast.43), kind=kOutput, calls=%fused_computation.4 | convolution fusion | flops 470679552 | bytes 3735552 | tf_op jit(solution)/shard_map/dot_general | solution.py:305
  36.0 0.4 broadcast_in_dim.46
  36.4 51.8 %all_to_all.10 = bf16[16,32,3584]{2,1,0:T(8,128)(2,1)S(1)} all-to-all(bf16[16,32,3584]{2,1,0:T(8,128)(2,1)S(1)} %bitcast.41), channel_id=1, replica_groups=mesh['grp'=16,'ep'=16] {'ep'}, dimensions={0} | all-to-all | bytes 7340032 | tf_op jit(solution)/shard_map/all_to_all | solution.py:309
  88.3 2.1 %fusion.5 = f32[512,512]{1,0:T(8,128)S(1)} fusion(bf16[512,3584]{1,0:T(8,128)(2,1)S(1)} %bitcast.47, bf16[1,3584,512]{2,1,0:T(8,128)(2,1)S(1)} %copy-done.3), kind=kOutput, calls=%fused_computation.9 | convolution fusion | flops 1879048192 | bytes 8388608 | tf_op jit(solution)/shard_map/dot_general | solution.py:259
  90.3 2.1 %fusion.12 = bf16[512,512]{1,0:T(8,128)(2,1)S(1)} fusion(bf16[512,3584]{1,0:T(8,128)(2,1)S(1)} %bitcast.48, bf16[1,3584,512]{2,1,0:T(8,128)(2,1)S(1)} %copy-done.4, f32[512,512]{1,0:T(8,128)S(1)} %fusion.5), kind=kOutput, calls=%fused_computation.16 | convolution fusion | flops 1880621056 | bytes 8912896 | tf_op jit(solution)/shard_map/dot_general | solution.py:260
  92.5 3.9 %convolution_convert_fusion = bf16[512,3584]{1,0:T(8,128)(2,1)} fusion(bf16[512,512]{1,0:T(8,128)(2,1)S(1)} %fusion.12, bf16[1,512,3584]{2,1,0:T(8,128)(2,1)S(1)} %copy-done.5), kind=kOutput, calls=%fused_computation.1 | convolution fusion | flops 1880883200 | bytes 7864320 | tf_op jit(solution)/shard_map/dot_general | solution.py:262
  96.4 4.6 %all-to-all-start.1 = ((bf16[16,32,3584]{2,1,0:T(8,128)(2,1)}), bf16[16,32,3584]{2,1,0:T(8,128)(2,1)}, u32[]{:S(2)}, u32[]{:S(2)}) async-start(bf16[16,32,3584]{2,1,0:T(8,128)(2,1)} %bitcast.46), calls=%async_computation.1 | async-start | bytes 7340032 | tf_op jit(solution)/shard_map/all_to_all | solution.py:313
  101.3 0.1 copy.44
  102.1 0.3 fusion.16
  102.4 0.2 fusion.36
  102.7 1.5 select_reduce_fusion
  104.2 1.2 fusion.19
  105.4 48.7 %all-to-all-done.1 = bf16[16,32,3584]{2,1,0:T(8,128)(2,1)} async-done(((bf16[16,32,3584]{2,1,0:T(8,128)(2,1)}), bf16[16,32,3584]{2,1,0:T(8,128)(2,1)}, u32[]{:S(2)}, u32[]{:S(2)}) %all-to-all-start.1) | async-done | bytes 3670048 | tf_op jit(solution)/shard_map/all_to_all | solution.py:313
  154.1 2.8 %bitcast_reduce_fusion = bf16[8,32,3584]{2,1,0:T(8,128)(2,1)S(1)} fusion(bf16[16,32,3584]{2,1,0:T(8,128)(2,1)} %all-to-all-done.1), kind=kLoop, calls=%fused_computation.5 | loop fusion | flops 917504 | bytes 5505024 | tf_op jit(solution)/shard_map/reduce_sum | solution.py:323
  156.9 0.7 fusion.25
  157.5 1.9 %fusion.1 = bf16[256,3584]{1,0:T(8,128)(2,1)} fusion(f32[256,3584]{1,0:T(8,128)S(1)} %fusion.25, bf16[256,3584]{1,0:T(8,128)(2,1)S(1)} %bitcast.40, f32[256,256]{1,0:T(8,128)S(1)} %select_reduce_fusion), kind=kOutput, calls=%fused_computation.3 | convolution fusion | flops 471859200 | bytes 7602176 | tf_op jit(solution)/shard_map/dot_general | solution.py:329
  159.5 22.7 %shard_map.114 = bf16[16,3584]{1,0:T(8,128)(2,1)} custom-call(bf16[16,16,3584]{2,1,0:T(8,128)(2,1)} %bitcast.45), custom_call_target="tpu_custom_call" | custom-call | tf_op jit(solution)/shard_map/pallas_call | solution.py:240
  182.2 1.6 copy.51
  (26 shorter events, 0.6 us)
Async XLA Ops:
  0.6 101.4 %copy-start = (bf16[4,64,576]{2,1,0:T(8,128)(2,1)S(1)}, bf16[4,64,576]{2,1,0:T(8,128)(2,1)}, u32[]{:S(2)}) copy-start(bf16[4,64,576]{2,1,0:T(8,128)(2,1)} %param.10) | copy-start | bytes 884740
  36.4 51.8 %copy-start.3 = (bf16[1,3584,512]{2,1,0:T(8,128)(2,1)S(1)}, bf16[1,3584,512]{2,1,0:T(8,128)(2,1)}, u32[]{:S(2)}) copy-start(bf16[1,3584,512]{2,1,0:T(8,128)(2,1)} %param.17) | copy-start | bytes 11010052
  88.3 2.1 %copy-start.4 = (bf16[1,3584,512]{2,1,0:T(8,128)(2,1)S(1)}, bf16[1,3584,512]{2,1,0:T(8,128)(2,1)}, u32[]{:S(2)}) copy-start(bf16[1,3584,512]{2,1,0:T(8,128)(2,1)} %param.18) | copy-start | bytes 11010052
  90.3 2.2 %copy-start.5 = (bf16[1,512,3584]{2,1,0:T(8,128)(2,1)S(1)}, bf16[1,512,3584]{2,1,0:T(8,128)(2,1)}, u32[]{:S(2)}) copy-start(bf16[1,512,3584]{2,1,0:T(8,128)(2,1)} %param.19) | copy-start | bytes 11010052
  96.4 5.6 %copy-start.1 = (bf16[4,256,576]{1,2,0:T(8,128)(2,1)S(1)}, bf16[4,256,576]{1,2,0:T(8,128)(2,1)}, u32[]{:S(2)}) copy-start(bf16[4,256,576]{1,2,0:T(8,128)(2,1)} %param.11) | copy-start | bytes 3538948
  96.4 5.7 %copy-start.2 = (s32[4]{0:T(128)S(1)}, s32[4]{0:T(128)}, u32[]{:S(2)}) copy-start(s32[4]{0:T(128)} %param.12) | copy-start | bytes 52
  96.4 57.7 %all-to-all-start.1 = ((bf16[16,32,3584]{2,1,0:T(8,128)(2,1)}), bf16[16,32,3584]{2,1,0:T(8,128)(2,1)}, u32[]{:S(2)}, u32[]{:S(2)}) async-start(bf16[16,32,3584]{2,1,0:T(8,128)(2,1)} %bitcast.46), calls=%async_computation.1 | async-start | bytes 7340032 | tf_op jit(solution)/shard_map/all_to_all | solution.py:313

commit v12 on v11

--- a/solution.py
+++ b/solution.py
@@ -317,17 +317,21 @@
         concat_axis=0,
         tiled=True,
     )
-    expert_out = (
-        returned.reshape(pair_count, 2, expert_slots, feature)
-        .astype(jnp.float32)
-        .sum(axis=1)
-        .astype(jnp.bfloat16)
-        .reshape(slot_count, feature)
-    )
-    weight_high = combine.astype(jnp.bfloat16)
-    weight_low = (combine - weight_high.astype(jnp.float32)).astype(jnp.bfloat16)
-    column_mixed = jnp.dot(weight_high, expert_out, preferred_element_type=jnp.float32) + jnp.dot(
-        weight_low, expert_out, preferred_element_type=jnp.float32
+    half_slots = jnp.arange(2 * slot_count, dtype=jnp.int32)
+    half_weight = 0.0
+    for half in range(2):
+        placed = slot_id + half * expert_slots + experts[None, :] * expert_slots
+        placed = jnp.where(token_hot > 0, placed, 2 * slot_count)
+        half_weight = half_weight + jnp.sum(
+            jnp.where(placed[:, :, None] == half_slots[None, None, :], gate_of[:, :, None], 0.0),
+            axis=1,
+        )
+    weight_high = half_weight.astype(jnp.bfloat16)
+    weight_low = (half_weight - weight_high.astype(jnp.float32)).astype(jnp.bfloat16)
+    weight_high, weight_low = lax.optimization_barrier((weight_high, weight_low))
+    halves = returned.reshape(2 * slot_count, feature)
+    column_mixed = jnp.dot(weight_high, halves, preferred_element_type=jnp.float32) + jnp.dot(
+        weight_low, halves, preferred_element_type=jnp.float32
     )
     mixed = ring_scatter(
         column_mixed.astype(jnp.bfloat16).reshape(group_count, row_count, feature), group_count

time: 184 us -> 187 us (1.016)
  matrix products: 14.5 us -> 19.5 us
  waiting for transfers between devices: 48.7 us -> 45.8 us
    dot_general x2, matrix products: 2.59 us -> 7.64 us  [the longest x1 4.49 us: per_device(): jnp.dot(weight_low, halves, preferred_element_type=jnp.float32)]
    all_to_all x1, waiting for transfers between devices: 48.7 us -> 45.8 us  [per_device(): lax.all_to_all(partials.reshape(peer_count, expert_slots, feature), 'ep',...]
    reduce_sum x2 -> x1, other arithmetic: 4.27 us -> 3.77 us  [per_device(): jnp.sum(jnp.where(placed[:, :, None] == half_slots[None, None, :], gate_o...]
  transfers between devices with their start and end apart: 1 -> 1, of which waited for: 1 -> 1; matrix products, arithmetic and copies ran while one was open for 2% -> 3% of each run, Pallas kernels for 0% -> 0%
where the time goes in v12:
time: 187 us; the launch traced here: 186 us
  blocking collectives  51.8 us (28%)
  Pallas kernels  48.6 us (26%)
  waiting for transfers between devices  45.8 us (24%)
  matrix products  19.5 us (10%)
  other arithmetic  8.84 us (5%)
  local copies, waits for them, and re-layouts  5.07 us (3%)
  starting transfers between devices  4.81 us (3%)
    all_to_all x1, blocking collectives, per_device(): lax.all_to_all(doubled, 'ep', split_axis=0, concat_axis=0, tiled=True)  51.8 us
    all_to_all x1, waiting for transfers between devices, per_device(): lax.all_to_all(partials.reshape(peer_count, expert_slots, feature), 'ep',...  45.8 us
    pallas_call x1, Pallas kernels, ring_gather(): pl.pallas_call(functools.partial(gather_kernel, chips, widths), out_shape...  26 us
    pallas_call x1, Pallas kernels, ring_scatter(): pl.pallas_call(functools.partial(scatter_kernel, chips, widths), out_shap...  22.7 us
    all_to_all x1, starting transfers between devices, per_device(): lax.all_to_all(partials.reshape(peer_count, expert_slots, feature), 'ep',...  4.81 us
    dot_general x1, matrix products, per_device(): jnp.dot(weight_low, halves, preferred_element_type=jnp.float32)  4.49 us
    dot_general x1, matrix products, expert_partial(): return jnp.dot(hidden, w_down[0], preferred_element_type=jnp.float32)  3.91 us
    reduce_sum x1, other arithmetic, per_device(): jnp.sum(jnp.where(placed[:, :, None] == half_slots[None, None, :], gate_o...  3.77 us
  transfers between devices with their start and end apart: 1, of which 1 were waited for; matrix products, arithmetic and copies ran while one was open for 3% of the time, Pallas kernels for 0%

profile of v12, /device:TPU:1, one launch (start us, length us, event | category | flops | bytes accessed | tf_op | source)
XLA Modules:
  0.0 186.0 jit_solution(17712753465017624380)
XLA Ops:
  0.6 0.7 convert_element_type.60
  1.4 0.8 copy.39
  2.2 0.7 convert_element_type.59
  3.1 1.6 pad_maximum_fusion.x_ref
  4.7 26.0 %shard_map.113 = bf16[16,16,3712]{2,1,0:T(8,128)(2,1)} custom-call(bf16[16,3712]{1,0:T(8,128)(2,1)} %pad_maximum_fusion.x_ref), custom_call_target="tpu_custom_call" | custom-call | tf_op jit(solution)/shard_map/pallas_call | solution.py:124
  30.6 1.1 fusion.32
  31.9 0.1 copy.43
  32.0 0.7 fusion.34
  32.7 0.1 copy.44
  32.8 0.1 reduce_window_sum.14
  33.0 0.1 copy.50
  33.1 0.7 fusion.7
  33.8 2.2 %convolution_convert_fusion.1 = bf16[256,3584]{1,0:T(8,128)(2,1)S(1)} fusion(pred[256,256]{1,0:T(8,128)(4,1)S(1)} %fusion.7, bf16[256,3712]{1,0:T(8,128)(2,1)} %bitcast.41), kind=kOutput, calls=%fused_computation.4 | convolution fusion | flops 470679552 | bytes 3735552 | tf_op jit(solution)/shard_map/dot_general | solution.py:305
  36.0 0.4 broadcast_in_dim.62
  36.4 51.8 %all_to_all.10 = bf16[16,32,3584]{2,1,0:T(8,128)(2,1)S(1)} all-to-all(bf16[16,32,3584]{2,1,0:T(8,128)(2,1)S(1)} %bitcast.39), channel_id=1, replica_groups=mesh['grp'=16,'ep'=16] {'ep'}, dimensions={0} | all-to-all | bytes 7340032 | tf_op jit(solution)/shard_map/all_to_all | solution.py:309
  88.3 2.1 %fusion.5 = f32[512,512]{1,0:T(8,128)S(1)} fusion(bf16[512,3584]{1,0:T(8,128)(2,1)S(1)} %bitcast.45, bf16[1,3584,512]{2,1,0:T(8,128)(2,1)S(1)} %copy-done.3), kind=kOutput, calls=%fused_computation.12 | convolution fusion | flops 1879048192 | bytes 8388608 | tf_op jit(solution)/shard_map/dot_general | solution.py:259
  90.4 2.1 %fusion.12 = bf16[512,512]{1,0:T(8,128)(2,1)S(1)} fusion(bf16[512,3584]{1,0:T(8,128)(2,1)S(1)} %bitcast.46, bf16[1,3584,512]{2,1,0:T(8,128)(2,1)S(1)} %copy-done.4, f32[512,512]{1,0:T(8,128)S(1)} %fusion.5), kind=kOutput, calls=%fused_computation.18 | convolution fusion | flops 1880621056 | bytes 8912896 | tf_op jit(solution)/shard_map/dot_general | solution.py:260
  92.5 3.9 %convolution_convert_fusion = bf16[512,3584]{1,0:T(8,128)(2,1)} fusion(bf16[512,512]{1,0:T(8,128)(2,1)S(1)} %fusion.12, bf16[1,512,3584]{2,1,0:T(8,128)(2,1)S(1)} %copy-done.5), kind=kOutput, calls=%fused_computation.1 | convolution fusion | flops 1880883200 | bytes 7864320 | tf_op jit(solution)/shard_map/dot_general | solution.py:262
  96.4 4.8 %all-to-all-start.1 = ((bf16[16,32,3584]{2,1,0:T(8,128)(2,1)}), bf16[16,32,3584]{2,1,0:T(8,128)(2,1)}, u32[]{:S(2)}, u32[]{:S(2)}) async-start(bf16[16,32,3584]{2,1,0:T(8,128)(2,1)} %bitcast.44), calls=%async_computation.1 | async-start | bytes 7340032 | tf_op jit(solution)/shard_map/all_to_all | solution.py:313
  101.3 0.1 copy.49
  101.4 0.1 copy.45
  101.8 0.1 copy.48
  101.9 3.8 %select_reduce_fusion = (f32[256,512]{1,0:T(8,128)S(1)}, f32[256,512]{1,0:T(8,128)S(1)}) fusion(s32[256,8]{1,0:T(8,128)S(1)} %copy.49, f32[256,8]{1,0:T(8,128)S(1)} %copy.48, s32[256,8]{1,0:T(8,128)S(1)} %copy.45), kind=kLoop, calls=%fused_computation.5 | loop fusion | flops 6029312 | bytes 1073152 | tf_op jit(solution)/shard_map/reduce_sum | solution.py:325
  105.7 0.1 subtract_convert_fusion
  106.5 0.3 fusion.16
  106.9 0.2 fusion.33
  107.1 1.2 fusion.19
  108.3 45.8 %all-to-all-done.1 = bf16[16,32,3584]{2,1,0:T(8,128)(2,1)} async-done(((bf16[16,32,3584]{2,1,0:T(8,128)(2,1)}), bf16[16,32,3584]{2,1,0:T(8,128)(2,1)}, u32[]{:S(2)}, u32[]{:S(2)}) %all-to-all-start.1) | async-done | bytes 3670048 | tf_op jit(solution)/shard_map/all_to_all | solution.py:313
  154.1 3.1 %fusion.35 = f32[256,3584]{1,0:T(8,128)S(1)} fusion(bf16[256,512]{1,0:T(8,128)(2,1)S(1)} %get-tuple-element.4, bf16[512,3584]{1,0:T(8,128)(2,1)} %bitcast.9), kind=kOutput, calls=%fused_computation.63 | convolution fusion | flops 939524096 | bytes 7602176 | tf_op jit(solution)/shard_map/dot_general | solution.py:333
  157.3 4.5 %fusion.1 = bf16[256,3584]{1,0:T(8,128)(2,1)} fusion(f32[256,3584]{1,0:T(8,128)S(1)} %fusion.35, bf16[256,512]{1,0:T(8,128)(2,1)S(1)} %get-tuple-element.5, bf16[512,3584]{1,0:T(8,128)(2,1)} %bitcast.9), kind=kOutput, calls=%fused_computation.3 | convolution fusion | flops 941359104 | bytes 9437184 | tf_op jit(solution)/shard_map/dot_general | solution.py:333
  161.7 22.7 %shard_map.114 = bf16[16,3584]{1,0:T(8,128)(2,1)} custom-call(bf16[16,16,3584]{2,1,0:T(8,128)(2,1)} %bitcast.42), custom_call_target="tpu_custom_call" | custom-call | tf_op jit(solution)/shard_map/pallas_call | solution.py:240
  184.4 1.6 copy.57
  (29 shorter events, 0.8 us)
Async XLA Ops:
  0.6 105.8 %copy-start = (bf16[4,64,576]{2,1,0:T(8,128)(2,1)S(1)}, bf16[4,64,576]{2,1,0:T(8,128)(2,1)}, u32[]{:S(2)}) copy-start(bf16[4,64,576]{2,1,0:T(8,128)(2,1)} %param.10) | copy-start | bytes 884740
  36.4 51.8 %copy-start.3 = (bf16[1,3584,512]{2,1,0:T(8,128)(2,1)S(1)}, bf16[1,3584,512]{2,1,0:T(8,128)(2,1)}, u32[]{:S(2)}) copy-start(bf16[1,3584,512]{2,1,0:T(8,128)(2,1)} %param.17) | copy-start | bytes 11010052
  88.3 2.1 %copy-start.4 = (bf16[1,3584,512]{2,1,0:T(8,128)(2,1)S(1)}, bf16[1,3584,512]{2,1,0:T(8,128)(2,1)}, u32[]{:S(2)}) copy-start(bf16[1,3584,512]{2,1,0:T(8,128)(2,1)} %param.18) | copy-start | bytes 11010052
  90.3 2.2 %copy-start.5 = (bf16[1,512,3584]{2,1,0:T(8,128)(2,1)S(1)}, bf16[1,512,3584]{2,1,0:T(8,128)(2,1)}, u32[]{:S(2)}) copy-start(bf16[1,512,3584]{2,1,0:T(8,128)(2,1)} %param.19) | copy-start | bytes 11010052
  96.4 10.1 %copy-start.1 = (bf16[4,256,576]{1,2,0:T(8,128)(2,1)S(1)}, bf16[4,256,576]{1,2,0:T(8,128)(2,1)}, u32[]{:S(2)}) copy-start(bf16[4,256,576]{1,2,0:T(8,128)(2,1)} %param.11) | copy-start | bytes 3538948
  96.4 10.1 %copy-start.2 = (s32[4]{0:T(128)S(1)}, s32[4]{0:T(128)}, u32[]{:S(2)}) copy-start(s32[4]{0:T(128)} %param.12) | copy-start | bytes 52
  96.4 57.7 %all-to-all-start.1 = ((bf16[16,32,3584]{2,1,0:T(8,128)(2,1)}), bf16[16,32,3584]{2,1,0:T(8,128)(2,1)}, u32[]{:S(2)}, u32[]{:S(2)}) async-start(bf16[16,32,3584]{2,1,0:T(8,128)(2,1)} %bitcast.44), calls=%async_computation.1 | async-start | bytes 7340032 | tf_op jit(solution)/shard_map/all_to_all | solution.py:313

commit v13 on v11

--- a/solution.py
+++ b/solution.py
@@ -36,7 +36,7 @@
     return jnp.where(request_slot < live_count, context, jnp.zeros_like(context))
 
 
-def gather_kernel(chips, widths, x_ref, out_ref, send_sem, recv_sem):
+def gather_kernel(chips, windows, x_ref, m_ref, out_ref, mout_ref, send_sem, recv_sem):
     group = lax.axis_index("grp")
     peer_col = lax.axis_index("ep")
     z = group // 2
@@ -44,7 +44,8 @@
     right = lax.rem(z + 1, chips) * 2 + core
     left = lax.rem(z + chips - 1, chips) * 2 + core
     partner = z * 2 + (1 - core)
-    starts = [sum(widths[:piece]) for piece in range(len(widths))]
+    sources = (x_ref, m_ref)
+    targets = (out_ref, mout_ref)
 
     barrier = pltpu.get_barrier_semaphore()
     for peer in (left, right, partner):
@@ -53,16 +54,17 @@
 
     started = []
 
-    def window(ref, origin, piece):
-        columns = pl.ds(starts[piece], widths[piece])
+    def window(refs, origin, piece):
+        which, start, width = windows[piece]
+        columns = pl.ds(start, width)
         if origin is None:
-            return ref.at[:, columns]
-        return ref.at[origin, :, columns]
+            return refs[which].at[:, columns]
+        return refs[which].at[origin, :, columns]
 
     def send(origin, piece, peer, from_input):
         copy = pltpu.make_async_remote_copy(
-            src_ref=window(x_ref, None, piece) if from_input else window(out_ref, origin, piece),
-            dst_ref=window(out_ref, origin, piece),
+            src_ref=window(sources, None, piece) if from_input else window(targets, origin, piece),
+            dst_ref=window(targets, origin, piece),
             send_sem=send_sem.at[len(started)],
             recv_sem=recv_sem.at[origin, piece],
             device_id=(peer, peer_col),
@@ -73,37 +75,38 @@
 
     def arrive(origin, piece, peer):
         pltpu.make_async_remote_copy(
-            src_ref=window(out_ref, origin, piece),
-            dst_ref=window(out_ref, origin, piece),
+            src_ref=window(targets, origin, piece),
+            dst_ref=window(targets, origin, piece),
             send_sem=send_sem.at[0],
             recv_sem=recv_sem.at[origin, piece],
             device_id=(peer, peer_col),
             device_id_type=MESH,
         ).wait_recv()
 
-    for piece in range(len(widths)):
+    for piece in range(len(windows)):
         send(group, piece, right, True)
         send(group, piece, left, True)
         send(group, piece, partner, True)
     out_ref[group] = x_ref[...]
+    mout_ref[group] = m_ref[...]
     forward_hops = chips // 2
     backward_hops = (chips - 1) // 2
     for step in range(1, forward_hops + 1):
         origin = lax.rem(z + chips - step, chips) * 2 + core
-        for piece in range(len(widths)):
+        for piece in range(len(windows)):
             arrive(origin, piece, left)
             if step < forward_hops:
                 send(origin, piece, right, False)
             send(origin, piece, partner, False)
         if step <= backward_hops:
             origin = lax.rem(z + step, chips) * 2 + core
-            for piece in range(len(widths)):
+            for piece in range(len(windows)):
                 arrive(origin, piece, right)
                 if step < backward_hops:
                     send(origin, piece, left, False)
                 send(origin, piece, partner, False)
     for other in range(chips):
-        for piece in range(len(widths)):
+        for piece in range(len(windows)):
             arrive(other * 2 + (1 - core), piece, partner)
     for copy in started:
         copy.wait_send()
@@ -115,23 +118,27 @@
     return 3 + 2 * forward_hops - 1 + 2 * backward_hops - 1
 
 
-def ring_gather(block, group_count):
+def ring_gather(block, meta, group_count):
     chips = group_count // 2
     lanes = block.shape[1] // 128
-    widths = tuple(
-        (lanes * (piece + 1) // CHUNKS - lanes * piece // CHUNKS) * 128 for piece in range(CHUNKS)
-    )
+    windows = tuple(
+        (0, lanes * piece // CHUNKS * 128, (lanes * (piece + 1) // CHUNKS - lanes * piece // CHUNKS) * 128)
+        for piece in range(CHUNKS)
+    ) + ((1, 0, meta.shape[1]),)
     return pl.pallas_call(
-        functools.partial(gather_kernel, chips, widths),
-        out_shape=jax.ShapeDtypeStruct((group_count,) + block.shape, block.dtype),
-        in_specs=[pl.BlockSpec(memory_space=pltpu.VMEM)],
-        out_specs=pl.BlockSpec(memory_space=pltpu.VMEM),
+        functools.partial(gather_kernel, chips, windows),
+        out_shape=(
+            jax.ShapeDtypeStruct((group_count,) + block.shape, block.dtype),
+            jax.ShapeDtypeStruct((group_count,) + meta.shape, meta.dtype),
+        ),
+        in_specs=[pl.BlockSpec(memory_space=pltpu.VMEM)] * 2,
+        out_specs=(pl.BlockSpec(memory_space=pltpu.VMEM),) * 2,
         scratch_shapes=[
-            pltpu.SemaphoreType.DMA((send_count(chips) * len(widths),)),
-            pltpu.SemaphoreType.DMA((group_count, len(widths))),
+            pltpu.SemaphoreType.DMA((send_count(chips) * len(windows),)),
+            pltpu.SemaphoreType.DMA((group_count, len(windows))),
         ],
         compiler_params=pltpu.CompilerParams(collective_id=0, has_side_effects=True),
-    )(block)
+    )(block, meta)
 
 
 def scatter_kernel(
@@ -277,13 +284,12 @@
     gate_low = (gates - gate_high.astype(jnp.float32)).astype(jnp.bfloat16)
     meta = jnp.concatenate([ids.astype(jnp.bfloat16), gate_high, gate_low], axis=1)
     meta = jnp.pad(meta, ((0, 0), (0, 128 - meta.shape[1])))
-    packed = ring_gather(jnp.concatenate([tokens, meta], axis=1), group_count).reshape(
-        column_rows, feature + meta.shape[1]
-    )
-    all_tokens = packed[:, :feature]
-    all_ids = packed[:, feature : feature + TOPK].astype(jnp.int32)
-    all_gates = packed[:, feature + TOPK : feature + 2 * TOPK].astype(jnp.float32) + packed[
-        :, feature + 2 * TOPK : feature + 3 * TOPK
+    gathered, gathered_meta = ring_gather(tokens, meta, group_count)
+    all_tokens = gathered.reshape(column_rows, feature)
+    packed = gathered_meta.reshape(column_rows, meta.shape[1])
+    all_ids = packed[:, :TOPK].astype(jnp.int32)
+    all_gates = packed[:, TOPK : 2 * TOPK].astype(jnp.float32) + packed[
+        :, 2 * TOPK : 3 * TOPK
     ].astype(jnp.float32)
 
     my_group = lax.axis_index("grp")

time: 184 us -> 182 us (0.989)
  no operation moved by 1% of the time
where the time goes in v13:
time: 182 us
  blocking collectives  51.9 us (29%)
  waiting for transfers between devices  48.7 us (27%)
  Pallas kernels  47.6 us (26%)
  matrix products  14.5 us (8%)
  other arithmetic  8.19 us (4%)
  local copies, waits for them, and re-layouts  4.81 us (3%)
  starting transfers between devices  4.63 us (3%)
    all_to_all x1, blocking collectives, per_device(): lax.all_to_all(doubled, 'ep', split_axis=0, concat_axis=0, tiled=True)  51.9 us
    all_to_all x1, waiting for transfers between devices, per_device(): lax.all_to_all(partials.reshape(peer_count, expert_slots, feature), 'ep',...  48.7 us
    pallas_call x1, Pallas kernels, ring_gather(): pl.pallas_call(functools.partial(gather_kernel, chips, windows), out_shap...  26.2 us
    pallas_call x1, Pallas kernels, ring_scatter(): pl.pallas_call(functools.partial(scatter_kernel, chips, widths), out_shap...  21.4 us
    all_to_all x1, starting transfers between devices, per_device(): lax.all_to_all(partials.reshape(peer_count, expert_slots, feature), 'ep',...  4.63 us
    dot_general x1, matrix products, expert_partial(): return jnp.dot(hidden, w_down[0], preferred_element_type=jnp.float32)  3.91 us
  transfers between devices with their start and end apart: 1, of which 1 were waited for; matrix products, arithmetic and copies ran while one was open for 2% of the time, Pallas kernels for 0%

profile of v13, /device:TPU:1, one launch (start us, length us, event | category | flops | bytes accessed | tf_op | source)
XLA Modules:
  0.0 181.9 jit_solution(11883603791224034162)
XLA Ops:
  0.6 0.7 convert_element_type.62
  1.4 0.8 copy.35
  2.1 0.1 copy.37
  2.2 0.7 convert_element_type.61
  2.9 0.1 copy.36
  3.0 0.7 fusion.30.m_ref
  3.7 26.2 %shard_map.113 = (bf16[16,16,3584]{2,1,0:T(8,128)(2,1)}, bf16[16,16,128]{2,1,0:T(8,128)(2,1)}) custom-call(bf16[16,3584]{1,0:T(8,128)(2,1)} %x_ref.1, bf16[16,128]{1,0:T(8,128)(2,1)} %fusion.30.m_ref), custom_call_target="tpu_custom_call" | custom-call | tf_op jit(solution)/shard_map/pallas_call | solution.py:128
  29.9 1.1 fusion.34
  31.2 0.1 copy.39
  31.3 0.7 fusion.36
  32.0 0.1 copy.40
  32.1 0.1 reduce_window_sum.14
  32.3 0.1 copy.41
  32.4 0.7 fusion.7
  33.1 2.2 %convolution_convert_fusion.1 = bf16[256,3584]{1,0:T(8,128)(2,1)S(1)} fusion(pred[256,256]{1,0:T(8,128)(4,1)S(1)} %fusion.7, bf16[256,3584]{1,0:T(8,128)(2,1)} %bitcast.49), kind=kOutput, calls=%fused_computation.4 | convolution fusion | flops 470679552 | bytes 3735552 | tf_op jit(solution)/shard_map/dot_general | solution.py:311
  35.3 0.4 broadcast_in_dim.46
  35.7 51.9 %all_to_all.10 = bf16[16,32,3584]{2,1,0:T(8,128)(2,1)S(1)} all-to-all(bf16[16,32,3584]{2,1,0:T(8,128)(2,1)S(1)} %bitcast.43), channel_id=1, replica_groups=mesh['grp'=16,'ep'=16] {'ep'}, dimensions={0} | all-to-all | bytes 7340032 | tf_op jit(solution)/shard_map/all_to_all | solution.py:315
  87.6 2.1 %fusion.5 = f32[512,512]{1,0:T(8,128)S(1)} fusion(bf16[512,3584]{1,0:T(8,128)(2,1)S(1)} %bitcast.47, bf16[1,3584,512]{2,1,0:T(8,128)(2,1)S(1)} %copy-done.3), kind=kOutput, calls=%fused_computation.9 | convolution fusion | flops 1879048192 | bytes 8388608 | tf_op jit(solution)/shard_map/dot_general | solution.py:266
  89.7 2.1 %fusion.11 = bf16[512,512]{1,0:T(8,128)(2,1)S(1)} fusion(bf16[512,3584]{1,0:T(8,128)(2,1)S(1)} %bitcast.48, bf16[1,3584,512]{2,1,0:T(8,128)(2,1)S(1)} %copy-done.4, f32[512,512]{1,0:T(8,128)S(1)} %fusion.5), kind=kOutput, calls=%fused_computation.15 | convolution fusion | flops 1880621056 | bytes 8912896 | tf_op jit(solution)/shard_map/dot_general | solution.py:267
  91.8 3.9 %convolution_convert_fusion = bf16[512,3584]{1,0:T(8,128)(2,1)} fusion(bf16[512,512]{1,0:T(8,128)(2,1)S(1)} %fusion.11, bf16[1,512,3584]{2,1,0:T(8,128)(2,1)S(1)} %copy-done.5), kind=kOutput, calls=%fused_computation.1 | convolution fusion | flops 1880883200 | bytes 7864320 | tf_op jit(solution)/shard_map/dot_general | solution.py:269
  95.8 4.6 %all-to-all-start.1 = ((bf16[16,32,3584]{2,1,0:T(8,128)(2,1)}), bf16[16,32,3584]{2,1,0:T(8,128)(2,1)}, u32[]{:S(2)}, u32[]{:S(2)}) async-start(bf16[16,32,3584]{2,1,0:T(8,128)(2,1)} %bitcast.46), calls=%async_computation.1 | async-start | bytes 7340032 | tf_op jit(solution)/shard_map/all_to_all | solution.py:319
  100.6 0.1 copy.44
  101.4 0.3 fusion.15
  101.8 0.2 fusion.35
  102.0 1.5 select_reduce_fusion
  103.5 1.2 fusion.18
  104.7 48.7 %all-to-all-done.1 = bf16[16,32,3584]{2,1,0:T(8,128)(2,1)} async-done(((bf16[16,32,3584]{2,1,0:T(8,128)(2,1)}), bf16[16,32,3584]{2,1,0:T(8,128)(2,1)}, u32[]{:S(2)}, u32[]{:S(2)}) %all-to-all-start.1) | async-done | bytes 3670048 | tf_op jit(solution)/shard_map/all_to_all | solution.py:319
  153.5 2.8 %bitcast_reduce_fusion = bf16[8,32,3584]{2,1,0:T(8,128)(2,1)S(1)} fusion(bf16[16,32,3584]{2,1,0:T(8,128)(2,1)} %all-to-all-done.1), kind=kLoop, calls=%fused_computation.5 | loop fusion | flops 917504 | bytes 5505024 | tf_op jit(solution)/shard_map/reduce_sum | solution.py:329
  156.3 0.7 fusion.24
  156.9 1.9 %fusion.1 = bf16[256,3584]{1,0:T(8,128)(2,1)} fusion(f32[256,3584]{1,0:T(8,128)S(1)} %fusion.24, bf16[256,3584]{1,0:T(8,128)(2,1)S(1)} %bitcast.42, f32[256,256]{1,0:T(8,128)S(1)} %select_reduce_fusion), kind=kOutput, calls=%fused_computation.3 | convolution fusion | flops 471859200 | bytes 7602176 | tf_op jit(solution)/shard_map/dot_general | solution.py:335
  158.9 21.4 %shard_map.114 = bf16[16,3584]{1,0:T(8,128)(2,1)} custom-call(bf16[16,16,3584]{2,1,0:T(8,128)(2,1)} %bitcast.45), custom_call_target="tpu_custom_call" | custom-call | tf_op jit(solution)/shard_map/pallas_call | solution.py:247
  180.3 1.6 copy.51
  (25 shorter events, 0.5 us)
Async XLA Ops:
  0.6 100.8 %copy-start = (bf16[4,64,576]{2,1,0:T(8,128)(2,1)S(1)}, bf16[4,64,576]{2,1,0:T(8,128)(2,1)}, u32[]{:S(2)}) copy-start(bf16[4,64,576]{2,1,0:T(8,128)(2,1)} %param.10) | copy-start | bytes 884740
  35.7 51.9 %copy-start.3 = (bf16[1,3584,512]{2,1,0:T(8,128)(2,1)S(1)}, bf16[1,3584,512]{2,1,0:T(8,128)(2,1)}, u32[]{:S(2)}) copy-start(bf16[1,3584,512]{2,1,0:T(8,128)(2,1)} %param.17) | copy-start | bytes 11010052
  87.6 2.1 %copy-start.4 = (bf16[1,3584,512]{2,1,0:T(8,128)(2,1)S(1)}, bf16[1,3584,512]{2,1,0:T(8,128)(2,1)}, u32[]{:S(2)}) copy-start(bf16[1,3584,512]{2,1,0:T(8,128)(2,1)} %param.18) | copy-start | bytes 11010052
  89.7 2.2 %copy-start.5 = (bf16[1,512,3584]{2,1,0:T(8,128)(2,1)S(1)}, bf16[1,512,3584]{2,1,0:T(8,128)(2,1)}, u32[]{:S(2)}) copy-start(bf16[1,512,3584]{2,1,0:T(8,128)(2,1)} %param.19) | copy-start | bytes 11010052
  95.7 5.6 %copy-start.1 = (bf16[4,256,576]{1,2,0:T(8,128)(2,1)S(1)}, bf16[4,256,576]{1,2,0:T(8,128)(2,1)}, u32[]{:S(2)}) copy-start(bf16[4,256,576]{1,2,0:T(8,128)(2,1)} %param.11) | copy-start | bytes 3538948
  95.7 5.7 %copy-start.2 = (s32[4]{0:T(128)S(1)}, s32[4]{0:T(128)}, u32[]{:S(2)}) copy-start(s32[4]{0:T(128)} %param.12) | copy-start | bytes 52
  95.8 57.7 %all-to-all-start.1 = ((bf16[16,32,3584]{2,1,0:T(8,128)(2,1)}), bf16[16,32,3584]{2,1,0:T(8,128)(2,1)}, u32[]{:S(2)}, u32[]{:S(2)}) async-start(bf16[16,32,3584]{2,1,0:T(8,128)(2,1)} %bitcast.46), calls=%async_computation.1 | async-start | bytes 7340032 | tf_op jit(solution)/shard_map/all_to_all | solution.py:319

commit v14 on v13

--- a/solution.py
+++ b/solution.py
@@ -280,17 +280,13 @@
     slot_count = pair_count * expert_slots
     column_rows = group_count * row_count
 
-    gate_high = gates.astype(jnp.bfloat16)
-    gate_low = (gates - gate_high.astype(jnp.float32)).astype(jnp.bfloat16)
-    meta = jnp.concatenate([ids.astype(jnp.bfloat16), gate_high, gate_low], axis=1)
+    meta = jnp.concatenate([ids.astype(jnp.float32), gates], axis=1)
     meta = jnp.pad(meta, ((0, 0), (0, 128 - meta.shape[1])))
     gathered, gathered_meta = ring_gather(tokens, meta, group_count)
     all_tokens = gathered.reshape(column_rows, feature)
     packed = gathered_meta.reshape(column_rows, meta.shape[1])
     all_ids = packed[:, :TOPK].astype(jnp.int32)
-    all_gates = packed[:, TOPK : 2 * TOPK].astype(jnp.float32) + packed[
-        :, 2 * TOPK : 3 * TOPK
-    ].astype(jnp.float32)
+    all_gates = packed[:, TOPK : 2 * TOPK]
 
     my_group = lax.axis_index("grp")
     local = all_ids - pair_count * my_group

time: 182 us -> 181 us (level)
  no operation moved by 1% of the time
where the time goes in v14:
time: 181 us
  blocking collectives  51.9 us (29%)
  waiting for transfers between devices  48.8 us (27%)
  Pallas kernels  47.2 us (26%)
  matrix products  14.5 us (8%)
  other arithmetic  7.47 us (4%)
  local copies, waits for them, and re-layouts  4.64 us (3%)
  starting transfers between devices  4.63 us (3%)
    all_to_all x1, blocking collectives, per_device(): lax.all_to_all(doubled, 'ep', split_axis=0, concat_axis=0, tiled=True)  51.9 us
    all_to_all x1, waiting for transfers between devices, per_device(): lax.all_to_all(partials.reshape(peer_count, expert_slots, feature), 'ep',...  48.8 us
    pallas_call x1, Pallas kernels, ring_gather(): pl.pallas_call(functools.partial(gather_kernel, chips, windows), out_shap...  26.5 us
    pallas_call x1, Pallas kernels, ring_scatter(): pl.pallas_call(functools.partial(scatter_kernel, chips, widths), out_shap...  20.7 us
    all_to_all x1, starting transfers between devices, per_device(): lax.all_to_all(partials.reshape(peer_count, expert_slots, feature), 'ep',...  4.63 us
    dot_general x1, matrix products, expert_partial(): return jnp.dot(hidden, w_down[0], preferred_element_type=jnp.float32)  3.91 us
  transfers between devices with their start and end apart: 1, of which 1 were waited for; matrix products, arithmetic and copies ran while one was open for 2% of the time, Pallas kernels for 0%

profile of v14, /device:TPU:1, one launch (start us, length us, event | category | flops | bytes accessed | tf_op | source)
XLA Modules:
  0.0 180.6 jit_solution(12837748943944298309)
XLA Ops:
  0.7 0.7 convert_element_type.46
  1.4 0.1 copy.31
  1.5 0.8 copy.32
  2.2 0.7 select_maximum_fusion.m_ref
  2.9 26.5 %shard_map.113 = (bf16[16,16,3584]{2,1,0:T(8,128)(2,1)}, f32[16,16,128]{2,1,0:T(8,128)}) custom-call(bf16[16,3584]{1,0:T(8,128)(2,1)} %x_ref.1, f32[16,128]{1,0:T(8,128)} %select_maximum_fusion.m_ref), custom_call_target="tpu_custom_call" | custom-call | tf_op jit(solution)/shard_map/pallas_call | solution.py:128
  29.4 1.1 fusion.29
  30.6 0.1 reshape.124
  30.7 0.1 copy.34
  30.8 0.7 fusion.31
  31.5 0.1 copy.35
  31.6 0.1 reduce_window_sum.14
  31.7 0.1 add_select_fusion
  31.8 0.1 copy.36
  31.9 0.7 fusion.7
  32.6 2.2 %convolution_convert_fusion.1 = bf16[256,3584]{1,0:T(8,128)(2,1)S(1)} fusion(pred[256,256]{1,0:T(8,128)(4,1)S(1)} %fusion.7, bf16[256,3584]{1,0:T(8,128)(2,1)} %bitcast.49), kind=kOutput, calls=%fused_computation.4 | convolution fusion | flops 470679552 | bytes 3735552 | tf_op jit(solution)/shard_map/dot_general | solution.py:307
  34.8 0.4 broadcast_in_dim.46
  35.2 51.9 %all_to_all.10 = bf16[16,32,3584]{2,1,0:T(8,128)(2,1)S(1)} all-to-all(bf16[16,32,3584]{2,1,0:T(8,128)(2,1)S(1)} %bitcast.43), channel_id=1, replica_groups=mesh['grp'=16,'ep'=16] {'ep'}, dimensions={0} | all-to-all | bytes 7340032 | tf_op jit(solution)/shard_map/all_to_all | solution.py:311
  87.1 2.1 %fusion.5 = f32[512,512]{1,0:T(8,128)S(1)} fusion(bf16[512,3584]{1,0:T(8,128)(2,1)S(1)} %bitcast.47, bf16[1,3584,512]{2,1,0:T(8,128)(2,1)S(1)} %copy-done.3), kind=kOutput, calls=%fused_computation.9 | convolution fusion | flops 1879048192 | bytes 8388608 | tf_op jit(solution)/shard_map/dot_general | solution.py:266
  89.2 2.1 %fusion.11 = bf16[512,512]{1,0:T(8,128)(2,1)S(1)} fusion(bf16[512,3584]{1,0:T(8,128)(2,1)S(1)} %bitcast.48, bf16[1,3584,512]{2,1,0:T(8,128)(2,1)S(1)} %copy-done.4, f32[512,512]{1,0:T(8,128)S(1)} %fusion.5), kind=kOutput, calls=%fused_computation.15 | convolution fusion | flops 1880621056 | bytes 8912896 | tf_op jit(solution)/shard_map/dot_general | solution.py:267
  91.3 3.9 %convolution_convert_fusion = bf16[512,3584]{1,0:T(8,128)(2,1)} fusion(bf16[512,512]{1,0:T(8,128)(2,1)S(1)} %fusion.11, bf16[1,512,3584]{2,1,0:T(8,128)(2,1)S(1)} %copy-done.5), kind=kOutput, calls=%fused_computation.1 | convolution fusion | flops 1880883200 | bytes 7864320 | tf_op jit(solution)/shard_map/dot_general | solution.py:269
  95.2 4.6 %all-to-all-start.1 = ((bf16[16,32,3584]{2,1,0:T(8,128)(2,1)}), bf16[16,32,3584]{2,1,0:T(8,128)(2,1)}, u32[]{:S(2)}, u32[]{:S(2)}) async-start(bf16[16,32,3584]{2,1,0:T(8,128)(2,1)} %bitcast.46), calls=%async_computation.1 | async-start | bytes 7340032 | tf_op jit(solution)/shard_map/all_to_all | solution.py:315
  100.0 0.1 copy.38
  100.8 0.3 fusion.15
  101.2 0.2 fusion.30
  101.4 1.5 select_reduce_fusion
  102.9 1.2 fusion.18
  104.1 48.8 %all-to-all-done.1 = bf16[16,32,3584]{2,1,0:T(8,128)(2,1)} async-done(((bf16[16,32,3584]{2,1,0:T(8,128)(2,1)}), bf16[16,32,3584]{2,1,0:T(8,128)(2,1)}, u32[]{:S(2)}, u32[]{:S(2)}) %all-to-all-start.1) | async-done | bytes 3670048 | tf_op jit(solution)/shard_map/all_to_all | solution.py:315
  153.0 2.8 %bitcast_reduce_fusion = bf16[8,32,3584]{2,1,0:T(8,128)(2,1)S(1)} fusion(bf16[16,32,3584]{2,1,0:T(8,128)(2,1)} %all-to-all-done.1), kind=kLoop, calls=%fused_computation.5 | loop fusion | flops 917504 | bytes 5505024 | tf_op jit(solution)/shard_map/reduce_sum | solution.py:325
  155.8 0.7 fusion.24
  156.4 1.9 %fusion.1 = bf16[256,3584]{1,0:T(8,128)(2,1)} fusion(f32[256,3584]{1,0:T(8,128)S(1)} %fusion.24, bf16[256,3584]{1,0:T(8,128)(2,1)S(1)} %bitcast.42, f32[256,256]{1,0:T(8,128)S(1)} %select_reduce_fusion), kind=kOutput, calls=%fused_computation.3 | convolution fusion | flops 471859200 | bytes 7602176 | tf_op jit(solution)/shard_map/dot_general | solution.py:331
  158.4 20.7 %shard_map.114 = bf16[16,3584]{1,0:T(8,128)(2,1)} custom-call(bf16[16,16,3584]{2,1,0:T(8,128)(2,1)} %bitcast.45), custom_call_target="tpu_custom_call" | custom-call | tf_op jit(solution)/shard_map/pallas_call | solution.py:247
  179.1 1.6 copy.43
  (20 shorter events, 0.2 us)
Async XLA Ops:
  0.6 100.1 %copy-start = (bf16[4,64,576]{2,1,0:T(8,128)(2,1)S(1)}, bf16[4,64,576]{2,1,0:T(8,128)(2,1)}, u32[]{:S(2)}) copy-start(bf16[4,64,576]{2,1,0:T(8,128)(2,1)} %param.10) | copy-start | bytes 884740
  35.2 51.9 %copy-start.3 = (bf16[1,3584,512]{2,1,0:T(8,128)(2,1)S(1)}, bf16[1,3584,512]{2,1,0:T(8,128)(2,1)}, u32[]{:S(2)}) copy-start(bf16[1,3584,512]{2,1,0:T(8,128)(2,1)} %param.17) | copy-start | bytes 11010052
  87.1 2.1 %copy-start.4 = (bf16[1,3584,512]{2,1,0:T(8,128)(2,1)S(1)}, bf16[1,3584,512]{2,1,0:T(8,128)(2,1)}, u32[]{:S(2)}) copy-start(bf16[1,3584,512]{2,1,0:T(8,128)(2,1)} %param.18) | copy-start | bytes 11010052
  89.2 2.2 %copy-start.5 = (bf16[1,512,3584]{2,1,0:T(8,128)(2,1)S(1)}, bf16[1,512,3584]{2,1,0:T(8,128)(2,1)}, u32[]{:S(2)}) copy-start(bf16[1,512,3584]{2,1,0:T(8,128)(2,1)} %param.19) | copy-start | bytes 11010052
  95.2 5.5 %copy-start.1 = (bf16[4,256,576]{1,2,0:T(8,128)(2,1)S(1)}, bf16[4,256,576]{1,2,0:T(8,128)(2,1)}, u32[]{:S(2)}) copy-start(bf16[4,256,576]{1,2,0:T(8,128)(2,1)} %param.11) | copy-start | bytes 3538948
  95.2 5.6 %copy-start.2 = (s32[4]{0:T(128)S(1)}, s32[4]{0:T(128)}, u32[]{:S(2)}) copy-start(s32[4]{0:T(128)} %param.12) | copy-start | bytes 52
  95.2 57.7 %all-to-all-start.1 = ((bf16[16,32,3584]{2,1,0:T(8,128)(2,1)}), bf16[16,32,3584]{2,1,0:T(8,128)(2,1)}, u32[]{:S(2)}, u32[]{:S(2)}) async-start(bf16[16,32,3584]{2,1,0:T(8,128)(2,1)} %bitcast.46), calls=%async_computation.1 | async-start | bytes 7340032 | tf_op jit(solution)/shard_map/all_to_all | solution.py:315

commit v15 on v14

--- a/solution.py
+++ b/solution.py
@@ -36,7 +36,9 @@
     return jnp.where(request_slot < live_count, context, jnp.zeros_like(context))
 
 
-def gather_kernel(chips, windows, x_ref, m_ref, out_ref, mout_ref, send_sem, recv_sem):
+def gather_kernel(
+    chips, windows, x_ref, i_ref, g_ref, out_ref, iout_ref, gout_ref, send_sem, recv_sem
+):
     group = lax.axis_index("grp")
     peer_col = lax.axis_index("ep")
     z = group // 2
@@ -44,8 +46,8 @@
     right = lax.rem(z + 1, chips) * 2 + core
     left = lax.rem(z + chips - 1, chips) * 2 + core
     partner = z * 2 + (1 - core)
-    sources = (x_ref, m_ref)
-    targets = (out_ref, mout_ref)
+    sources = (x_ref, i_ref, g_ref)
+    targets = (out_ref, iout_ref, gout_ref)
 
     barrier = pltpu.get_barrier_semaphore()
     for peer in (left, right, partner):
@@ -87,8 +89,8 @@
         send(group, piece, right, True)
         send(group, piece, left, True)
         send(group, piece, partner, True)
-    out_ref[group] = x_ref[...]
-    mout_ref[group] = m_ref[...]
+    for source, target in zip(sources, targets):
+        target[group] = source[...]
     forward_hops = chips // 2
     backward_hops = (chips - 1) // 2
     for step in range(1, forward_hops + 1):
@@ -118,27 +120,27 @@
     return 3 + 2 * forward_hops - 1 + 2 * backward_hops - 1
 
 
-def ring_gather(block, meta, group_count):
+def ring_gather(block, ids, gates, group_count):
     chips = group_count // 2
     lanes = block.shape[1] // 128
     windows = tuple(
         (0, lanes * piece // CHUNKS * 128, (lanes * (piece + 1) // CHUNKS - lanes * piece // CHUNKS) * 128)
         for piece in range(CHUNKS)
-    ) + ((1, 0, meta.shape[1]),)
+    ) + ((1, 0, ids.shape[1]), (2, 0, gates.shape[1]))
     return pl.pallas_call(
         functools.partial(gather_kernel, chips, windows),
-        out_shape=(
-            jax.ShapeDtypeStruct((group_count,) + block.shape, block.dtype),
-            jax.ShapeDtypeStruct((group_count,) + meta.shape, meta.dtype),
+        out_shape=tuple(
+            jax.ShapeDtypeStruct((group_count,) + part.shape, part.dtype)
+            for part in (block, ids, gates)
         ),
-        in_specs=[pl.BlockSpec(memory_space=pltpu.VMEM)] * 2,
-        out_specs=(pl.BlockSpec(memory_space=pltpu.VMEM),) * 2,
+        in_specs=[pl.BlockSpec(memory_space=pltpu.VMEM)] * 3,
+        out_specs=(pl.BlockSpec(memory_space=pltpu.VMEM),) * 3,
         scratch_shapes=[
             pltpu.SemaphoreType.DMA((send_count(chips) * len(windows),)),
             pltpu.SemaphoreType.DMA((group_count, len(windows))),
         ],
         compiler_params=pltpu.CompilerParams(collective_id=0, has_side_effects=True),
-    )(block, meta)
+    )(block, ids, gates)
 
 
 def scatter_kernel(
@@ -280,13 +282,10 @@
     slot_count = pair_count * expert_slots
     column_rows = group_count * row_count
 
-    meta = jnp.concatenate([ids.astype(jnp.float32), gates], axis=1)
-    meta = jnp.pad(meta, ((0, 0), (0, 128 - meta.shape[1])))
-    gathered, gathered_meta = ring_gather(tokens, meta, group_count)
+    gathered, gathered_ids, gathered_gates = ring_gather(tokens, ids, gates, group_count)
     all_tokens = gathered.reshape(column_rows, feature)
-    packed = gathered_meta.reshape(column_rows, meta.shape[1])
-    all_ids = packed[:, :TOPK].astype(jnp.int32)
-    all_gates = packed[:, TOPK : 2 * TOPK]
+    all_ids = gathered_ids.reshape(column_rows, TOPK)
+    all_gates = gathered_gates.reshape(column_rows, TOPK)
 
     my_group = lax.axis_index("grp")
     local = all_ids - pair_count * my_group

time: 181 us -> 182 us (level)
    unnamed x15 -> x17, local copies, waits for them, and re-layouts: 2.4 us -> 4.34 us
where the time goes in v15:
time: 182 us
  blocking collectives  51.9 us (29%)
  waiting for transfers between devices  48.9 us (27%)
  Pallas kernels  47.8 us (26%)
  matrix products  14.5 us (8%)
  other arithmetic  6.97 us (4%)
  local copies, waits for them, and re-layouts  5.49 us (3%)
  starting transfers between devices  4.63 us (3%)
    all_to_all x1, blocking collectives, per_device(): lax.all_to_all(doubled, 'ep', split_axis=0, concat_axis=0, tiled=True)  51.9 us
    all_to_all x1, waiting for transfers between devices, per_device(): lax.all_to_all(partials.reshape(peer_count, expert_slots, feature), 'ep',...  48.9 us
    pallas_call x1, Pallas kernels, ring_gather(): pl.pallas_call(functools.partial(gather_kernel, chips, windows), out_shap...  27.4 us
    pallas_call x1, Pallas kernels, ring_scatter(): pl.pallas_call(functools.partial(scatter_kernel, chips, widths), out_shap...  20.5 us
    all_to_all x1, starting transfers between devices, per_device(): lax.all_to_all(partials.reshape(peer_count, expert_slots, feature), 'ep',...  4.63 us
    unnamed x17, local copies, waits for them, and re-layouts  4.34 us
    dot_general x1, matrix products, expert_partial(): return jnp.dot(hidden, w_down[0], preferred_element_type=jnp.float32)  3.91 us
  transfers between devices with their start and end apart: 1, of which 1 were waited for; matrix products, arithmetic and copies ran while one was open for 2% of the time, Pallas kernels for 0%

profile of v15, /device:TPU:1, one launch (start us, length us, event | category | flops | bytes accessed | tf_op | source)
XLA Modules:
  0.0 181.7 jit_solution(9079446706575324859)
XLA Ops:
  0.7 1.4 copy.22.i_ref
  2.1 1.4 copy.23.g_ref
  3.4 27.4 %shard_map.113 = (bf16[16,16,3584]{2,1,0:T(8,128)(2,1)}, s32[16,16,8]{2,1,0:T(8,128)}, f32[16,16,8]{2,1,0:T(8,128)}) custom-call(bf16[16,3584]{1,0:T(8,128)(2,1)} %x_ref.1, s32[16,8]{1,0:T(8,128)} %copy.22.i_ref, f32[16,8]{1,0:T(8,128)} %copy.23.g_ref), custom_call_target="tpu_custom_call" | custom-call | tf_op jit(solution)/shard_map/pallas_call | solution.py:130
  30.8 0.9 broadcast_subtract_fusion
  31.7 0.1 copy.24
  31.8 0.1 reshape.127
  31.9 0.1 copy.25
  32.1 0.7 fusion.30
  32.7 0.1 copy.26
  32.8 0.1 reduce_window_sum.14
  32.9 0.1 add_select_fusion
  33.0 0.1 copy.27
  33.1 0.7 fusion.7
  33.9 2.2 %convolution_convert_fusion.1 = bf16[256,3584]{1,0:T(8,128)(2,1)S(1)} fusion(pred[256,256]{1,0:T(8,128)(4,1)S(1)} %fusion.7, bf16[256,3584]{1,0:T(8,128)(2,1)} %bitcast.50), kind=kOutput, calls=%fused_computation.4 | convolution fusion | flops 470679552 | bytes 3735552 | tf_op jit(solution)/shard_map/dot_general | solution.py:306
  36.1 0.4 broadcast_in_dim.45
  36.5 51.9 %all_to_all.10 = bf16[16,32,3584]{2,1,0:T(8,128)(2,1)S(1)} all-to-all(bf16[16,32,3584]{2,1,0:T(8,128)(2,1)S(1)} %bitcast.44), channel_id=1, replica_groups=mesh['grp'=16,'ep'=16] {'ep'}, dimensions={0} | all-to-all | bytes 7340032 | tf_op jit(solution)/shard_map/all_to_all | solution.py:310
  88.4 2.0 %fusion.5 = f32[512,512]{1,0:T(8,128)S(1)} fusion(bf16[512,3584]{1,0:T(8,128)(2,1)S(1)} %bitcast.48, bf16[1,3584,512]{2,1,0:T(8,128)(2,1)S(1)} %copy-done.4), kind=kOutput, calls=%fused_computation.9 | convolution fusion | flops 1879048192 | bytes 8388608 | tf_op jit(solution)/shard_map/dot_general | solution.py:268
  90.4 2.1 %fusion.11 = bf16[512,512]{1,0:T(8,128)(2,1)S(1)} fusion(bf16[512,3584]{1,0:T(8,128)(2,1)S(1)} %bitcast.49, bf16[1,3584,512]{2,1,0:T(8,128)(2,1)S(1)} %copy-done.5, f32[512,512]{1,0:T(8,128)S(1)} %fusion.5), kind=kOutput, calls=%fused_computation.15 | convolution fusion | flops 1880621056 | bytes 8912896 | tf_op jit(solution)/shard_map/dot_general | solution.py:269
  92.6 3.9 %convolution_convert_fusion = bf16[512,3584]{1,0:T(8,128)(2,1)} fusion(bf16[512,512]{1,0:T(8,128)(2,1)S(1)} %fusion.11, bf16[1,512,3584]{2,1,0:T(8,128)(2,1)S(1)} %copy-done.6), kind=kOutput, calls=%fused_computation.1 | convolution fusion | flops 1880883200 | bytes 7864320 | tf_op jit(solution)/shard_map/dot_general | solution.py:271
  96.5 4.6 %all-to-all-start.1 = ((bf16[16,32,3584]{2,1,0:T(8,128)(2,1)}), bf16[16,32,3584]{2,1,0:T(8,128)(2,1)}, u32[]{:S(2)}, u32[]{:S(2)}) async-start(bf16[16,32,3584]{2,1,0:T(8,128)(2,1)} %bitcast.47), calls=%async_computation.1 | async-start | bytes 7340032 | tf_op jit(solution)/shard_map/all_to_all | solution.py:314
  101.2 0.1 copy.28
  101.3 0.1 copy.29
  102.1 0.3 fusion.15
  102.4 0.2 fusion.29
  102.7 1.5 select_reduce_fusion
  104.2 1.2 fusion.18
  105.4 48.9 %all-to-all-done.1 = bf16[16,32,3584]{2,1,0:T(8,128)(2,1)} async-done(((bf16[16,32,3584]{2,1,0:T(8,128)(2,1)}), bf16[16,32,3584]{2,1,0:T(8,128)(2,1)}, u32[]{:S(2)}, u32[]{:S(2)}) %all-to-all-start.1) | async-done | bytes 3670048 | tf_op jit(solution)/shard_map/all_to_all | solution.py:314
  154.3 2.8 %bitcast_reduce_fusion = bf16[8,32,3584]{2,1,0:T(8,128)(2,1)S(1)} fusion(bf16[16,32,3584]{2,1,0:T(8,128)(2,1)} %all-to-all-done.1), kind=kLoop, calls=%fused_computation.5 | loop fusion | flops 917504 | bytes 5505024 | tf_op jit(solution)/shard_map/reduce_sum | solution.py:324
  157.1 0.7 fusion.24
  157.8 1.9 %fusion.1 = bf16[256,3584]{1,0:T(8,128)(2,1)} fusion(f32[256,3584]{1,0:T(8,128)S(1)} %fusion.24, bf16[256,3584]{1,0:T(8,128)(2,1)S(1)} %bitcast.43, f32[256,256]{1,0:T(8,128)S(1)} %select_reduce_fusion), kind=kOutput, calls=%fused_computation.3 | convolution fusion | flops 471859200 | bytes 7602176 | tf_op jit(solution)/shard_map/dot_general | solution.py:330
  159.7 20.5 %shard_map.114 = bf16[16,3584]{1,0:T(8,128)(2,1)} custom-call(bf16[16,16,3584]{2,1,0:T(8,128)(2,1)} %bitcast.46), custom_call_target="tpu_custom_call" | custom-call | tf_op jit(solution)/shard_map/pallas_call | solution.py:249
  180.2 1.6 copy.33
  (19 shorter events, 0.1 us)
Async XLA Ops:
  0.6 101.4 %copy-start = (bf16[4,64,576]{2,1,0:T(8,128)(2,1)S(1)}, bf16[4,64,576]{2,1,0:T(8,128)(2,1)}, u32[]{:S(2)}) copy-start(bf16[4,64,576]{2,1,0:T(8,128)(2,1)} %param.10) | copy-start | bytes 884740
  36.5 51.9 %copy-start.4 = (bf16[1,3584,512]{2,1,0:T(8,128)(2,1)S(1)}, bf16[1,3584,512]{2,1,0:T(8,128)(2,1)}, u32[]{:S(2)}) copy-start(bf16[1,3584,512]{2,1,0:T(8,128)(2,1)} %param.17) | copy-start | bytes 11010052
  88.4 2.1 %copy-start.5 = (bf16[1,3584,512]{2,1,0:T(8,128)(2,1)S(1)}, bf16[1,3584,512]{2,1,0:T(8,128)(2,1)}, u32[]{:S(2)}) copy-start(bf16[1,3584,512]{2,1,0:T(8,128)(2,1)} %param.18) | copy-start | bytes 11010052
  90.4 2.2 %copy-start.6 = (bf16[1,512,3584]{2,1,0:T(8,128)(2,1)S(1)}, bf16[1,512,3584]{2,1,0:T(8,128)(2,1)}, u32[]{:S(2)}) copy-start(bf16[1,512,3584]{2,1,0:T(8,128)(2,1)} %param.19) | copy-start | bytes 11010052
  96.5 4.6 %copy-start.2 = (f32[16,16,8]{2,1,0:T(8,128)S(1)}, f32[16,16,8]{2,1,0:T(8,128)}, u32[]{:S(2)}) copy-start(f32[16,16,8]{2,1,0:T(8,128)} %get-tuple-element.6) | copy-start | bytes 24580
  96.5 5.6 %copy-start.1 = (bf16[4,256,576]{1,2,0:T(8,128)(2,1)S(1)}, bf16[4,256,576]{1,2,0:T(8,128)(2,1)}, u32[]{:S(2)}) copy-start(bf16[4,256,576]{1,2,0:T(8,128)(2,1)} %param.11) | copy-start | bytes 3538948
  96.5 5.6 %copy-start.3 = (s32[4]{0:T(128)S(1)}, s32[4]{0:T(128)}, u32[]{:S(2)}) copy-start(s32[4]{0:T(128)} %param.12) | copy-start | bytes 52
  96.5 57.8 %all-to-all-start.1 = ((bf16[16,32,3584]{2,1,0:T(8,128)(2,1)}), bf16[16,32,3584]{2,1,0:T(8,128)(2,1)}, u32[]{:S(2)}, u32[]{:S(2)}) async-start(bf16[16,32,3584]{2,1,0:T(8,128)(2,1)} %bitcast.47), calls=%async_computation.1 | async-start | bytes 7340032 | tf_op jit(solution)/shard_map/all_to_all | solution.py:314

commit v16 on v14

--- a/solution.py
+++ b/solution.py
@@ -246,7 +246,7 @@
     sends = (chips + forward_hops + backward_hops) * len(widths)
     return pl.pallas_call(
         functools.partial(scatter_kernel, chips, widths),
-        out_shape=jax.ShapeDtypeStruct(block, parts.dtype),
+        out_shape=jax.ShapeDtypeStruct(block, jnp.float32),
         in_specs=[pl.BlockSpec(memory_space=pltpu.VMEM)],
         out_specs=pl.BlockSpec(memory_space=pltpu.VMEM),
         scratch_shapes=[
@@ -333,7 +333,7 @@
     )
     mixed = ring_scatter(
         column_mixed.astype(jnp.bfloat16).reshape(group_count, row_count, feature), group_count
-    )
+    ).astype(jnp.bfloat16)
     return (context, mixed)
 
 

time: 181 us -> 181 us (level)
  no operation moved by 1% of the time
where the time goes in v16:
time: 181 us
  blocking collectives  51.9 us (29%)
  waiting for transfers between devices  48.8 us (27%)
  Pallas kernels  47.3 us (26%)
  matrix products  14.5 us (8%)
  other arithmetic  9.06 us (5%)
  starting transfers between devices  4.63 us (3%)
  local copies, waits for them, and re-layouts  3.09 us (2%)
    all_to_all x1, blocking collectives, per_device(): lax.all_to_all(doubled, 'ep', split_axis=0, concat_axis=0, tiled=True)  51.9 us
    all_to_all x1, waiting for transfers between devices, per_device(): lax.all_to_all(partials.reshape(peer_count, expert_slots, feature), 'ep',...  48.8 us
    pallas_call x1, Pallas kernels, ring_gather(): pl.pallas_call(functools.partial(gather_kernel, chips, windows), out_shap...  26.5 us
    pallas_call x1, Pallas kernels, ring_scatter(): pl.pallas_call(functools.partial(scatter_kernel, chips, widths), out_shap...  20.8 us
    all_to_all x1, starting transfers between devices, per_device(): lax.all_to_all(partials.reshape(peer_count, expert_slots, feature), 'ep',...  4.63 us
    dot_general x1, matrix products, expert_partial(): return jnp.dot(hidden, w_down[0], preferred_element_type=jnp.float32)  3.91 us
  transfers between devices with their start and end apart: 1, of which 1 were waited for; matrix products, arithmetic and copies ran while one was open for 2% of the time, Pallas kernels for 0%

profile of v16, /device:TPU:1, one launch (start us, length us, event | category | flops | bytes accessed | tf_op | source)
XLA Modules:
  0.0 180.7 jit_solution(7356027684397454207)
XLA Ops:
  0.7 0.7 convert_element_type.49
  1.4 0.1 copy.31
  1.5 0.8 copy.32
  2.2 0.7 select_maximum_fusion.m_ref
  2.9 26.5 %shard_map.113 = (bf16[16,16,3584]{2,1,0:T(8,128)(2,1)}, f32[16,16,128]{2,1,0:T(8,128)}) custom-call(bf16[16,3584]{1,0:T(8,128)(2,1)} %x_ref.1, f32[16,128]{1,0:T(8,128)} %select_maximum_fusion.m_ref), custom_call_target="tpu_custom_call" | custom-call | tf_op jit(solution)/shard_map/pallas_call | solution.py:128
  29.4 1.1 fusion.29
  30.6 0.1 reshape.124
  30.7 0.1 copy.34
  30.8 0.7 fusion.31
  31.5 0.1 copy.35
  31.6 0.1 reduce_window_sum.14
  31.7 0.1 add_select_fusion
  31.8 0.1 copy.36
  31.9 0.7 fusion.7
  32.6 2.2 %convolution_convert_fusion.1 = bf16[256,3584]{1,0:T(8,128)(2,1)S(1)} fusion(pred[256,256]{1,0:T(8,128)(4,1)S(1)} %fusion.7, bf16[256,3584]{1,0:T(8,128)(2,1)} %bitcast.49), kind=kOutput, calls=%fused_computation.4 | convolution fusion | flops 470679552 | bytes 3735552 | tf_op jit(solution)/shard_map/dot_general | solution.py:307
  34.8 0.4 broadcast_in_dim.46
  35.2 51.9 %all_to_all.10 = bf16[16,32,3584]{2,1,0:T(8,128)(2,1)S(1)} all-to-all(bf16[16,32,3584]{2,1,0:T(8,128)(2,1)S(1)} %bitcast.43), channel_id=1, replica_groups=mesh['grp'=16,'ep'=16] {'ep'}, dimensions={0} | all-to-all | bytes 7340032 | tf_op jit(solution)/shard_map/all_to_all | solution.py:311
  87.1 2.0 %fusion.5 = f32[512,512]{1,0:T(8,128)S(1)} fusion(bf16[512,3584]{1,0:T(8,128)(2,1)S(1)} %bitcast.47, bf16[1,3584,512]{2,1,0:T(8,128)(2,1)S(1)} %copy-done.3), kind=kOutput, calls=%fused_computation.9 | convolution fusion | flops 1879048192 | bytes 8388608 | tf_op jit(solution)/shard_map/dot_general | solution.py:266
  89.2 2.1 %fusion.11 = bf16[512,512]{1,0:T(8,128)(2,1)S(1)} fusion(bf16[512,3584]{1,0:T(8,128)(2,1)S(1)} %bitcast.48, bf16[1,3584,512]{2,1,0:T(8,128)(2,1)S(1)} %copy-done.4, f32[512,512]{1,0:T(8,128)S(1)} %fusion.5), kind=kOutput, calls=%fused_computation.15 | convolution fusion | flops 1880621056 | bytes 8912896 | tf_op jit(solution)/shard_map/dot_general | solution.py:267
  91.3 3.9 %convolution_convert_fusion = bf16[512,3584]{1,0:T(8,128)(2,1)} fusion(bf16[512,512]{1,0:T(8,128)(2,1)S(1)} %fusion.11, bf16[1,512,3584]{2,1,0:T(8,128)(2,1)S(1)} %copy-done.5), kind=kOutput, calls=%fused_computation.1 | convolution fusion | flops 1880883200 | bytes 7864320 | tf_op jit(solution)/shard_map/dot_general | solution.py:269
  95.2 4.6 %all-to-all-start.1 = ((bf16[16,32,3584]{2,1,0:T(8,128)(2,1)}), bf16[16,32,3584]{2,1,0:T(8,128)(2,1)}, u32[]{:S(2)}, u32[]{:S(2)}) async-start(bf16[16,32,3584]{2,1,0:T(8,128)(2,1)} %bitcast.46), calls=%async_computation.1 | async-start | bytes 7340032 | tf_op jit(solution)/shard_map/all_to_all | solution.py:315
  100.0 0.1 copy.38
  100.8 0.3 fusion.15
  101.1 0.2 fusion.30
  101.4 1.5 select_reduce_fusion
  102.9 1.2 fusion.18
  104.1 48.8 %all-to-all-done.1 = bf16[16,32,3584]{2,1,0:T(8,128)(2,1)} async-done(((bf16[16,32,3584]{2,1,0:T(8,128)(2,1)}), bf16[16,32,3584]{2,1,0:T(8,128)(2,1)}, u32[]{:S(2)}, u32[]{:S(2)}) %all-to-all-start.1) | async-done | bytes 3670048 | tf_op jit(solution)/shard_map/all_to_all | solution.py:315
  153.0 2.8 %bitcast_reduce_fusion = bf16[8,32,3584]{2,1,0:T(8,128)(2,1)S(1)} fusion(bf16[16,32,3584]{2,1,0:T(8,128)(2,1)} %all-to-all-done.1), kind=kLoop, calls=%fused_computation.5 | loop fusion | flops 917504 | bytes 5505024 | tf_op jit(solution)/shard_map/reduce_sum | solution.py:325
  155.8 0.7 fusion.24
  156.4 1.9 %fusion.1 = bf16[256,3584]{1,0:T(8,128)(2,1)} fusion(f32[256,3584]{1,0:T(8,128)S(1)} %fusion.24, bf16[256,3584]{1,0:T(8,128)(2,1)S(1)} %bitcast.42, f32[256,256]{1,0:T(8,128)S(1)} %select_reduce_fusion), kind=kOutput, calls=%fused_computation.3 | convolution fusion | flops 471859200 | bytes 7602176 | tf_op jit(solution)/shard_map/dot_general | solution.py:331
  158.4 20.8 %shard_map.114 = f32[16,3584]{1,0:T(8,128)} custom-call(bf16[16,16,3584]{2,1,0:T(8,128)(2,1)} %bitcast.45), custom_call_target="tpu_custom_call" | custom-call | tf_op jit(solution)/shard_map/pallas_call | solution.py:247
  179.1 1.6 convert_element_type.60
  (20 shorter events, 0.2 us)
Async XLA Ops:
  0.6 100.1 %copy-start = (bf16[4,64,576]{2,1,0:T(8,128)(2,1)S(1)}, bf16[4,64,576]{2,1,0:T(8,128)(2,1)}, u32[]{:S(2)}) copy-start(bf16[4,64,576]{2,1,0:T(8,128)(2,1)} %param.10) | copy-start | bytes 884740
  35.2 51.9 %copy-start.3 = (bf16[1,3584,512]{2,1,0:T(8,128)(2,1)S(1)}, bf16[1,3584,512]{2,1,0:T(8,128)(2,1)}, u32[]{:S(2)}) copy-start(bf16[1,3584,512]{2,1,0:T(8,128)(2,1)} %param.17) | copy-start | bytes 11010052
  87.1 2.1 %copy-start.4 = (bf16[1,3584,512]{2,1,0:T(8,128)(2,1)S(1)}, bf16[1,3584,512]{2,1,0:T(8,128)(2,1)}, u32[]{:S(2)}) copy-start(bf16[1,3584,512]{2,1,0:T(8,128)(2,1)} %param.18) | copy-start | bytes 11010052
  89.1 2.2 %copy-start.5 = (bf16[1,512,3584]{2,1,0:T(8,128)(2,1)S(1)}, bf16[1,512,3584]{2,1,0:T(8,128)(2,1)}, u32[]{:S(2)}) copy-start(bf16[1,512,3584]{2,1,0:T(8,128)(2,1)} %param.19) | copy-start | bytes 11010052
  95.2 5.5 %copy-start.1 = (bf16[4,256,576]{1,2,0:T(8,128)(2,1)S(1)}, bf16[4,256,576]{1,2,0:T(8,128)(2,1)}, u32[]{:S(2)}) copy-start(bf16[4,256,576]{1,2,0:T(8,128)(2,1)} %param.11) | copy-start | bytes 3538948
  95.2 5.6 %copy-start.2 = (s32[4]{0:T(128)S(1)}, s32[4]{0:T(128)}, u32[]{:S(2)}) copy-start(s32[4]{0:T(128)} %param.12) | copy-start | bytes 52
  95.2 57.7 %all-to-all-start.1 = ((bf16[16,32,3584]{2,1,0:T(8,128)(2,1)}), bf16[16,32,3584]{2,1,0:T(8,128)(2,1)}, u32[]{:S(2)}, u32[]{:S(2)}) async-start(bf16[16,32,3584]{2,1,0:T(8,128)(2,1)} %bitcast.46), calls=%async_computation.1 | async-start | bytes 7340032 | tf_op jit(solution)/shard_map/all_to_all | solution.py:315

commit v17 on v14

--- a/solution.py
+++ b/solution.py
@@ -328,8 +328,10 @@
     )
     weight_high = combine.astype(jnp.bfloat16)
     weight_low = (combine - weight_high.astype(jnp.float32)).astype(jnp.bfloat16)
-    column_mixed = jnp.dot(weight_high, expert_out, preferred_element_type=jnp.float32) + jnp.dot(
-        weight_low, expert_out, preferred_element_type=jnp.float32
+    column_mixed = jnp.dot(
+        jnp.concatenate([weight_high, weight_low], axis=1),
+        jnp.concatenate([expert_out, expert_out], axis=0),
+        preferred_element_type=jnp.float32,
     )
     mixed = ring_scatter(
         column_mixed.astype(jnp.bfloat16).reshape(group_count, row_count, feature), group_count

time: 181 us -> 181 us (level)
  no operation moved by 1% of the time
where the time goes in v17:
time: 181 us; the launch traced here: 180 us
  blocking collectives  51.9 us (29%)
  waiting for transfers between devices  48.8 us (27%)
  Pallas kernels  47.2 us (26%)
  matrix products  14.3 us (8%)
  other arithmetic  7.49 us (4%)
  local copies, waits for them, and re-layouts  4.64 us (3%)
  starting transfers between devices  4.63 us (3%)
    all_to_all x1, blocking collectives, per_device(): lax.all_to_all(doubled, 'ep', split_axis=0, concat_axis=0, tiled=True)  51.9 us
    all_to_all x1, waiting for transfers between devices, per_device(): lax.all_to_all(partials.reshape(peer_count, expert_slots, feature), 'ep',...  48.8 us
    pallas_call x1, Pallas kernels, ring_gather(): pl.pallas_call(functools.partial(gather_kernel, chips, windows), out_shap...  26.5 us
    pallas_call x1, Pallas kernels, ring_scatter(): pl.pallas_call(functools.partial(scatter_kernel, chips, widths), out_shap...  20.7 us
    all_to_all x1, starting transfers between devices, per_device(): lax.all_to_all(partials.reshape(peer_count, expert_slots, feature), 'ep',...  4.63 us
    dot_general x1, matrix products, expert_partial(): return jnp.dot(hidden, w_down[0], preferred_element_type=jnp.float32)  3.91 us
  transfers between devices with their start and end apart: 1, of which 1 were waited for; matrix products, arithmetic and copies ran while one was open for 2% of the time, Pallas kernels for 0%

profile of v17, /device:TPU:1, one launch (start us, length us, event | category | flops | bytes accessed | tf_op | source)
XLA Modules:
  0.0 180.4 jit_solution(16162086267465129073)
XLA Ops:
  0.7 0.7 convert_element_type.46
  1.4 0.1 copy.31
  1.5 0.8 copy.32
  2.2 0.7 select_maximum_fusion.m_ref
  2.9 26.5 %shard_map.113 = (bf16[16,16,3584]{2,1,0:T(8,128)(2,1)}, f32[16,16,128]{2,1,0:T(8,128)}) custom-call(bf16[16,3584]{1,0:T(8,128)(2,1)} %x_ref.1, f32[16,128]{1,0:T(8,128)} %select_maximum_fusion.m_ref), custom_call_target="tpu_custom_call" | custom-call | tf_op jit(solution)/shard_map/pallas_call | solution.py:128
  29.4 1.1 fusion.32
  30.5 0.1 copy.40
  30.6 0.1 reshape.124
  30.7 0.1 copy.34
  30.8 0.7 fusion.34
  31.5 0.1 copy.35
  31.6 0.1 reduce_window_sum.14
  31.7 0.1 add_select_fusion
  31.8 0.1 copy.36
  31.9 0.7 fusion.9
  32.6 2.2 %convolution_convert_fusion.2 = bf16[256,3584]{1,0:T(8,128)(2,1)S(1)} fusion(pred[256,256]{1,0:T(8,128)(4,1)S(1)} %fusion.9, bf16[256,3584]{1,0:T(8,128)(2,1)} %bitcast.44), kind=kOutput, calls=%fused_computation.3 | convolution fusion | flops 470679552 | bytes 3735552 | tf_op jit(solution)/shard_map/dot_general | solution.py:307
  34.8 0.4 broadcast_in_dim.46
  35.2 51.9 %all_to_all.10 = bf16[16,32,3584]{2,1,0:T(8,128)(2,1)S(1)} all-to-all(bf16[16,32,3584]{2,1,0:T(8,128)(2,1)S(1)} %bitcast.39), channel_id=1, replica_groups=mesh['grp'=16,'ep'=16] {'ep'}, dimensions={0} | all-to-all | bytes 7340032 | tf_op jit(solution)/shard_map/all_to_all | solution.py:311
  87.1 2.1 %fusion.7 = f32[512,512]{1,0:T(8,128)S(1)} fusion(bf16[512,3584]{1,0:T(8,128)(2,1)S(1)} %bitcast.42, bf16[1,3584,512]{2,1,0:T(8,128)(2,1)S(1)} %copy-done.3), kind=kOutput, calls=%fused_computation.11 | convolution fusion | flops 1879048192 | bytes 8388608 | tf_op jit(solution)/shard_map/dot_general | solution.py:266
  89.2 2.1 %fusion.13 = bf16[512,512]{1,0:T(8,128)(2,1)S(1)} fusion(bf16[512,3584]{1,0:T(8,128)(2,1)S(1)} %bitcast.43, bf16[1,3584,512]{2,1,0:T(8,128)(2,1)S(1)} %copy-done.4, f32[512,512]{1,0:T(8,128)S(1)} %fusion.7), kind=kOutput, calls=%fused_computation.17 | convolution fusion | flops 1880621056 | bytes 8912896 | tf_op jit(solution)/shard_map/dot_general | solution.py:267
  91.3 3.9 %convolution_convert_fusion = bf16[512,3584]{1,0:T(8,128)(2,1)} fusion(bf16[512,512]{1,0:T(8,128)(2,1)S(1)} %fusion.13, bf16[1,512,3584]{2,1,0:T(8,128)(2,1)S(1)} %copy-done.5), kind=kOutput, calls=%fused_computation.1 | convolution fusion | flops 1880883200 | bytes 7864320 | tf_op jit(solution)/shard_map/dot_general | solution.py:269
  95.2 4.6 %all-to-all-start.1 = ((bf16[16,32,3584]{2,1,0:T(8,128)(2,1)}), bf16[16,32,3584]{2,1,0:T(8,128)(2,1)}, u32[]{:S(2)}, u32[]{:S(2)}) async-start(bf16[16,32,3584]{2,1,0:T(8,128)(2,1)} %bitcast.41), calls=%async_computation.1 | async-start | bytes 7340032 | tf_op jit(solution)/shard_map/all_to_all | solution.py:315
  100.0 0.1 copy.38
  100.8 0.3 fusion.17
  101.2 0.2 fusion.33
  101.4 1.5 select_reduce_fusion
  102.9 1.2 fusion.20
  104.2 48.8 %all-to-all-done.1 = bf16[16,32,3584]{2,1,0:T(8,128)(2,1)} async-done(((bf16[16,32,3584]{2,1,0:T(8,128)(2,1)}), bf16[16,32,3584]{2,1,0:T(8,128)(2,1)}, u32[]{:S(2)}, u32[]{:S(2)}) %all-to-all-start.1) | async-done | bytes 3670048 | tf_op jit(solution)/shard_map/all_to_all | solution.py:315
  153.0 2.8 %bitcast_reduce_fusion = bf16[8,32,3584]{2,1,0:T(8,128)(2,1)S(1)} fusion(bf16[16,32,3584]{2,1,0:T(8,128)(2,1)} %all-to-all-done.1), kind=kLoop, calls=%fused_computation.7 | loop fusion | flops 917504 | bytes 5505024 | tf_op jit(solution)/shard_map/reduce_sum | solution.py:325
  155.8 2.4 %convolution_convert_fusion.1 = bf16[256,3584]{1,0:T(8,128)(2,1)} fusion(bf16[256,3584]{1,0:T(8,128)(2,1)S(1)} %bitcast.46, bf16[256,256]{1,0:T(8,128)(2,1)S(1)} %get-tuple-element.6, bf16[256,256]{1,0:T(8,128)(2,1)S(1)} %get-tuple-element.7), kind=kOutput, calls=%fused_computation.2 | convolution fusion | flops 948305920 | bytes 3932160 | tf_op jit(solution)/shard_map/dot_general | solution.py:331
  158.1 20.7 %shard_map.114 = bf16[16,3584]{1,0:T(8,128)(2,1)} custom-call(bf16[16,16,3584]{2,1,0:T(8,128)(2,1)} %bitcast.45), custom_call_target="tpu_custom_call" | custom-call | tf_op jit(solution)/shard_map/pallas_call | solution.py:247
  178.9 1.6 copy.43
  (20 shorter events, 0.2 us)
Async XLA Ops:
  0.6 100.1 %copy-start = (bf16[4,64,576]{2,1,0:T(8,128)(2,1)S(1)}, bf16[4,64,576]{2,1,0:T(8,128)(2,1)}, u32[]{:S(2)}) copy-start(bf16[4,64,576]{2,1,0:T(8,128)(2,1)} %param.10) | copy-start | bytes 884740
  35.2 51.9 %copy-start.3 = (bf16[1,3584,512]{2,1,0:T(8,128)(2,1)S(1)}, bf16[1,3584,512]{2,1,0:T(8,128)(2,1)}, u32[]{:S(2)}) copy-start(bf16[1,3584,512]{2,1,0:T(8,128)(2,1)} %param.17) | copy-start | bytes 11010052
  87.1 2.1 %copy-start.4 = (bf16[1,3584,512]{2,1,0:T(8,128)(2,1)S(1)}, bf16[1,3584,512]{2,1,0:T(8,128)(2,1)}, u32[]{:S(2)}) copy-start(bf16[1,3584,512]{2,1,0:T(8,128)(2,1)} %param.18) | copy-start | bytes 11010052
  89.2 2.2 %copy-start.5 = (bf16[1,512,3584]{2,1,0:T(8,128)(2,1)S(1)}, bf16[1,512,3584]{2,1,0:T(8,128)(2,1)}, u32[]{:S(2)}) copy-start(bf16[1,512,3584]{2,1,0:T(8,128)(2,1)} %param.19) | copy-start | bytes 11010052
  95.2 5.5 %copy-start.1 = (bf16[4,256,576]{1,2,0:T(8,128)(2,1)S(1)}, bf16[4,256,576]{1,2,0:T(8,128)(2,1)}, u32[]{:S(2)}) copy-start(bf16[4,256,576]{1,2,0:T(8,128)(2,1)} %param.11) | copy-start | bytes 3538948
  95.2 5.6 %copy-start.2 = (s32[4]{0:T(128)S(1)}, s32[4]{0:T(128)}, u32[]{:S(2)}) copy-start(s32[4]{0:T(128)} %param.12) | copy-start | bytes 52
  95.2 57.7 %all-to-all-start.1 = ((bf16[16,32,3584]{2,1,0:T(8,128)(2,1)}), bf16[16,32,3584]{2,1,0:T(8,128)(2,1)}, u32[]{:S(2)}, u32[]{:S(2)}) async-start(bf16[16,32,3584]{2,1,0:T(8,128)(2,1)} %bitcast.41), calls=%async_computation.1 | async-start | bytes 7340032 | tf_op jit(solution)/shard_map/all_to_all | solution.py:315
